TPU v7x, 512 devices: a whole 4x8x8 slice. The times are simulated.
512 devices in a mesh: dp: 64 (over x, y, z_lo), tensor: 8 (over z_hi, core).
Axes of the slice: x: 4, y: 8, z: 8 (z_hi: 4, z_lo: 2; z = z_hi * 2 + z_lo), core: 2. Of those that a mesh axis runs over, the one named last changes fastest.
Arguments:
- tokens: bfloat16 [8192, 2048], P('dp'), may hold values from -6 to 6
- cotangent: bfloat16 [8192, 2048], P('dp'), may hold values from -6 to 6
- expert_ids: int32 [8192, 4], P('dp'), may hold values from 0 to 63, all different within a row; in each aligned block of 128 rows (0 to 127, 128 to 255, ...) at most 10 rows name the same one
- route_weight: float32 [8192, 4], P('dp'), may hold values from 0.05 to 1
- forget_mask: int32 [8192], P('dp'), may hold values from 0 to 1, as said below
- lengths: int32 [2], replicated, may hold values from 1024 to 4096, as said below
- gate_weight: bfloat16 [64, 1024, 2048], P('dp', 'tensor'), may hold values from -0.125 to 0.125
- up_weight: bfloat16 [64, 1024, 2048], P('dp', 'tensor'), may hold values from -0.125 to 0.125
- down_weight: bfloat16 [64, 1024, 2048], P('dp', 'tensor'), may hold values from -0.1875 to 0.1875
Outputs:
- mixed_out: bfloat16 [8192, 2048], P('dp', 'tensor')
- grad_gate: bfloat16 [64, 1024, 2048], P('dp', 'tensor')
- grad_up: bfloat16 [64, 1024, 2048], P('dp', 'tensor')
- grad_down: bfloat16 [64, 1024, 2048], P('dp', 'tensor')
Inputs may be any that keep to these rules, and one draw needn't show every extreme that they name: `expert_ids`: among the rows of one index of dp (aligned blocks of 128 tokens), no expert is named more than 10 times. `forget_mask`: the first token slot of every sequence is 0 and the second is 1. `lengths`: at least one sequence uses all 4096 slots.
All inputs are finite; a program needn't handle non-finite values.
Results may differ from a plain program's by a relative error of at most 0.019.
Values may be sent and summed in bfloat16 or wider, within the bound.
A program may use at most 128 MiB of HBM per device.

v0:
```python
import jax
import jax.numpy as jnp
from jax import lax
from jax.sharding import PartitionSpec as P


def body(
    tokens,
    cotangent,
    expert_ids,
    route_weight,
    forget_mask,
    lengths,
    gate_weight,
    up_weight,
    down_weight,
):
    tok_rows = tokens.shape[0]
    features = tokens.shape[1]
    top_count = expert_ids.shape[1]
    owners = lax.axis_size("dp")
    capacity = 5 * tok_rows * top_count // (4 * owners)
    seq_count = lengths.shape[0]
    seq_len = tok_rows * owners // seq_count
    token_index = lax.axis_index("dp") * tok_rows + jnp.arange(tok_rows, dtype=jnp.int32)
    seq_id = token_index // seq_len
    seq_pos = token_index - seq_id * seq_len
    in_seq = seq_id[:, None] == jnp.arange(seq_count, dtype=jnp.int32)[None, :]
    limits = jnp.sum(jnp.where(in_seq, lengths[None, :], 0), axis=1)
    is_valid = (seq_pos < limits).astype(jnp.int32)
    forget = is_valid * forget_mask
    retain = is_valid - forget
    n_forget, n_retain = lax.psum((jnp.sum(forget), jnp.sum(retain)), "dp")
    coefficient = float(top_count * tok_rows) * (
        retain.astype(jnp.float32) / n_retain.astype(jnp.float32)
        - forget.astype(jnp.float32) / n_forget.astype(jnp.float32)
    )
    shares = route_weight / jnp.sum(route_weight, axis=1, keepdims=True)
    share_flat = shares.reshape(-1)
    assigned = tok_rows * top_count
    flat_ids = expert_ids.reshape(-1)
    one_hot = (flat_ids[:, None] == jnp.arange(owners, dtype=jnp.int32)[None, :]).astype(jnp.int32)
    before = jnp.cumsum(one_hot, axis=0) - one_hot
    slot_id = jnp.sum(before * one_hot, axis=1)
    target = flat_ids * capacity + slot_id
    slots_all = owners * capacity
    source = (
        jnp.full((slots_all,), assigned, jnp.int32)
        .at[target]
        .set(jnp.arange(assigned, dtype=jnp.int32))
    )
    is_live = source < assigned
    source_row = jnp.minimum(source, assigned - 1)
    source_tok = source_row // top_count
    send_rows = jnp.where(
        is_live[:, None], tokens[source_tok], jnp.zeros((), tokens.dtype)
    ).reshape(owners, capacity, features)
    slot_weight = jnp.where(is_live, coefficient[source_tok] * share_flat[source_row], 0.0)
    send_cotan = (
        (slot_weight[:, None] * cotangent[source_tok].astype(jnp.float32))
        .astype(jnp.bfloat16)
        .reshape(owners, capacity, features)
    )
    recv_rows, recv_cotan = (
        lax.all_to_all(send_rows, "dp", split_axis=0, concat_axis=0, tiled=True),
        lax.all_to_all(send_cotan, "dp", split_axis=0, concat_axis=0, tiled=True),
    )
    rows_in = recv_rows.reshape(slots_all, features)
    contract_last = (((1,), (1,)), ((), ()))
    contract_first = (((0,), (0,)), ((), ()))
    gate_pre = lax.dot_general(
        gate_weight[0], rows_in, contract_last, preferred_element_type=jnp.float32
    )
    up_pre = lax.dot_general(
        up_weight[0], rows_in, contract_last, preferred_element_type=jnp.float32
    )
    sigmoid_gate = jax.nn.sigmoid(gate_pre)
    hidden = (gate_pre * sigmoid_gate * up_pre).astype(jnp.bfloat16)
    partial_out = lax.dot_general(
        hidden, down_weight[0], contract_first, preferred_element_type=jnp.float32
    )
    returned = lax.all_to_all(
        partial_out.astype(jnp.bfloat16).reshape(owners, capacity, features),
        "dp",
        split_axis=0,
        concat_axis=0,
        tiled=True,
    )
    picked = returned.reshape(slots_all, features)[target].astype(jnp.float32) * share_flat[:, None]
    token_terms = jnp.sum(picked.reshape(tok_rows, top_count, features), axis=1)
    mixed_out = lax.psum_scatter(
        token_terms.astype(jnp.bfloat16), "tensor", scatter_dimension=1, tiled=True
    )
    routed = recv_cotan.reshape(slots_all, features)
    grad_down = jnp.dot(hidden, routed, preferred_element_type=jnp.float32)
    dhidden = lax.dot_general(
        down_weight[0], routed, contract_last, preferred_element_type=jnp.float32
    )
    dgate = (dhidden * up_pre * sigmoid_gate * (1.0 + gate_pre * (1.0 - sigmoid_gate))).astype(
        jnp.bfloat16
    )
    dup = (dhidden * gate_pre * sigmoid_gate).astype(jnp.bfloat16)
    grad_gate = jnp.dot(dgate, rows_in, preferred_element_type=jnp.float32)
    grad_up = jnp.dot(dup, rows_in, preferred_element_type=jnp.float32)
    return (
        mixed_out,
        grad_gate.astype(jnp.bfloat16)[None],
        grad_up.astype(jnp.bfloat16)[None],
        grad_down.astype(jnp.bfloat16)[None],
    )


def solution(mesh):
    in_specs = (
        P("dp", None),
        P("dp", None),
        P("dp", None),
        P("dp", None),
        P("dp"),
        P(),
        P("dp", "tensor", None),
        P("dp", "tensor", None),
        P("dp", "tensor", None),
    )
    out_specs = (
        P("dp", "tensor"),
        P("dp", "tensor", None),
        P("dp", "tensor", None),
        P("dp", "tensor", None),
    )
    return jax.shard_map(body, mesh=mesh, in_specs=in_specs, out_specs=out_specs, check_vma=False)
```

profile of v0, /device:TPU:6, one launch (start us, length us, event | category | flops | bytes accessed | tf_op | source)
XLA Modules:
  0.0 427.1 jit_solution(7708130593639780527)
XLA Ops:
  7.2 0.7 broadcast_multiply_fusion
  7.9 0.8 copy.21
  9.0 0.7 fusion.17
  9.7 1.3 fusion.19
  11.0 22.5 %all-reduce = (s32[]{:T(128)}, s32[]{:T(128)}) all-reduce(s32[]{:T(128)} %get-tuple-element.5, s32[]{:T(128)} %get-tuple-element.4), channel_id=1, replica_groups=mesh['dp'=64,'tensor'=8] {'dp'}, use_global_device_ids=true, to_apply=%region_11.12 | all-reduce | flops 2 | bytes 16 | tf_op jit(solution)/shard_map/psum | solution.py:33
  34.8 0.7 reduce_sum.58
  35.5 0.7 broadcast_divide_fusion
  36.2 0.1 copy.24
  36.3 0.1 reshape.122
  36.4 0.1 copy.20
  36.5 0.1 mul.84
  36.7 1.2 reduce-window.6
  37.9 0.2 slice_reduce_fusion
  38.2 0.1 fusion.11
  38.3 2.4 scatter_custom_fusion
  40.8 4.3 %gather_fusion.3 = f32[640]{0:T(1024)S(1)} fusion(f32[512]{0:T(512)S(1)} %reshape.122, s32[1024]{0:T(1024)S(1)} %get-tuple-element.15), kind=kCustom, calls=%fused_computation.3 | custom fusion | bytes 7680 | tf_op jit(solution)/shard_map/gather | solution.py:58
  45.2 4.1 gather_fusion.2
  49.3 0.1 broadcast_in_dim.56
  49.5 4.1 gather_fusion
  53.6 5.4 %gather.18 = bf16[64,10,2048]{2,1,0:T(8,128)(2,1)} reshape(bf16[640,2048]{1,0:T(8,128)(2,1)} %gather_fusion) | data formatting | bytes 5242880 | tf_op jit(solution)/shard_map/gather | solution.py:56
  58.9 4.5 %broadcast_select_fusion = bf16[64,10,2048]{2,1,0:T(8,128)(2,1)} fusion(bf16[64,10,2048]{2,1,0:T(8,128)(2,1)} %gather.18, pred[64,10]{1,0:T(8,128)(4,1)S(1)} %broadcast_in_dim.56), kind=kLoop, calls=%fused_computation.8 | loop fusion | flops 1310720 | bytes 5243520 | tf_op jit(solution)/shard_map/jit(_where)/select_n | solution.py:55
  63.4 9.8 %all-to-all-start = ((bf16[64,10,2048]{2,1,0:T(8,128)(2,1)}), bf16[64,10,2048]{2,1,0:T(8,128)(2,1)}, u32[]{:S(2)}, u32[]{:S(2)}) async-start(bf16[64,10,2048]{2,1,0:T(8,128)(2,1)} %broadcast_select_fusion), calls=%async_computation | async-start | bytes 8388608 | tf_op jit(solution)/shard_map/all_to_all | solution.py:65
  73.2 0.1 mul.96
  73.3 4.2 gather_fusion.4
  77.5 5.8 %reshape.125 = f32[64,10,2048]{2,1,0:T(8,128)} reshape(bf16[640,2048]{1,0:T(8,128)(2,1)} %gather_fusion.4) | data formatting | bytes 7864320 | tf_op jit(solution)/shard_map/convert_element_type | solution.py:60
  83.3 5.8 %multiply_convert_fusion = bf16[64,10,2048]{2,1,0:T(8,128)(2,1)} fusion(f32[64,10,2048]{2,1,0:T(8,128)} %reshape.125, f32[64,10]{1,0:T(8,128)S(1)} %mul.96), kind=kLoop, calls=%fused_computation.6 | loop fusion | flops 2621440 | bytes 7866880 | tf_op jit(solution)/shard_map/convert_element_type | solution.py:61
  89.2 73.0 %all-to-all-done = bf16[64,10,2048]{2,1,0:T(8,128)(2,1)} async-done(((bf16[64,10,2048]{2,1,0:T(8,128)(2,1)}), bf16[64,10,2048]{2,1,0:T(8,128)(2,1)}, u32[]{:S(2)}, u32[]{:S(2)}) %all-to-all-start) | async-done | bytes 2621472 | tf_op jit(solution)/shard_map/all_to_all | solution.py:65
  162.2 8.5 %all-to-all-start.2 = ((bf16[64,10,2048]{2,1,0:T(8,128)(2,1)}), bf16[64,10,2048]{2,1,0:T(8,128)(2,1)}, u32[]{:S(2)}, u32[]{:S(2)}) async-start(bf16[64,10,2048]{2,1,0:T(8,128)(2,1)} %multiply_convert_fusion), calls=%async_computation.3 | async-start | bytes 8388608 | tf_op jit(solution)/shard_map/all_to_all | solution.py:66
  170.7 4.1 reshape.119
  174.8 2.3 convolution_bitcast_fusion.2
  177.2 1.6 multiply_convert_fusion.3
  178.7 0.7 copy-done.6
  179.4 0.8 convolution_convert_fusion
  180.3 2.8 reshape.120
  183.0 77.5 %all-to-all-done.2 = bf16[64,10,2048]{2,1,0:T(8,128)(2,1)} async-done(((bf16[64,10,2048]{2,1,0:T(8,128)(2,1)}), bf16[64,10,2048]{2,1,0:T(8,128)(2,1)}, u32[]{:S(2)}, u32[]{:S(2)}) %all-to-all-start.2) | async-done | bytes 2621472 | tf_op jit(solution)/shard_map/all_to_all | solution.py:66
  260.5 8.5 %all-to-all-start.1 = ((bf16[64,10,2048]{2,1,0:T(8,128)(2,1)}), bf16[64,10,2048]{2,1,0:T(8,128)(2,1)}, u32[]{:S(2)}, u32[]{:S(2)}) async-start(bf16[64,10,2048]{2,1,0:T(8,128)(2,1)} %reshape.120), calls=%async_computation.1 | async-start | bytes 8388608 | tf_op jit(solution)/shard_map/all_to_all | solution.py:82
  269.1 5.5 %reshape.123 = bf16[640,2048]{1,0:T(8,128)(2,1)} reshape(bf16[64,10,2048]{2,1,0:T(8,128)(2,1)} %all-to-all-done.2) | data formatting | bytes 5242880 | tf_op jit(solution)/shard_map/reshape | solution.py:94
  274.7 85.1 %all-to-all-done.1 = bf16[64,10,2048]{2,1,0:T(8,128)(2,1)} async-done(((bf16[64,10,2048]{2,1,0:T(8,128)(2,1)}), bf16[64,10,2048]{2,1,0:T(8,128)(2,1)}, u32[]{:S(2)}, u32[]{:S(2)}) %all-to-all-start.1) | async-done | bytes 2621472 | tf_op jit(solution)/shard_map/all_to_all | solution.py:82
  359.8 4.1 reshape.121
  363.9 3.3 gather_fusion.1
  367.2 4.8 %reshape.124 = f32[128,4,2048]{2,1,0:T(4,128)} reshape(bf16[512,2048]{1,0:T(8,128)(2,1)} %gather_fusion.1) | data formatting | bytes 6291456 | tf_op jit(solution)/shard_map/convert_element_type | solution.py:89
  372.0 6.4 %multiply_reduce_fusion = bf16[128,2048]{1,0:T(8,128)(2,1)} fusion(f32[128,4,2048]{2,1,0:T(4,128)} %reshape.124, f32[128,4]{1,0:T(8,128)S(1)} %copy.24), kind=kLoop, calls=%fused_computation.7 | loop fusion | flops 1835008 | bytes 4720640 | tf_op jit(solution)/shard_map/reduce_sum | solution.py:90
  378.4 2.3 fusion.2
  380.7 0.8 convolution_bitcast_fusion
  381.6 0.9 copy-done.4
  382.5 1.4 fusion.1
  383.9 1.5 fusion
  385.4 34.9 %reduce-scatter.2.cloned.1.call-done = bf16[128,256]{1,0:T(8,128)(2,1)} async-done(((bf16[128,2048]{1,0:T(8,128)(2,1)}), bf16[128,256]{1,0:T(8,128)(2,1)}) %reduce-scatter.2.cloned.1.call-update) | async-done | bytes 65552 | tf_op jit(solution)/shard_map/reduce_scatter | solution.py:91
  (33 shorter events, 0.4 us)
Async XLA Ops:
  7.2 172.2 %copy-start = (bf16[1,128,2048]{2,1,0:T(8,128)(2,1)S(1)}, bf16[1,128,2048]{2,1,0:T(8,128)(2,1)}, u32[]{:S(2)}) copy-start(bf16[1,128,2048]{2,1,0:T(8,128)(2,1)} %param.17) | copy-start | bytes 1572868
  8.9 36.2 %copy-start.8 = (s32[128]{0:T(128)S(1)}, s32[128]{0:T(128)}, u32[]{:S(2)}) copy-start(s32[128]{0:T(128)} %param.13) | copy-start | bytes 1540
  45.1 4.3 %copy-start.1 = (bf16[128,2048]{1,0:T(8,128)(2,1)S(1)}, bf16[128,2048]{1,0:T(8,128)(2,1)}, u32[]{:S(2)}) copy-start(bf16[128,2048]{1,0:T(8,128)(2,1)} %param.9) | copy-start | bytes 1572868
  63.4 9.9 %copy-start.2 = (bf16[128,2048]{1,0:T(8,128)(2,1)S(1)}, bf16[128,2048]{1,0:T(8,128)(2,1)}, u32[]{:S(2)}) copy-start(bf16[128,2048]{1,0:T(8,128)(2,1)} %param.10) | copy-start | bytes 1572868
  63.4 98.8 %all-to-all-start = ((bf16[64,10,2048]{2,1,0:T(8,128)(2,1)}), bf16[64,10,2048]{2,1,0:T(8,128)(2,1)}, u32[]{:S(2)}, u32[]{:S(2)}) async-start(bf16[64,10,2048]{2,1,0:T(8,128)(2,1)} %broadcast_select_fusion), calls=%async_computation | async-start | bytes 8388608 | tf_op jit(solution)/shard_map/all_to_all | solution.py:65
  162.2 98.3 %all-to-all-start.2 = ((bf16[64,10,2048]{2,1,0:T(8,128)(2,1)}), bf16[64,10,2048]{2,1,0:T(8,128)(2,1)}, u32[]{:S(2)}, u32[]{:S(2)}) async-start(bf16[64,10,2048]{2,1,0:T(8,128)(2,1)} %multiply_convert_fusion), calls=%async_computation.3 | async-start | bytes 8388608 | tf_op jit(solution)/shard_map/all_to_all | solution.py:66
  174.8 2.4 copy-start.3
  174.8 2.4 copy-start.9
  178.7 0.7 copy-start.6
  260.5 99.3 %all-to-all-start.1 = ((bf16[64,10,2048]{2,1,0:T(8,128)(2,1)}), bf16[64,10,2048]{2,1,0:T(8,128)(2,1)}, u32[]{:S(2)}, u32[]{:S(2)}) async-start(bf16[64,10,2048]{2,1,0:T(8,128)(2,1)} %reshape.120), calls=%async_computation.1 | async-start | bytes 8388608 | tf_op jit(solution)/shard_map/all_to_all | solution.py:82
  269.1 151.2 %reduce-scatter.2.cloned.1.call-start = ((), (), s32[]{:S(2)}) async-start(), calls=%async_computation.4 | async-start | bytes 589824 | tf_op jit(solution)/shard_map/reduce_scatter | solution.py:91
  372.0 6.4 %copy-start.5 = (bf16[640,2048]{1,0:T(8,128)(2,1)S(1)}, bf16[640,2048]{1,0:T(8,128)(2,1)}, u32[]{:S(2)}) copy-start(bf16[640,2048]{1,0:T(8,128)(2,1)} %reshape.123) | copy-start | bytes 7864324
  380.7 1.7 copy-start.4
  382.4 1.4 copy-start.7
Sparse Core Ops, SparseCore 0:
  378.5 41.7 reduce-scatter.1
where the time goes:
time: 428 us; the launch traced here: 427 us
  waiting for transfers between devices  271 us (63%)
  local copies, waits for them, and re-layouts  58.4 us (14%)
  starting transfers between devices  26.8 us (6%)
  blocking collectives  22.5 us (5%)
  other arithmetic  22.3 us (5%)
  between operations  15.6 us (4%)
  matrix products  10.8 us (3%)
    all_to_all x1, waiting for transfers between devices, body(): lax.all_to_all(partial_out.astype(jnp.bfloat16).reshape(owners, capacity,...  85.1 us
    all_to_all x1, waiting for transfers between devices, body(): lax.all_to_all(send_cotan, 'dp', split_axis=0, concat_axis=0, tiled=True)  77.5 us
    all_to_all x1, waiting for transfers between devices, body(): lax.all_to_all(send_rows, 'dp', split_axis=0, concat_axis=0, tiled=True)  73 us
    reduce_scatter x1, waiting for transfers between devices, body(): lax.psum_scatter(token_terms.astype(jnp.bfloat16), 'tensor', scatter_dime...  34.9 us
    psum x1, blocking collectives, body(): n_forget, n_retain = lax.psum((jnp.sum(forget), jnp.sum(retain)), 'dp')  22.5 us
    all_to_all x1, starting transfers between devices, body(): lax.all_to_all(send_rows, 'dp', split_axis=0, concat_axis=0, tiled=True)  9.79 us
    gather x2, local copies, waits for them, and re-layouts, body(): tokens[source_tok]  9.44 us
  transfers between devices with their start and end apart: 4, of which 4 were waited for; matrix products, arithmetic and copies ran while one was open for 9% of the time, Pallas kernels for 0%

commit v1 on v0

v1 whole, which is shorter than its diff:
```python
import jax
import jax.numpy as jnp
import numpy as np
from jax import lax
from jax.sharding import Mesh
from jax.sharding import PartitionSpec as P


def _swap_pair(x):
    return lax.ppermute(x, "core", [(0, 1), (1, 0)])


def body(
    tokens,
    cotangent,
    expert_ids,
    route_weight,
    forget_mask,
    lengths,
    gate_weight,
    up_weight,
    down_weight,
):
    tok_rows = tokens.shape[0]
    features = tokens.shape[1]
    half = features // 2
    top_count = expert_ids.shape[1]
    owners = lax.axis_size("dp")
    groups = lax.axis_size("zh")
    block = features // (2 * groups)
    capacity = 5 * tok_rows * top_count // (4 * owners)
    core = lax.axis_index("core")
    is_first = core == 0

    seq_count = lengths.shape[0]
    seq_len = tok_rows * owners // seq_count
    token_index = lax.axis_index("dp") * tok_rows + jnp.arange(tok_rows, dtype=jnp.int32)
    seq_id = token_index // seq_len
    seq_pos = token_index - seq_id * seq_len
    in_seq = seq_id[:, None] == jnp.arange(seq_count, dtype=jnp.int32)[None, :]
    limits = jnp.sum(jnp.where(in_seq, lengths[None, :], 0), axis=1)
    is_valid = (seq_pos < limits).astype(jnp.int32)
    forget = is_valid * forget_mask
    retain = is_valid - forget

    shares = route_weight / jnp.sum(route_weight, axis=1, keepdims=True)
    share_flat = shares.reshape(-1)
    assigned = tok_rows * top_count
    flat_ids = expert_ids.reshape(-1)
    one_hot = (flat_ids[:, None] == jnp.arange(owners, dtype=jnp.int32)[None, :]).astype(jnp.int32)
    before = jnp.cumsum(one_hot, axis=0) - one_hot
    slot_id = jnp.sum(before * one_hot, axis=1)
    target = flat_ids * capacity + slot_id
    slots_all = owners * capacity
    source = (
        jnp.full((slots_all,), assigned, jnp.int32)
        .at[target]
        .set(jnp.arange(assigned, dtype=jnp.int32))
    )
    is_live = source < assigned
    source_row = jnp.minimum(source, assigned - 1)
    source_tok = source_row // top_count

    my_tokens = lax.dynamic_slice_in_dim(tokens, core * half, half, axis=1)
    send_rows = jnp.where(
        is_live[:, None], my_tokens[source_tok], jnp.zeros((), tokens.dtype)
    ).reshape(owners, capacity, half)
    recv_rows = lax.all_to_all(send_rows, "dp", split_axis=0, concat_axis=0, tiled=True)
    recv_rows = recv_rows.reshape(slots_all, half)
    other_rows = _swap_pair(recv_rows)
    rows_in = jnp.concatenate(
        [jnp.where(is_first, recv_rows, other_rows), jnp.where(is_first, other_rows, recv_rows)],
        axis=1,
    )

    n_forget, n_retain = lax.psum((jnp.sum(forget), jnp.sum(retain)), "dp")
    coefficient = float(top_count * tok_rows) * (
        retain.astype(jnp.float32) / n_retain.astype(jnp.float32)
        - forget.astype(jnp.float32) / n_forget.astype(jnp.float32)
    )
    slot_weight = jnp.where(is_live, coefficient[source_tok] * share_flat[source_row], 0.0)
    my_cotan = lax.dynamic_slice_in_dim(cotangent, core * half, half, axis=1)
    send_cotan = (
        (slot_weight[:, None] * my_cotan[source_tok].astype(jnp.float32))
        .astype(jnp.bfloat16)
        .reshape(owners, capacity, half)
    )
    recv_cotan = lax.all_to_all(send_cotan, "dp", split_axis=0, concat_axis=0, tiled=True)
    recv_cotan = recv_cotan.reshape(slots_all, half)
    other_cotan = _swap_pair(recv_cotan)
    routed = jnp.concatenate(
        [jnp.where(is_first, recv_cotan, other_cotan), jnp.where(is_first, other_cotan, recv_cotan)],
        axis=1,
    )

    contract_last = (((1,), (1,)), ((), ()))
    contract_first = (((0,), (0,)), ((), ()))
    gate_pre = lax.dot_general(
        gate_weight[0], rows_in, contract_last, preferred_element_type=jnp.float32
    )
    up_pre = lax.dot_general(
        up_weight[0], rows_in, contract_last, preferred_element_type=jnp.float32
    )
    sigmoid_gate = jax.nn.sigmoid(gate_pre)
    hidden = (gate_pre * sigmoid_gate * up_pre).astype(jnp.bfloat16)
    partial_out = lax.dot_general(
        hidden, down_weight[0], contract_first, preferred_element_type=jnp.float32
    ).astype(jnp.bfloat16)
    pieces = partial_out.reshape(slots_all, groups, 2, block)
    keep = jnp.where(is_first, pieces[:, :, 0, :], pieces[:, :, 1, :])
    give = jnp.where(is_first, pieces[:, :, 1, :], pieces[:, :, 0, :])
    pair_sum = (keep.astype(jnp.float32) + _swap_pair(give).astype(jnp.float32)).astype(jnp.bfloat16)
    returned = lax.all_to_all(
        pair_sum.reshape(owners, capacity, groups * block),
        "dp",
        split_axis=0,
        concat_axis=0,
        tiled=True,
    )
    picked = returned.reshape(slots_all, groups * block)[target].astype(jnp.float32) * share_flat[:, None]
    token_terms = jnp.sum(picked.reshape(tok_rows, top_count, groups, block), axis=1)
    mixed_out = lax.psum_scatter(token_terms, "zh", scatter_dimension=1, tiled=True)
    mixed_out = mixed_out.reshape(tok_rows, block).astype(jnp.bfloat16)

    grad_down = jnp.dot(hidden, routed, preferred_element_type=jnp.float32)
    dhidden = lax.dot_general(
        down_weight[0], routed, contract_last, preferred_element_type=jnp.float32
    )
    dgate = (dhidden * up_pre * sigmoid_gate * (1.0 + gate_pre * (1.0 - sigmoid_gate))).astype(
        jnp.bfloat16
    )
    dup = (dhidden * gate_pre * sigmoid_gate).astype(jnp.bfloat16)
    grad_gate = jnp.dot(dgate, rows_in, preferred_element_type=jnp.float32)
    grad_up = jnp.dot(dup, rows_in, preferred_element_type=jnp.float32)
    return (
        mixed_out,
        grad_gate.astype(jnp.bfloat16)[None],
        grad_up.astype(jnp.bfloat16)[None],
        grad_down.astype(jnp.bfloat16)[None],
    )


def solution(mesh):
    n_dp = mesh.shape["dp"]
    n_tensor = mesh.shape["tensor"]
    fine = Mesh(
        np.asarray(mesh.devices).reshape(n_dp, n_tensor // 2, 2), ("dp", "zh", "core")
    )
    tp = ("zh", "core")
    in_specs = (
        P("dp", None),
        P("dp", None),
        P("dp", None),
        P("dp", None),
        P("dp"),
        P(),
        P("dp", tp, None),
        P("dp", tp, None),
        P("dp", tp, None),
    )
    out_specs = (
        P("dp", tp),
        P("dp", tp, None),
        P("dp", tp, None),
        P("dp", tp, None),
    )
    return jax.shard_map(body, mesh=fine, in_specs=in_specs, out_specs=out_specs, check_vma=False)
```

time: 428 us -> 288 us (0.67)
  waiting for transfers between devices: 271 us -> 95.8 us
  blocking collectives: 22.5 us -> 76.6 us
  local copies, waits for them, and re-layouts: 58.4 us -> 49.8 us
  other arithmetic: 22.3 us -> 16.6 us
  starting transfers between devices: 26.8 us -> 22.3 us
    all_to_all x2 -> x1, waiting for transfers between devices: 158 us -> 43.6 us  [body(): lax.all_to_all(pair_sum.reshape(owners, capacity, groups * block), 'dp',...]
    all_to_all x0 -> x1, blocking collectives: none -> 54.1 us  [body(): lax.all_to_all(send_rows, 'dp', split_axis=0, concat_axis=0, tiled=True)]
    all_to_all x1, waiting for transfers between devices: 77.5 us -> 25.9 us  [body(): lax.all_to_all(send_cotan, 'dp', split_axis=0, concat_axis=0, tiled=True)]
    reduce_scatter x1, waiting for transfers between devices: 34.9 us -> 23.3 us  [body(): lax.psum_scatter(token_terms, 'zh', scatter_dimension=1, tiled=True)]
    all_to_all x2 -> x1, starting transfers between devices: 18.3 us -> 8.42 us  [body(): lax.all_to_all(pair_sum.reshape(owners, capacity, groups * block), 'dp',...]
    ppermute x0 -> x3, starting transfers between devices: none -> 5.96 us  [_swap_pair(): return lax.ppermute(x, 'core', [(0, 1), (1, 0)])]
    gather x4, local copies, waits for them, and re-layouts: 16.9 us -> 11.5 us  [the longest x2 5.84 us: body(): my_tokens[source_tok]]
    convert_element_type x2 -> x3, local copies, waits for them, and re-layouts: 10.6 us -> 5.11 us  [the longest x1 2.1 us: body(): my_cotan[source_tok].astype(jnp.float32)]
  transfers between devices with their start and end apart: 4 -> 6, of which waited for: 4 -> 4; matrix products, arithmetic and copies ran while one was open for 9% -> 16% of each run, Pallas kernels for 0% -> 0%
where the time goes in v1:
time: 288 us; the launch traced here: 287 us
  waiting for transfers between devices  95.8 us (33%)
  blocking collectives  76.6 us (27%)
  local copies, waits for them, and re-layouts  49.8 us (17%)
  starting transfers between devices  22.3 us (8%)
  other arithmetic  16.6 us (6%)
  between operations  15.7 us (5%)
  matrix products  9.92 us (3%)
    all_to_all x1, blocking collectives, body(): lax.all_to_all(send_rows, 'dp', split_axis=0, concat_axis=0, tiled=True)  54.1 us
    all_to_all x1, waiting for transfers between devices, body(): lax.all_to_all(pair_sum.reshape(owners, capacity, groups * block), 'dp',...  43.6 us
    all_to_all x1, waiting for transfers between devices, body(): lax.all_to_all(send_cotan, 'dp', split_axis=0, concat_axis=0, tiled=True)  25.9 us
    reduce_scatter x1, waiting for transfers between devices, body(): lax.psum_scatter(token_terms, 'zh', scatter_dimension=1, tiled=True)  23.3 us
    psum x1, blocking collectives, body(): n_forget, n_retain = lax.psum((jnp.sum(forget), jnp.sum(retain)), 'dp')  22.5 us
    all_to_all x1, starting transfers between devices, body(): lax.all_to_all(pair_sum.reshape(owners, capacity, groups * block), 'dp',...  8.42 us
    all_to_all x1, starting transfers between devices, body(): lax.all_to_all(send_cotan, 'dp', split_axis=0, concat_axis=0, tiled=True)  7.9 us
    ppermute x3, starting transfers between devices, _swap_pair(): return lax.ppermute(x, 'core', [(0, 1), (1, 0)])  5.96 us
  transfers between devices with their start and end apart: 6, of which 4 were waited for; matrix products, arithmetic and copies ran while one was open for 16% of the time, Pallas kernels for 0%

profile of v1, /device:TPU:6, one launch (start us, length us, event | category | flops | bytes accessed | tf_op | source)
XLA Modules:
  0.0 286.8 jit_solution(14487706611005433770)
XLA Ops:
  7.2 0.8 copy.56
  8.2 0.7 broadcast_multiply_fusion
  8.9 0.7 fusion.20
  9.7 1.3 fusion.22
  11.0 22.5 %all-reduce = (s32[]{:T(128)}, s32[]{:T(128)}) all-reduce(s32[]{:T(128)} %get-tuple-element.5, s32[]{:T(128)} %get-tuple-element.4), channel_id=1, replica_groups=mesh['dp'=64,'zh'=4,'core'=2] {'dp'}, use_global_device_ids=true, to_apply=%region_11.12 | all-reduce | flops 2 | bytes 16 | tf_op jit(solution)/shard_map/psum | solution.py:76
  34.8 1.2 reduce-window.6
  36.7 2.4 scatter_custom_fusion
  39.1 0.7 reduce_sum.58
  41.4 4.1 %gather_fusion.2 = f32[640]{0:T(1024)S(1)} fusion(f32[128]{0:T(128)S(1)} %fusion.21, s32[1024]{0:T(1024)S(1)} %get-tuple-element.24), kind=kCustom, calls=%fused_computation.2 | custom fusion | bytes 7680 | tf_op jit(solution)/shard_map/gather | solution.py:81
  45.6 4.3 %gather_fusion.3 = f32[640]{0:T(1024)S(1)} fusion(f32[512]{0:T(512)S(1)} %reshape.134, s32[1024]{0:T(1024)S(1)} %get-tuple-element.23), kind=kCustom, calls=%fused_computation.3 | custom fusion | bytes 7680 | tf_op jit(solution)/shard_map/gather | solution.py:81
  50.2 3.5 %gather_fusion = bf16[640,1024]{1,0:T(8,128)(2,1)} fusion(bf16[128,1024]{1,0:T(8,128)(2,1)S(1)} %get-tuple-element.22, s32[1024]{0:T(1024)S(1)} %get-tuple-element.24), kind=kCustom, calls=%fused_computation | custom fusion | bytes 2624000 | tf_op jit(solution)/shard_map/gather | solution.py:66
  53.6 2.4 gather.18
  56.2 54.1 %all_to_all.15 = bf16[64,10,1024]{2,1,0:T(8,128)(2,1)S(1)} all-to-all(bf16[64,10,1024]{2,1,0:T(8,128)(2,1)S(1)} %broadcast_select_fusion), channel_id=1, replica_groups=mesh['dp'=64,'zh'=4,'core'=2] {'dp'}, dimensions={0} | all-to-all | bytes 2621440 | tf_op jit(solution)/shard_map/all_to_all | solution.py:68
  110.3 1.3 reshape.130
  111.6 1.9 collective-permute-start
  113.7 2.8 gather_fusion.4
  116.5 2.1 reshape.138
  118.6 3.8 %multiply_convert_fusion = bf16[64,10,1024]{2,1,0:T(8,128)(2,1)} fusion(f32[64,10,1024]{2,1,0:T(8,128)} %reshape.138, f32[64,10]{1,0:T(8,128)S(1)} %mul.101), kind=kLoop, calls=%fused_computation.6 | loop fusion | flops 1310720 | bytes 3934720 | tf_op jit(solution)/shard_map/convert_element_type | solution.py:85
  122.5 7.9 %all-to-all-start.2 = ((bf16[64,10,1024]{2,1,0:T(8,128)(2,1)}), bf16[64,10,1024]{2,1,0:T(8,128)(2,1)}, u32[]{:S(2)}, u32[]{:S(2)}) async-start(bf16[64,10,1024]{2,1,0:T(8,128)(2,1)} %multiply_convert_fusion), calls=%async_computation.3 | async-start | bytes 4194304 | tf_op jit(solution)/shard_map/all_to_all | solution.py:88
  130.6 0.8 copy-done.8
  131.4 0.8 convolution_bitcast_fusion.1
  132.5 1.6 multiply_convert_fusion.3
  134.1 2.3 convolution_convert_fusion
  136.4 4.3 %reshape.131 = bf16[640,4,2,256]{3,2,1,0:T(2,128)(2,1)S(1)} reshape(bf16[640,2048]{1,0:T(8,128)(2,1)} %convolution_convert_fusion) | data formatting | bytes 5242880 | tf_op jit(solution)/shard_map/reshape | solution.py:109
  140.7 3.7 %fusion.28 = (bf16[640,4,1,256]{3,2,1,0:T(2,128)(2,1)S(1)}, bf16[640,4,1,256]{3,2,1,0:T(2,128)(2,1)S(1)}) fusion(bf16[640,4,2,256]{3,2,1,0:T(2,128)(2,1)S(1)} %reshape.131), kind=kLoop, calls=%fused_computation.88 | loop fusion | bytes 5242880 | tf_op jit(solution)/shard_map/slice | solution.py:110
  144.5 0.8 select_bitcast_fusion
  145.2 1.9 collective-permute-start.1
  147.2 3.0 %collective-permute-done.1 = bf16[640,4,256]{2,0,1:T(8,128)(2,1)S(1)} collective-permute-done((bf16[640,4,256]{2,0,1:T(8,128)(2,1)S(1)}, bf16[640,4,256]{2,0,1:T(8,128)(2,1)S(1)}, u32[]{:S(2)}, u32[]{:S(2)}) %collective-permute-start.1) | collective-permute-done | bytes 1310752 | tf_op jit(solution)/shard_map/ppermute | solution.py:10
  150.2 1.0 fusion
  151.2 1.0 copy.61
  152.2 1.9 reshape.132
  154.1 25.9 %all-to-all-done.2 = bf16[64,10,1024]{2,1,0:T(8,128)(2,1)} async-done(((bf16[64,10,1024]{2,1,0:T(8,128)(2,1)}), bf16[64,10,1024]{2,1,0:T(8,128)(2,1)}, u32[]{:S(2)}, u32[]{:S(2)}) %all-to-all-start.2) | async-done | bytes 1310752 | tf_op jit(solution)/shard_map/all_to_all | solution.py:88
  180.1 8.4 %all-to-all-start.1 = ((bf16[64,10,1024]{2,1,0:T(8,128)(2,1)}), bf16[64,10,1024]{2,1,0:T(8,128)(2,1)}, u32[]{:S(2)}, u32[]{:S(2)}) async-start(bf16[64,10,1024]{2,1,0:T(8,128)(2,1)} %reshape.132), calls=%async_computation.1 | async-start | bytes 4194304 | tf_op jit(solution)/shard_map/all_to_all | solution.py:113
  188.5 3.6 %reshape.135 = bf16[640,1024]{1,0:T(8,128)(2,1)} reshape(bf16[64,10,1024]{2,1,0:T(8,128)(2,1)} %all-to-all-done.2) | data formatting | bytes 2621440 | tf_op jit(solution)/shard_map/reshape | solution.py:89
  192.2 2.1 collective-permute-start.2
  194.3 43.6 %all-to-all-done.1 = bf16[64,10,1024]{2,1,0:T(8,128)(2,1)} async-done(((bf16[64,10,1024]{2,1,0:T(8,128)(2,1)}), bf16[64,10,1024]{2,1,0:T(8,128)(2,1)}, u32[]{:S(2)}, u32[]{:S(2)}) %all-to-all-start.1) | async-done | bytes 1310752 | tf_op jit(solution)/shard_map/all_to_all | solution.py:113
  237.9 2.6 reshape.133
  240.5 2.8 gather_fusion.1
  243.3 2.0 reshape.137
  245.3 0.9 multiply_reduce_fusion
  246.2 0.9 copy.63
  247.1 1.9 broadcast_select_fusion.2
  249.0 1.4 fusion.3
  250.4 0.9 fusion.5
  252.2 1.4 fusion.2
  253.6 1.5 fusion.1
  255.1 23.3 %reduce-scatter.2.cloned.1.call-done = f32[128,1,256]{2,0,1:T(8,128)} async-done(((f32[128,4,256]{2,0,1:T(8,128)}), f32[128,1,256]{2,0,1:T(8,128)}) %reduce-scatter.2.cloned.1.call-update) | async-done | bytes 131088 | tf_op jit(solution)/shard_map/reduce_scatter | solution.py:122
  278.4 1.5 convert_bitcast_fusion
  (54 shorter events, 4.4 us)
Async XLA Ops:
  7.2 126.9 %copy-start = (bf16[1,128,2048]{2,1,0:T(8,128)(2,1)S(1)}, bf16[1,128,2048]{2,1,0:T(8,128)(2,1)}, u32[]{:S(2)}) copy-start(bf16[1,128,2048]{2,1,0:T(8,128)(2,1)} %param.17) | copy-start | bytes 1572868
  45.6 4.5 %copy-start.6 = (bf16[128,2048]{1,0:T(8,128)(2,1)S(1)}, bf16[128,2048]{1,0:T(8,128)(2,1)}, u32[]{:S(2)}) copy-start(bf16[128,2048]{1,0:T(8,128)(2,1)} %param.10) | copy-start | bytes 1572868
  45.6 4.5 %copy-start.7 = (bf16[128,2048]{1,0:T(8,128)(2,1)S(1)}, bf16[128,2048]{1,0:T(8,128)(2,1)}, u32[]{:S(2)}) copy-start(bf16[128,2048]{1,0:T(8,128)(2,1)} %param.9) | copy-start | bytes 1572868
  111.6 18.8 %collective-permute-start = (bf16[640,1024]{1,0:T(8,128)(2,1)}, bf16[640,1024]{1,0:T(8,128)(2,1)S(1)}, u32[]{:S(2)}, u32[]{:S(2)}) collective-permute-start(bf16[640,1024]{1,0:T(8,128)(2,1)} %reshape.130), channel_id=1, source_target_pairs={{0,1},{1,0},{2,3},{3,2},{4,5},{5,4},{6,7},{7,6},{8,9},{9,8},{10,11... | collective-permute-start | bytes 3932168 | tf_op jit(solution)/shard_map/ppermute | solution.py:10
  122.5 7.9 %copy-start.1 = (bf16[640,1024]{1,0:T(8,128)(2,1)S(1)}, bf16[640,1024]{1,0:T(8,128)(2,1)}, u32[]{:S(2)}) copy-start(bf16[640,1024]{1,0:T(8,128)(2,1)} %reshape.130) | copy-start | bytes 3932164
  122.5 57.6 %all-to-all-start.2 = ((bf16[64,10,1024]{2,1,0:T(8,128)(2,1)}), bf16[64,10,1024]{2,1,0:T(8,128)(2,1)}, u32[]{:S(2)}, u32[]{:S(2)}) async-start(bf16[64,10,1024]{2,1,0:T(8,128)(2,1)} %multiply_convert_fusion), calls=%async_computation.3 | async-start | bytes 4194304 | tf_op jit(solution)/shard_map/all_to_all | solution.py:88
  130.4 1.0 copy-start.8
  130.6 1.7 copy-start.2
  130.6 1.7 copy-start.4
  131.4 1.1 copy-start.9
  132.5 1.6 copy-start.10
  145.2 4.9 %collective-permute-start.1 = (bf16[640,4,256]{2,0,1:T(8,128)(2,1)S(1)}, bf16[640,4,256]{2,0,1:T(8,128)(2,1)S(1)}, u32[]{:S(2)}, u32[]{:S(2)}) collective-permute-start(bf16[640,4,256]{2,0,1:T(8,128)(2,1)S(1)} %select_bitcast_fusion), channel_id=1, source_target_pairs={{0,1},{1,0},{2,3},{3,2},{4,5},{5,4},{6,7},{7,6},{8,9},{9,8},{10,11... | collective-permute-start | bytes 3932168 | tf_op jit(solution)/shard_map/ppermute | solution.py:10
  180.1 57.8 %all-to-all-start.1 = ((bf16[64,10,1024]{2,1,0:T(8,128)(2,1)}), bf16[64,10,1024]{2,1,0:T(8,128)(2,1)}, u32[]{:S(2)}, u32[]{:S(2)}) async-start(bf16[64,10,1024]{2,1,0:T(8,128)(2,1)} %reshape.132), calls=%async_computation.1 | async-start | bytes 4194304 | tf_op jit(solution)/shard_map/all_to_all | solution.py:113
  188.5 89.9 %reduce-scatter.2.cloned.1.call-start = ((), (), s32[]{:S(2)}) async-start(), calls=%async_computation.4 | async-start | bytes 655360 | tf_op jit(solution)/shard_map/reduce_scatter | solution.py:122
  192.2 55.0 %collective-permute-start.2 = (bf16[640,1024]{1,0:T(8,128)(2,1)}, bf16[640,1024]{1,0:T(8,128)(2,1)}, u32[]{:S(2)}, u32[]{:S(2)}) collective-permute-start(bf16[640,1024]{1,0:T(8,128)(2,1)} %reshape.135), channel_id=1, source_target_pairs={{0,1},{1,0},{2,3},{3,2},{4,5},{5,4},{6,7},{7,6},{8,9},{9,8},{10,11... | collective-permute-start | bytes 3932168 | tf_op jit(solution)/shard_map/ppermute | solution.py:10
  250.4 1.3 copy-start.3
  250.4 1.7 copy-start.5
  250.4 1.8 copy-start.11
  252.2 1.4 copy-start.12
Sparse Core Ops, SparseCore 0:
  247.2 31.1 reduce-scatter.1

commit v2 on v1

--- a/solution.py
+++ b/solution.py
@@ -61,37 +61,47 @@
     source_row = jnp.minimum(source, assigned - 1)
     source_tok = source_row // top_count
 
+    live_f = is_live.astype(jnp.float32)
+    slot_share = jnp.where(is_live, share_flat[source_row], 0.0)
+    share_hi = lax.reduce_precision(slot_share, exponent_bits=8, mantissa_bits=7)
+    rest = slot_share - share_hi
+    share_mid = lax.reduce_precision(rest, exponent_bits=8, mantissa_bits=7)
+    share_lo = rest - share_mid
+    slot_forget = live_f * forget[source_tok].astype(jnp.float32)
+    slot_retain = live_f * retain[source_tok].astype(jnp.float32)
+    per_slot = jnp.stack([share_hi, share_mid, share_lo, slot_forget, slot_retain], axis=1)
+    per_slot = per_slot.reshape(owners, capacity * 5)
+    local_counts = jnp.stack([jnp.sum(forget), jnp.sum(retain)]).astype(jnp.float32)
+    meta = jnp.concatenate(
+        [
+            per_slot,
+            jnp.broadcast_to(local_counts[None, :], (owners, 2)),
+            jnp.zeros((owners, features - capacity * 5 - 2), jnp.float32),
+        ],
+        axis=1,
+    ).astype(jnp.bfloat16)
     my_tokens = lax.dynamic_slice_in_dim(tokens, core * half, half, axis=1)
-    send_rows = jnp.where(
-        is_live[:, None], my_tokens[source_tok], jnp.zeros((), tokens.dtype)
-    ).reshape(owners, capacity, half)
-    recv_rows = lax.all_to_all(send_rows, "dp", split_axis=0, concat_axis=0, tiled=True)
-    recv_rows = recv_rows.reshape(slots_all, half)
-    other_rows = _swap_pair(recv_rows)
-    rows_in = jnp.concatenate(
-        [jnp.where(is_first, recv_rows, other_rows), jnp.where(is_first, other_rows, recv_rows)],
-        axis=1,
+    my_cotan = lax.dynamic_slice_in_dim(cotangent, core * half, half, axis=1)
+    both = jnp.concatenate([my_tokens, my_cotan], axis=1)
+    send = jnp.where(is_live[:, None], both[source_tok], jnp.zeros((), tokens.dtype))
+    send = jnp.concatenate([send.reshape(owners, capacity, features), meta[:, None, :]], axis=1)
+    recv = lax.all_to_all(send, "dp", split_axis=0, concat_axis=0, tiled=True)
+    got = recv[:, :capacity, :].reshape(slots_all, features)
+    got_meta = recv[:, capacity, :].astype(jnp.float32)
+    other = _swap_pair(got)
+    lower = jnp.where(is_first, got, other)
+    upper = jnp.where(is_first, other, got)
+    rows_in = jnp.concatenate([lower[:, :half], upper[:, :half]], axis=1)
+    cot_in = jnp.concatenate([lower[:, half:], upper[:, half:]], axis=1)
+
+    n_forget = jnp.sum(got_meta[:, capacity * 5])
+    n_retain = jnp.sum(got_meta[:, capacity * 5 + 1])
+    slot_meta = got_meta[:, : capacity * 5].reshape(slots_all, 5)
+    got_share = (slot_meta[:, 0] + slot_meta[:, 1]) + slot_meta[:, 2]
+    coefficient = float(top_count * tok_rows) * (
+        slot_meta[:, 4] / n_retain - slot_meta[:, 3] / n_forget
     )
-
-    n_forget, n_retain = lax.psum((jnp.sum(forget), jnp.sum(retain)), "dp")
-    coefficient = float(top_count * tok_rows) * (
-        retain.astype(jnp.float32) / n_retain.astype(jnp.float32)
-        - forget.astype(jnp.float32) / n_forget.astype(jnp.float32)
-    )
-    slot_weight = jnp.where(is_live, coefficient[source_tok] * share_flat[source_row], 0.0)
-    my_cotan = lax.dynamic_slice_in_dim(cotangent, core * half, half, axis=1)
-    send_cotan = (
-        (slot_weight[:, None] * my_cotan[source_tok].astype(jnp.float32))
-        .astype(jnp.bfloat16)
-        .reshape(owners, capacity, half)
-    )
-    recv_cotan = lax.all_to_all(send_cotan, "dp", split_axis=0, concat_axis=0, tiled=True)
-    recv_cotan = recv_cotan.reshape(slots_all, half)
-    other_cotan = _swap_pair(recv_cotan)
-    routed = jnp.concatenate(
-        [jnp.where(is_first, recv_cotan, other_cotan), jnp.where(is_first, other_cotan, recv_cotan)],
-        axis=1,
-    )
+    routed = ((coefficient * got_share)[:, None] * cot_in.astype(jnp.float32)).astype(jnp.bfloat16)
 
     contract_last = (((1,), (1,)), ((), ()))
     contract_first = (((0,), (0,)), ((), ()))
@@ -119,8 +129,10 @@
     )
     picked = returned.reshape(slots_all, groups * block)[target].astype(jnp.float32) * share_flat[:, None]
     token_terms = jnp.sum(picked.reshape(tok_rows, top_count, groups, block), axis=1)
-    mixed_out = lax.psum_scatter(token_terms, "zh", scatter_dimension=1, tiled=True)
-    mixed_out = mixed_out.reshape(tok_rows, block).astype(jnp.bfloat16)
+    spread = lax.all_to_all(
+        jnp.transpose(token_terms, (1, 0, 2)), "zh", split_axis=0, concat_axis=0, tiled=True
+    )
+    mixed_out = jnp.sum(spread, axis=0).astype(jnp.bfloat16)
 
     grad_down = jnp.dot(hidden, routed, preferred_element_type=jnp.float32)
     dhidden = lax.dot_general(

time: 288 us -> 285 us (0.990)
  waiting for transfers between devices: 95.8 us -> 55 us
  blocking collectives: 76.6 us -> 107 us
  between operations: 15.7 us -> 1.14 us
  local copies, waits for them, and re-layouts: 49.8 us -> 59.7 us
  other arithmetic: 16.6 us -> 25.3 us
  matrix products: 9.92 us -> 12.8 us
    all_to_all x1, blocking collectives: 54.1 us -> 107 us  [body(): recv = lax.all_to_all(send, 'dp', split_axis=0, concat_axis=0, tiled=True)]
    reduce_scatter x1 -> x0, waiting for transfers between devices: 23.3 us -> none  [body(): lax.psum_scatter(token_terms, 'zh', scatter_dimension=1, tiled=True)]
    psum x1 -> x0, blocking collectives: 22.5 us -> none  [body(): n_forget, n_retain = lax.psum((jnp.sum(forget), jnp.sum(retain)), 'dp')]
    all_to_all x1, waiting for transfers between devices: 25.9 us -> 7.33 us  [body(): lax.all_to_all(jnp.transpose(token_terms, (1, 0, 2)), 'zh', split_axis=0,...]
    gather x5, local copies, waits for them, and re-layouts: 17.1 us -> 22 us  [the longest x2 9.45 us: body(): both[source_tok]]
    ppermute x3 -> x2, waiting for transfers between devices: 3.01 us -> 7.7 us  [_swap_pair(): return lax.ppermute(x, 'core', [(0, 1), (1, 0)])]
    select_n x5 -> x3, other arithmetic: 2.3 us -> 6.57 us  [the longest x1 4.47 us: body(): jnp.where(is_live[:, None], both[source_tok], jnp.zeros((), tokens.dtype))]
    all_to_all x1, waiting for transfers between devices: 43.6 us -> 40 us  [body(): lax.all_to_all(pair_sum.reshape(owners, capacity, groups * block), 'dp',...]
  transfers between devices with their start and end apart: 6 -> 4, of which waited for: 4 -> 4; matrix products, arithmetic and copies ran while one was open for 16% -> 5% of each run, Pallas kernels for 0% -> 0%
where the time goes in v2:
time: 285 us; the launch traced here: 283 us
  blocking collectives  107 us (38%)
  local copies, waits for them, and re-layouts  59.7 us (21%)
  waiting for transfers between devices  55 us (19%)
  other arithmetic  25.3 us (9%)
  starting transfers between devices  21.6 us (8%)
  matrix products  12.8 us (4%)
    all_to_all x1, blocking collectives, body(): recv = lax.all_to_all(send, 'dp', split_axis=0, concat_axis=0, tiled=True)  107 us
    all_to_all x1, waiting for transfers between devices, body(): lax.all_to_all(pair_sum.reshape(owners, capacity, groups * block), 'dp',...  40 us
    gather x2, local copies, waits for them, and re-layouts, body(): both[source_tok]  9.45 us
    all_to_all x1, starting transfers between devices, body(): lax.all_to_all(jnp.transpose(token_terms, (1, 0, 2)), 'zh', split_axis=0,...  9.4 us
    all_to_all x1, starting transfers between devices, body(): lax.all_to_all(pair_sum.reshape(owners, capacity, groups * block), 'dp',...  8.04 us
    ppermute x2, waiting for transfers between devices, _swap_pair(): return lax.ppermute(x, 'core', [(0, 1), (1, 0)])  7.7 us
    all_to_all x1, waiting for transfers between devices, body(): lax.all_to_all(jnp.transpose(token_terms, (1, 0, 2)), 'zh', split_axis=0,...  7.33 us
  transfers between devices with their start and end apart: 4, of which 4 were waited for; matrix products, arithmetic and copies ran while one was open for 5% of the time, Pallas kernels for 0%

profile of v2, /device:TPU:6, one launch (start us, length us, event | category | flops | bytes accessed | tf_op | source)
XLA Modules:
  0.0 282.5 jit_solution(1429404724152241695)
XLA Ops:
  0.6 0.8 copy.53
  2.4 1.2 reduce-window.6
  4.3 2.4 scatter_custom_fusion
  7.5 1.3 fusion.29
  9.5 4.1 %gather_fusion.2 = s32[640]{0:T(1024)S(1)} fusion(s32[128]{0:T(128)S(1)} %get-tuple-element.7, s32[1024]{0:T(1024)S(1)} %get-tuple-element.29), kind=kCustom, calls=%fused_computation.2 | custom fusion | bytes 7680 | tf_op jit(solution)/shard_map/gather | solution.py:70
  13.6 4.1 %gather_fusion.3 = s32[640]{0:T(1024)S(1)} fusion(s32[128]{0:T(128)S(1)} %get-tuple-element.9, s32[1024]{0:T(1024)S(1)} %get-tuple-element.29), kind=kCustom, calls=%fused_computation.3 | custom fusion | bytes 7680 | tf_op jit(solution)/shard_map/gather | solution.py:71
  18.2 4.3 %gather_fusion.1 = f32[640]{0:T(1024)S(1)} fusion(f32[512]{0:T(512)S(1)} %reshape.180, s32[1024]{0:T(1024)S(1)} %get-tuple-element.28), kind=kCustom, calls=%fused_computation.1 | custom fusion | bytes 7680 | tf_op jit(solution)/shard_map/gather | solution.py:65
  23.1 4.1 %gather_fusion = bf16[640,2048]{1,0:T(8,128)(2,1)} fusion(bf16[128,2048]{1,0:T(8,128)(2,1)S(1)} %pad_maximum_fusion.2, s32[1024]{0:T(1024)S(1)} %get-tuple-element.29), kind=kCustom, calls=%fused_computation | custom fusion | bytes 5245440 | tf_op jit(solution)/shard_map/gather | solution.py:86
  27.2 5.4 %gather.18 = bf16[64,10,2048]{2,1,0:T(8,128)(2,1)} reshape(bf16[640,2048]{1,0:T(8,128)(2,1)} %gather_fusion) | data formatting | bytes 5242880 | tf_op jit(solution)/shard_map/gather | solution.py:86
  32.5 1.4 fusion.24
  33.9 4.5 %broadcast_select_fusion = bf16[64,10,2048]{2,1,0:T(8,128)(2,1)} fusion(bf16[64,10,2048]{2,1,0:T(8,128)(2,1)} %gather.18, pred[64,10]{1,0:T(8,128)(4,1)S(1)} %broadcast_in_dim.66), kind=kLoop, calls=%fused_computation.8 | loop fusion | flops 1310720 | bytes 5243520 | tf_op jit(solution)/shard_map/jit(_where)/select_n | solution.py:86
  38.7 2.9 %concatenate.31 = bf16[64,1,2048]{2,1,0:T(2,128)(2,1)S(1)} concatenate(bf16[64,1,50]{2,1,0:T(2,128)(2,1)S(1)} %concatenate.35, bf16[64,1,2]{2,1,0:T(2,128)(2,1)S(1)} %broadcast_in_dim.74, bf16[64,1,1996]{2,1,0:T(2,128)(2,1)S(1)} %broadcast_in_dim.75), dimensions={2} | concatenate | bytes 524288 | tf_op jit(solution)/shard_map/concatenate | solution.py:75
  41.6 3.5 %pad_maximum_fusion = bf16[64,11,2048]{2,1,0:T(8,128)(2,1)S(1)} fusion(bf16[64,1,2048]{2,1,0:T(2,128)(2,1)S(1)} %concatenate.31, bf16[64,10,2048]{2,1,0:T(8,128)(2,1)} %broadcast_select_fusion), kind=kLoop, calls=%fused_computation.7 | loop fusion | flops 5767168 | bytes 5767168 | tf_op jit(solution)/shard_map/concatenate | solution.py:87
  45.1 107.0 %all_to_all.15 = bf16[64,11,2048]{2,1,0:T(8,128)(2,1)} all-to-all(bf16[64,11,2048]{2,1,0:T(8,128)(2,1)S(1)} %pad_maximum_fusion), channel_id=1, replica_groups=mesh['dp'=64,'zh'=4,'core'=2] {'dp'}, dimensions={0} | all-to-all | bytes 5767168 | tf_op jit(solution)/shard_map/all_to_all | solution.py:88
  152.0 4.1 %reshape.181 = bf16[640,2048]{1,0:T(8,128)(2,1)S(1)} reshape(bf16[64,10,2048]{2,1,0:T(8,128)(2,1)} %bitcast.60) | data formatting | bytes 5242880 | tf_op jit(solution)/shard_map/reshape | solution.py:89
  156.1 2.1 collective-permute-start
  158.2 4.8 %collective-permute-done = bf16[640,2048]{1,0:T(8,128)(2,1)} collective-permute-done((bf16[640,2048]{1,0:T(8,128)(2,1)S(1)}, bf16[640,2048]{1,0:T(8,128)(2,1)}, u32[]{:S(2)}, u32[]{:S(2)}) %collective-permute-start) | collective-permute-done | bytes 2621472 | tf_op jit(solution)/shard_map/ppermute | solution.py:10
  163.1 2.1 broadcast_select_fusion.2
  165.2 1.4 fusion.31
  166.5 1.4 fusion.32
  167.9 0.8 convolution_bitcast_fusion.2
  169.3 1.6 multiply_convert_fusion.3
  171.5 2.4 convolution_convert_fusion
  173.9 4.3 %reshape.182 = bf16[640,4,2,256]{3,2,1,0:T(2,128)(2,1)S(1)} reshape(bf16[640,2048]{1,0:T(8,128)(2,1)} %convolution_convert_fusion) | data formatting | bytes 5242880 | tf_op jit(solution)/shard_map/reshape | solution.py:119
  178.2 3.7 %fusion.33 = (bf16[640,4,1,256]{3,2,1,0:T(2,128)(2,1)S(1)}, bf16[640,4,1,256]{3,2,1,0:T(2,128)(2,1)S(1)}) fusion(bf16[640,4,2,256]{3,2,1,0:T(2,128)(2,1)S(1)} %reshape.182), kind=kLoop, calls=%fused_computation.105 | loop fusion | bytes 5242880 | tf_op jit(solution)/shard_map/slice | solution.py:120
  182.7 2.0 collective-permute-start.1
  184.8 2.9 %collective-permute-done.1 = bf16[640,4,256]{2,0,1:T(8,128)(2,1)S(1)} collective-permute-done((bf16[640,4,256]{2,0,1:T(8,128)(2,1)S(1)}, bf16[640,4,256]{2,0,1:T(8,128)(2,1)S(1)}, u32[]{:S(2)}, u32[]{:S(2)}) %collective-permute-start.1) | collective-permute-done | bytes 1310752 | tf_op jit(solution)/shard_map/ppermute | solution.py:10
  187.6 1.0 fusion
  188.7 1.0 copy.61
  189.7 1.9 reshape.183
  191.5 8.0 %all-to-all-start.1 = ((bf16[64,10,1024]{2,1,0:T(8,128)(2,1)}), bf16[64,10,1024]{2,1,0:T(8,128)(2,1)}, u32[]{:S(2)}, u32[]{:S(2)}) async-start(bf16[64,10,1024]{2,1,0:T(8,128)(2,1)} %reshape.183), calls=%async_computation.1 | async-start | bytes 4194304 | tf_op jit(solution)/shard_map/all_to_all | solution.py:123
  199.6 2.2 slice_convert_fusion
  202.0 0.8 copy-done.7
  203.4 0.9 reshape.185
  204.3 1.6 slice_reduce_fusion.2
  205.9 1.9 fusion.9
  207.8 1.6 convolution_bitcast_fusion
  209.5 40.0 %all-to-all-done.1 = bf16[64,10,1024]{2,1,0:T(8,128)(2,1)} async-done(((bf16[64,10,1024]{2,1,0:T(8,128)(2,1)}), bf16[64,10,1024]{2,1,0:T(8,128)(2,1)}, u32[]{:S(2)}, u32[]{:S(2)}) %all-to-all-start.1) | async-done | bytes 1310752 | tf_op jit(solution)/shard_map/all_to_all | solution.py:123
  249.5 2.6 reshape.184
  252.1 2.8 gather_fusion.4
  254.8 2.0 reshape.187
  256.9 0.9 multiply_reduce_fusion
  257.8 0.9 copy.63
  258.7 9.4 %all-to-all-start.2 = ((f32[4,128,256]{2,1,0:T(8,128)}), f32[4,128,256]{2,1,0:T(8,128)S(1)}, u32[]{:S(2)}, u32[]{:S(2)}) async-start(f32[4,128,256]{2,1,0:T(8,128)} %copy.63), calls=%async_computation.2 | async-start | bytes 1048576 | tf_op jit(solution)/shard_map/all_to_all | solution.py:132
  268.1 3.4 %fusion.3 = bf16[1,128,2048]{2,1,0:T(8,128)(2,1)} fusion(bf16[128,640]{0,1:T(8,128)(2,1)S(1)} %copy-done.9, bf16[640,1024]{1,0:T(8,128)(2,1)} %get-tuple-element.16, bf16[640,1024]{1,0:T(8,128)(2,1)} %get-tuple-element.14, f32[640]{0:T(1024)S(1)} %fusion.9), kind=kOutput, calls=%fused_computation.20 | convolution fusion | flops 343670784 | bytes 3312128 | tf_op jit(solution)/shard_map/dot_general | solution.py:137
  271.6 1.4 fusion.2
  273.0 1.5 fusion.1
  274.5 7.3 %all-to-all-done.2 = f32[4,128,256]{2,1,0:T(8,128)S(1)} async-done(((f32[4,128,256]{2,1,0:T(8,128)}), f32[4,128,256]{2,1,0:T(8,128)S(1)}, u32[]{:S(2)}, u32[]{:S(2)}) %all-to-all-start.2) | async-done | bytes 524320 | tf_op jit(solution)/shard_map/all_to_all | solution.py:132
  (78 shorter events, 7.6 us)
Async XLA Ops:
  0.6 170.9 %copy-start = (bf16[1,128,2048]{2,1,0:T(8,128)(2,1)S(1)}, bf16[1,128,2048]{2,1,0:T(8,128)(2,1)}, u32[]{:S(2)}) copy-start(bf16[1,128,2048]{2,1,0:T(8,128)(2,1)} %param.17) | copy-start | bytes 1572868
  13.6 4.2 %copy-start.12 = (f32[128,4]{0,1:T(4,128)S(1)}, f32[128,4]{0,1:T(4,128)}, u32[]{:S(2)}) copy-start(f32[128,4]{0,1:T(4,128)} %param.12) | copy-start | bytes 6148
  17.7 5.3 %copy-start.10 = (bf16[128,2048]{1,0:T(8,128)(2,1)S(1)}, bf16[128,2048]{1,0:T(8,128)(2,1)}, u32[]{:S(2)}) copy-start(bf16[128,2048]{1,0:T(8,128)(2,1)} %param.10) | copy-start | bytes 1572868
  17.7 5.3 %copy-start.11 = (bf16[128,2048]{1,0:T(8,128)(2,1)S(1)}, bf16[128,2048]{1,0:T(8,128)(2,1)}, u32[]{:S(2)}) copy-start(bf16[128,2048]{1,0:T(8,128)(2,1)} %param.9) | copy-start | bytes 1572868
  156.1 6.9 %collective-permute-start = (bf16[640,2048]{1,0:T(8,128)(2,1)S(1)}, bf16[640,2048]{1,0:T(8,128)(2,1)}, u32[]{:S(2)}, u32[]{:S(2)}) collective-permute-start(bf16[640,2048]{1,0:T(8,128)(2,1)S(1)} %reshape.181), channel_id=1, source_target_pairs={{0,1},{1,0},{2,3},{3,2},{4,5},{5,4},{6,7},{7,6},{8,9},{9,8},{10,11... | collective-permute-start | bytes 7864328 | tf_op jit(solution)/shard_map/ppermute | solution.py:10
  166.5 2.3 copy-start.1
  166.5 1.4 copy-start.13
  167.9 1.1 copy-start.3
  167.9 1.4 copy-start.14
  169.3 1.6 copy-start.15
  170.9 0.7 copy-start.8
  182.7 4.9 %collective-permute-start.1 = (bf16[640,4,256]{2,0,1:T(8,128)(2,1)S(1)}, bf16[640,4,256]{2,0,1:T(8,128)(2,1)S(1)}, u32[]{:S(2)}, u32[]{:S(2)}) collective-permute-start(bf16[640,4,256]{2,0,1:T(8,128)(2,1)S(1)} %select_bitcast_fusion), channel_id=1, source_target_pairs={{0,1},{1,0},{2,3},{3,2},{4,5},{5,4},{6,7},{7,6},{8,9},{9,8},{10,11... | collective-permute-start | bytes 3932168 | tf_op jit(solution)/shard_map/ppermute | solution.py:10
  191.5 57.9 %all-to-all-start.1 = ((bf16[64,10,1024]{2,1,0:T(8,128)(2,1)}), bf16[64,10,1024]{2,1,0:T(8,128)(2,1)}, u32[]{:S(2)}, u32[]{:S(2)}) async-start(bf16[64,10,1024]{2,1,0:T(8,128)(2,1)} %reshape.183), calls=%async_computation.1 | async-start | bytes 4194304 | tf_op jit(solution)/shard_map/all_to_all | solution.py:123
  199.6 8.2 %copy-start.5 = (bf16[640,1024]{1,0:T(8,128)(2,1)S(1)}, bf16[640,1024]{1,0:T(8,128)(2,1)}, u32[]{:S(2)}) copy-start(bf16[640,1024]{1,0:T(8,128)(2,1)} %get-tuple-element.14) | copy-start | bytes 3932164
  199.6 8.2 %copy-start.6 = (bf16[640,1024]{1,0:T(8,128)(2,1)S(1)}, bf16[640,1024]{1,0:T(8,128)(2,1)}, u32[]{:S(2)}) copy-start(bf16[640,1024]{1,0:T(8,128)(2,1)} %get-tuple-element.16) | copy-start | bytes 3932164
  202.0 0.8 copy-start.7
  256.9 11.2 %copy-start.9 = (bf16[128,640]{0,1:T(8,128)(2,1)S(1)}, bf16[128,640]{0,1:T(8,128)(2,1)}, u32[]{:S(2)}) copy-start(bf16[128,640]{0,1:T(8,128)(2,1)} %copy-done.8) | copy-start | bytes 491524
  258.7 23.2 %all-to-all-start.2 = ((f32[4,128,256]{2,1,0:T(8,128)}), f32[4,128,256]{2,1,0:T(8,128)S(1)}, u32[]{:S(2)}, u32[]{:S(2)}) async-start(f32[4,128,256]{2,1,0:T(8,128)} %copy.63), calls=%async_computation.2 | async-start | bytes 1048576 | tf_op jit(solution)/shard_map/all_to_all | solution.py:132
  268.1 3.4 %copy-start.2 = (bf16[640,1024]{1,0:T(8,128)(2,1)S(1)}, bf16[640,1024]{1,0:T(8,128)(2,1)}, u32[]{:S(2)}) copy-start(bf16[640,1024]{1,0:T(8,128)(2,1)} %copy-done.1) | copy-start | bytes 3932164
  268.1 3.4 %copy-start.4 = (bf16[640,1024]{1,0:T(8,128)(2,1)S(1)}, bf16[640,1024]{1,0:T(8,128)(2,1)}, u32[]{:S(2)}) copy-start(bf16[640,1024]{1,0:T(8,128)(2,1)} %copy-done.3) | copy-start | bytes 3932164
  268.1 3.4 %copy-start.16 = (f32[128,640]{0,1:T(8,128)S(1)}, f32[128,640]{0,1:T(8,128)}, u32[]{:S(2)}) copy-start(f32[128,640]{0,1:T(8,128)} %copy-done.15) | copy-start | bytes 983044
  268.1 3.4 %copy-start.18 = (f32[128,640]{0,1:T(8,128)S(1)}, f32[128,640]{0,1:T(8,128)}, u32[]{:S(2)}) copy-start(f32[128,640]{0,1:T(8,128)} %convolution_bitcast_fusion) | copy-start | bytes 983044
  271.6 1.5 copy-start.17

commit v3 on v2

--- a/solution.py
+++ b/solution.py
@@ -1,9 +1,81 @@
+import functools
+
 import jax
 import jax.numpy as jnp
 import numpy as np
 from jax import lax
+from jax.experimental import pallas as pl
+from jax.experimental.pallas import tpu as pltpu
 from jax.sharding import Mesh
 from jax.sharding import PartitionSpec as P
+
+
+MESH = pl.DeviceIdType.MESH
+
+
+def _exchange_kernel(n, x_ref, y_ref, send_sem, recv_sem, own_sem):
+    me = lax.axis_index("dp")
+
+    def copy_to(peer):
+        return pltpu.make_async_remote_copy(
+            src_ref=x_ref.at[peer],
+            dst_ref=y_ref.at[me],
+            send_sem=send_sem.at[peer],
+            recv_sem=recv_sem.at[me],
+            device_id={"dp": peer},
+            device_id_type=MESH,
+        )
+
+    def copy_from(source):
+        return pltpu.make_async_remote_copy(
+            src_ref=x_ref.at[source],
+            dst_ref=y_ref.at[source],
+            send_sem=send_sem.at[source],
+            recv_sem=recv_sem.at[source],
+            device_id={"dp": source},
+            device_id_type=MESH,
+        )
+
+    barrier = pltpu.get_barrier_semaphore()
+
+    def greet(i, carry):
+        pl.semaphore_signal(barrier, inc=1, device_id={"dp": lax.rem(me + i, n)}, device_id_type=MESH)
+        return carry
+
+    lax.fori_loop(1, n, greet, 0)
+    pl.semaphore_wait(barrier, n - 1)
+    own = pltpu.make_async_copy(x_ref.at[me], y_ref.at[me], own_sem)
+    own.start()
+
+    def send(i, carry):
+        copy_to(lax.rem(me + i, n)).start()
+        return carry
+
+    lax.fori_loop(1, n, send, 0)
+
+    def finish(i, carry):
+        copy_to(lax.rem(me + i, n)).wait_send()
+        copy_from(lax.rem(me + n - i, n)).wait_recv()
+        return carry
+
+    lax.fori_loop(1, n, finish, 0)
+    own.wait()
+
+
+def _exchange(x, collective_id):
+    n = x.shape[0]
+    return pl.pallas_call(
+        functools.partial(_exchange_kernel, n),
+        out_shape=jax.ShapeDtypeStruct(x.shape, x.dtype),
+        in_specs=[pl.BlockSpec(memory_space=pl.ANY)],
+        out_specs=pl.BlockSpec(memory_space=pl.ANY),
+        scratch_shapes=[
+            pltpu.SemaphoreType.DMA((n,)),
+            pltpu.SemaphoreType.DMA((n,)),
+            pltpu.SemaphoreType.DMA(()),
+        ],
+        compiler_params=pltpu.CompilerParams(collective_id=collective_id, has_side_effects=True),
+    )(x)
 
 
 def _swap_pair(x):
@@ -84,10 +156,14 @@
     my_cotan = lax.dynamic_slice_in_dim(cotangent, core * half, half, axis=1)
     both = jnp.concatenate([my_tokens, my_cotan], axis=1)
     send = jnp.where(is_live[:, None], both[source_tok], jnp.zeros((), tokens.dtype))
-    send = jnp.concatenate([send.reshape(owners, capacity, features), meta[:, None, :]], axis=1)
-    recv = lax.all_to_all(send, "dp", split_axis=0, concat_axis=0, tiled=True)
-    got = recv[:, :capacity, :].reshape(slots_all, features)
-    got_meta = recv[:, capacity, :].astype(jnp.float32)
+    lanes = 128
+    send = jnp.concatenate(
+        [send.reshape(owners, capacity * features // lanes, lanes), meta.reshape(owners, features // lanes, lanes)],
+        axis=1,
+    )
+    recv = _exchange(send, 0)
+    got = recv[:, : capacity * features // lanes, :].reshape(slots_all, features)
+    got_meta = recv[:, capacity * features // lanes :, :].reshape(owners, features).astype(jnp.float32)
     other = _swap_pair(got)
     lower = jnp.where(is_first, got, other)
     upper = jnp.where(is_first, other, got)
@@ -120,13 +196,7 @@
     keep = jnp.where(is_first, pieces[:, :, 0, :], pieces[:, :, 1, :])
     give = jnp.where(is_first, pieces[:, :, 1, :], pieces[:, :, 0, :])
     pair_sum = (keep.astype(jnp.float32) + _swap_pair(give).astype(jnp.float32)).astype(jnp.bfloat16)
-    returned = lax.all_to_all(
-        pair_sum.reshape(owners, capacity, groups * block),
-        "dp",
-        split_axis=0,
-        concat_axis=0,
-        tiled=True,
-    )
+    returned = _exchange(pair_sum.reshape(owners, capacity * groups * block // lanes, lanes), 1)
     picked = returned.reshape(slots_all, groups * block)[target].astype(jnp.float32) * share_flat[:, None]
     token_terms = jnp.sum(picked.reshape(tok_rows, top_count, groups, block), axis=1)
     spread = lax.all_to_all(

time: 285 us -> 238 us (0.84)
  Pallas kernels: 0 us -> 114 us
  blocking collectives: 107 us -> 0 us
  waiting for transfers between devices: 55 us -> 12.9 us
  starting transfers between devices: 21.6 us -> 13.8 us
    pallas_call x0 -> x2, Pallas kernels: none -> 114 us  [_exchange(): pl.pallas_call(functools.partial(_exchange_kernel, n), out_shape=jax.Shap...]
    all_to_all x1 -> x0, blocking collectives: 107 us -> none  [body(): recv = lax.all_to_all(send, 'dp', split_axis=0, concat_axis=0, tiled=True)]
    all_to_all x1 -> x0, waiting for transfers between devices: 40 us -> none  [body(): lax.all_to_all(pair_sum.reshape(owners, capacity, groups * block), 'dp',...]
    all_to_all x1 -> x0, starting transfers between devices: 8.04 us -> none  [body(): lax.all_to_all(pair_sum.reshape(owners, capacity, groups * block), 'dp',...]
    slice x1, local copies, waits for them, and re-layouts: 3.72 us -> 6.85 us  [body(): keep = jnp.where(is_first, pieces[:, :, 0, :], pieces[:, :, 1, :])]
    reshape x2 -> x3, local copies, waits for them, and re-layouts: 5.94 us -> 6.71 us  [the longest x1 3.47 us: body(): pair_sum.reshape(owners, capacity * groups * block // lanes, lanes)]
  transfers between devices with their start and end apart: 4 -> 3, of which waited for: 4 -> 2; matrix products, arithmetic and copies ran while one was open for 5% -> 6% of each run, Pallas kernels for 0% -> 0%
where the time goes in v3:
time: 238 us; the launch traced here: 235 us
  Pallas kernels  114 us (48%)
  local copies, waits for them, and re-layouts  58.4 us (25%)
  other arithmetic  23.1 us (10%)
  starting transfers between devices  13.8 us (6%)
  waiting for transfers between devices  12.9 us (5%)
  matrix products  12.4 us (5%)
    pallas_call x2, Pallas kernels, _exchange(): pl.pallas_call(functools.partial(_exchange_kernel, n), out_shape=jax.Shap...  114 us
    all_to_all x1, starting transfers between devices, body(): lax.all_to_all(jnp.transpose(token_terms, (1, 0, 2)), 'zh', split_axis=0,...  9.34 us
    all_to_all x1, waiting for transfers between devices, body(): lax.all_to_all(jnp.transpose(token_terms, (1, 0, 2)), 'zh', split_axis=0,...  7.97 us
    gather x2, local copies, waits for them, and re-layouts, body(): both[source_tok]  7.96 us
    slice x1, local copies, waits for them, and re-layouts, body(): keep = jnp.where(is_first, pieces[:, :, 0, :], pieces[:, :, 1, :])  6.85 us
    ppermute x2, waiting for transfers between devices, _swap_pair(): return lax.ppermute(x, 'core', [(0, 1), (1, 0)])  4.9 us
  transfers between devices with their start and end apart: 3, of which 2 were waited for; matrix products, arithmetic and copies ran while one was open for 6% of the time, Pallas kernels for 0%

profile of v3, /device:TPU:6, one launch (start us, length us, event | category | flops | bytes accessed | tf_op | source)
XLA Modules:
  0.0 235.3 jit_solution(8672342506129923930)
XLA Ops:
  0.6 0.8 copy.51
  1.7 0.7 broadcast_multiply_fusion
  2.4 1.2 reduce-window.6
  4.3 2.4 %scatter_custom_fusion = s32[640]{0:T(1024)S(1)} fusion(s32[512]{0:T(512)S(1)} %bitcast.71, s32[512]{0:T(512)S(1)} %iota.20, s32[]{:T(128)} %constant.56.clone.1), kind=kCustom, calls=%fused_computation.79 | custom fusion | bytes 2564 | tf_op jit(solution)/shard_map/scatter | solution.py:130
  6.8 0.7 fusion.23
  7.5 1.3 fusion.29
  9.5 4.1 %gather_fusion.2 = s32[640]{0:T(1024)S(1)} fusion(s32[128]{0:T(128)S(1)} %get-tuple-element.7, s32[1024]{0:T(1024)S(1)} %get-tuple-element.29), kind=kCustom, calls=%fused_computation.2 | custom fusion | bytes 7680 | tf_op jit(solution)/shard_map/gather | solution.py:142
  13.6 4.1 %gather_fusion.3 = s32[640]{0:T(1024)S(1)} fusion(s32[128]{0:T(128)S(1)} %get-tuple-element.9, s32[1024]{0:T(1024)S(1)} %get-tuple-element.29), kind=kCustom, calls=%fused_computation.3 | custom fusion | bytes 7680 | tf_op jit(solution)/shard_map/gather | solution.py:143
  18.2 4.3 %gather_fusion.1 = f32[640]{0:T(1024)S(1)} fusion(f32[512]{0:T(512)S(1)} %reshape.143, s32[1024]{0:T(1024)S(1)} %get-tuple-element.28), kind=kCustom, calls=%fused_computation.1 | custom fusion | bytes 7680 | tf_op jit(solution)/shard_map/gather | solution.py:137
  23.0 1.4 fusion.24
  24.8 4.1 %gather_fusion = bf16[640,2048]{1,0:T(8,128)(2,1)} fusion(bf16[128,2048]{1,0:T(8,128)(2,1)S(1)} %pad_maximum_fusion.2, s32[1024]{0:T(1024)S(1)} %get-tuple-element.29), kind=kCustom, calls=%fused_computation | custom fusion | bytes 5245440 | tf_op jit(solution)/shard_map/gather | solution.py:158
  28.9 3.9 %gather.18 = bf16[64,160,128]{2,1,0:T(8,128)(2,1)S(1)} reshape(bf16[640,2048]{1,0:T(8,128)(2,1)} %gather_fusion) | data formatting | bytes 5242880 | tf_op jit(solution)/shard_map/gather | solution.py:158
  33.0 2.0 broadcast_select_fusion
  35.0 1.8 pad_maximum_fusion.x_ref
  36.8 73.5 %shard_map.120 = bf16[64,176,128]{2,1,0:T(8,128)(2,1)} custom-call(bf16[64,176,128]{2,1,0:T(8,128)(2,1)} %pad_maximum_fusion.x_ref), custom_call_target="tpu_custom_call" | custom-call | tf_op jit(solution)/shard_map/pallas_call | solution.py:67
  110.3 1.7 slice-done
  112.1 3.1 %reshape.145 = bf16[640,2048]{1,0:T(8,128)(2,1)} reshape(bf16[64,160,128]{2,1,0:T(8,128)(2,1)S(1)} %slice-done) | data formatting | bytes 5242880 | tf_op jit(solution)/shard_map/reshape | solution.py:165
  115.2 2.1 collective-permute-start
  117.3 4.9 %collective-permute-done = bf16[640,2048]{1,0:T(8,128)(2,1)S(1)} collective-permute-done((bf16[640,2048]{1,0:T(8,128)(2,1)}, bf16[640,2048]{1,0:T(8,128)(2,1)S(1)}, u32[]{:S(2)}, u32[]{:S(2)}) %collective-permute-start) | collective-permute-done | bytes 2621472 | tf_op jit(solution)/shard_map/ppermute | solution.py:82
  122.2 2.1 broadcast_select_fusion.2
  124.2 1.3 fusion.31
  125.6 1.3 fusion.32
  127.0 0.8 convolution_bitcast_fusion.2
  128.4 1.6 multiply_convert_fusion.3
  130.0 0.8 convolution_convert_fusion
  130.8 3.6 %reshape.146 = bf16[640,4,2,256]{3,2,1,0:T(2,128)(2,1)} reshape(bf16[640,2048]{1,0:T(8,128)(2,1)S(1)} %convolution_convert_fusion) | data formatting | bytes 5242880 | tf_op jit(solution)/shard_map/reshape | solution.py:195
  134.4 6.9 %fusion.33 = (bf16[640,4,1,256]{3,2,1,0:T(2,128)(2,1)S(1)}, bf16[640,4,1,256]{3,2,1,0:T(2,128)(2,1)S(1)}) fusion(bf16[640,4,2,256]{3,2,1,0:T(2,128)(2,1)} %reshape.146), kind=kLoop, calls=%fused_computation.105 | loop fusion | bytes 5242880 | tf_op jit(solution)/shard_map/slice | solution.py:196
  141.3 2.1 select_bitcast_fusion
  143.4 2.4 %collective-permute-start.1 = (bf16[640,4,256]{2,1,0:T(4,128)(2,1)}, bf16[640,4,256]{2,1,0:T(4,128)(2,1)}, u32[]{:S(2)}, u32[]{:S(2)}) collective-permute-start(bf16[640,4,256]{2,1,0:T(4,128)(2,1)} %select_bitcast_fusion), channel_id=1, source_target_pairs={{0,1},{1,0},{2,3},{3,2},{4,5},{5,4},{6,7},{7,6},{8,9},{9,8},{10,11... | collective-permute-start | bytes 3932168 | tf_op jit(solution)/shard_map/ppermute | solution.py:82
  146.0 0.8 copy-done.8
  147.4 0.9 reshape.149
  148.3 1.6 slice_reduce_fusion.2
  150.0 1.9 fusion.9
  151.8 2.8 %convolution_bitcast_fusion = f32[128,640]{0,1:T(8,128)S(1)} fusion(bf16[1,128,2048]{2,1,0:T(8,128)(2,1)S(1)} %copy-done, bf16[640,1024]{1,0:T(8,128)(2,1)} %get-tuple-element.16, bf16[640,1024]{1,0:T(8,128)(2,1)} %get-tuple-element.14, f32[640]{0:T(1024)S(1)} %fusion.9), kind=kOutput, calls=%fused_computation.23 | convolution fusion | flops 343408640 | bytes 3475968 | tf_op jit(solution)/shard_map/dot_general | solution.py:208
  154.6 3.7 %fusion = bf16[640,4,256]{2,1,0:T(4,128)(2,1)} fusion(bf16[640,4,256]{2,1,0:T(4,128)(2,1)} %collective-permute-done.1, pred[]{:T(512)S(6)} %eq.41, bf16[640,4,1,256]{3,2,1,0:T(2,128)(2,1)S(1)} %copy-done.2, bf16[640,4,1,256]{3,2,1,0:T(2,128)(2,1)S(1)} %get-tuple-element.18), kind=kLoop, calls=%fused_computation.11 | loop fusion | flops 3276800 | bytes 5242881 | tf_op jit(solution)/shard_map/convert_element_type | solution.py:198
  158.3 3.5 %reshape.147.x_ref = bf16[64,80,128]{2,1,0:T(8,128)(2,1)} reshape(bf16[640,4,256]{2,1,0:T(4,128)(2,1)} %fusion) | data formatting | bytes 2621440 | tf_op jit(solution)/shard_map/reshape | solution.py:199
  161.8 40.0 %shard_map.121 = bf16[64,80,128]{2,1,0:T(8,128)(2,1)} custom-call(bf16[64,80,128]{2,1,0:T(8,128)(2,1)} %reshape.147.x_ref), custom_call_target="tpu_custom_call" | custom-call | tf_op jit(solution)/shard_map/pallas_call | solution.py:67
  201.9 2.4 %reshape.148 = bf16[640,1024]{1,0:T(8,128)(2,1)S(1)} reshape(bf16[64,80,128]{2,1,0:T(8,128)(2,1)} %shard_map.121) | data formatting | bytes 2621440 | tf_op jit(solution)/shard_map/reshape | solution.py:200
  204.2 2.8 %gather_fusion.4 = bf16[512,1024]{1,0:T(8,128)(2,1)} fusion(bf16[640,1024]{1,0:T(8,128)(2,1)S(1)} %reshape.148, s32[1024]{0:T(1024)S(1)} %pad_clamp_fusion), kind=kCustom, calls=%fused_computation.4 | custom fusion | bytes 2099200 | tf_op jit(solution)/shard_map/gather | solution.py:200
  207.0 2.0 reshape.151
  209.0 0.9 multiply_reduce_fusion
  210.0 0.9 copy.61
  210.9 9.3 %all-to-all-start = ((f32[4,128,256]{2,1,0:T(8,128)}), f32[4,128,256]{2,1,0:T(8,128)S(1)}, u32[]{:S(2)}, u32[]{:S(2)}) async-start(f32[4,128,256]{2,1,0:T(8,128)} %copy.61), calls=%async_computation | async-start | bytes 1048576 | tf_op jit(solution)/shard_map/all_to_all | solution.py:202
  220.2 3.4 %fusion.3 = bf16[1,128,2048]{2,1,0:T(8,128)(2,1)} fusion(bf16[128,640]{0,1:T(8,128)(2,1)S(1)} %copy-done.10, bf16[640,1024]{1,0:T(8,128)(2,1)} %get-tuple-element.16, bf16[640,1024]{1,0:T(8,128)(2,1)} %get-tuple-element.14, f32[640]{0:T(1024)S(1)} %fusion.9), kind=kOutput, calls=%fused_computation.20 | convolution fusion | flops 343670784 | bytes 3312128 | tf_op jit(solution)/shard_map/dot_general | solution.py:207
  223.7 1.4 fusion.2
  225.1 1.5 fusion.1
  226.6 8.0 %all-to-all-done = f32[4,128,256]{2,1,0:T(8,128)S(1)} async-done(((f32[4,128,256]{2,1,0:T(8,128)}), f32[4,128,256]{2,1,0:T(8,128)S(1)}, u32[]{:S(2)}, u32[]{:S(2)}) %all-to-all-start) | async-done | bytes 524320 | tf_op jit(solution)/shard_map/all_to_all | solution.py:202
  234.6 0.7 reduce_sum.90
  (82 shorter events, 4.5 us)
Async XLA Ops:
  0.6 129.3 %copy-start = (bf16[1,128,2048]{2,1,0:T(8,128)(2,1)S(1)}, bf16[1,128,2048]{2,1,0:T(8,128)(2,1)}, u32[]{:S(2)}) copy-start(bf16[1,128,2048]{2,1,0:T(8,128)(2,1)} %param.17) | copy-start | bytes 1572868
  13.6 4.2 %copy-start.13 = (f32[128,4]{0,1:T(4,128)S(1)}, f32[128,4]{0,1:T(4,128)}, u32[]{:S(2)}) copy-start(f32[128,4]{0,1:T(4,128)} %param.12) | copy-start | bytes 6148
  18.2 6.5 %copy-start.11 = (bf16[128,2048]{1,0:T(8,128)(2,1)S(1)}, bf16[128,2048]{1,0:T(8,128)(2,1)}, u32[]{:S(2)}) copy-start(bf16[128,2048]{1,0:T(8,128)(2,1)} %param.10) | copy-start | bytes 1572868
  18.2 6.5 %copy-start.12 = (bf16[128,2048]{1,0:T(8,128)(2,1)S(1)}, bf16[128,2048]{1,0:T(8,128)(2,1)}, u32[]{:S(2)}) copy-start(bf16[128,2048]{1,0:T(8,128)(2,1)} %param.9) | copy-start | bytes 1572868
  110.3 1.7 slice-start
  115.2 7.0 %collective-permute-start = (bf16[640,2048]{1,0:T(8,128)(2,1)}, bf16[640,2048]{1,0:T(8,128)(2,1)S(1)}, u32[]{:S(2)}, u32[]{:S(2)}) collective-permute-start(bf16[640,2048]{1,0:T(8,128)(2,1)} %reshape.145), channel_id=1, source_target_pairs={{0,1},{1,0},{2,3},{3,2},{4,5},{5,4},{6,7},{7,6},{8,9},{9,8},{10,11... | collective-permute-start | bytes 7864328 | tf_op jit(solution)/shard_map/ppermute | solution.py:82
  125.6 2.3 copy-start.4
  125.6 1.4 copy-start.14
  126.9 1.2 copy-start.6
  127.0 1.4 copy-start.15
  128.4 1.6 copy-start.16
  130.0 4.4 %copy-start.9 = (bf16[128,640]{0,1:T(8,128)(2,1)}, bf16[128,640]{0,1:T(8,128)(2,1)S(1)}, u32[]{:S(2)}) copy-start(bf16[128,640]{0,1:T(8,128)(2,1)S(1)} %get-tuple-element.26) | copy-start | bytes 491524
  141.2 2.2 copy-start.1
  141.3 4.5 %copy-start.3 = (bf16[64,176,128]{2,1,0:T(8,128)(2,1)S(1)}, bf16[64,176,128]{2,1,0:T(8,128)(2,1)}, u32[]{:S(2)}) copy-start(bf16[64,176,128]{2,1,0:T(8,128)(2,1)} %shard_map.120) | copy-start | bytes 8650756
  143.4 11.2 %collective-permute-start.1 = (bf16[640,4,256]{2,1,0:T(4,128)(2,1)}, bf16[640,4,256]{2,1,0:T(4,128)(2,1)}, u32[]{:S(2)}, u32[]{:S(2)}) collective-permute-start(bf16[640,4,256]{2,1,0:T(4,128)(2,1)} %select_bitcast_fusion), channel_id=1, source_target_pairs={{0,1},{1,0},{2,3},{3,2},{4,5},{5,4},{6,7},{7,6},{8,9},{9,8},{10,11... | collective-permute-start | bytes 3932168 | tf_op jit(solution)/shard_map/ppermute | solution.py:82
  146.0 0.8 copy-start.8
  151.8 2.8 %copy-start.2 = (bf16[640,4,1,256]{3,2,1,0:T(2,128)(2,1)S(1)}, bf16[640,4,1,256]{3,2,1,0:T(2,128)(2,1)}, u32[]{:S(2)}) copy-start(bf16[640,4,1,256]{3,2,1,0:T(2,128)(2,1)} %copy-done.1) | copy-start | bytes 3932164
  209.0 11.2 %copy-start.10 = (bf16[128,640]{0,1:T(8,128)(2,1)S(1)}, bf16[128,640]{0,1:T(8,128)(2,1)}, u32[]{:S(2)}) copy-start(bf16[128,640]{0,1:T(8,128)(2,1)} %copy-done.9) | copy-start | bytes 491524
  210.9 23.7 %all-to-all-start = ((f32[4,128,256]{2,1,0:T(8,128)}), f32[4,128,256]{2,1,0:T(8,128)S(1)}, u32[]{:S(2)}, u32[]{:S(2)}) async-start(f32[4,128,256]{2,1,0:T(8,128)} %copy.61), calls=%async_computation | async-start | bytes 1048576 | tf_op jit(solution)/shard_map/all_to_all | solution.py:202
  220.2 3.4 %copy-start.5 = (bf16[640,1024]{1,0:T(8,128)(2,1)S(1)}, bf16[640,1024]{1,0:T(8,128)(2,1)}, u32[]{:S(2)}) copy-start(bf16[640,1024]{1,0:T(8,128)(2,1)} %copy-done.4) | copy-start | bytes 3932164
  220.2 3.4 %copy-start.7 = (bf16[640,1024]{1,0:T(8,128)(2,1)S(1)}, bf16[640,1024]{1,0:T(8,128)(2,1)}, u32[]{:S(2)}) copy-start(bf16[640,1024]{1,0:T(8,128)(2,1)} %copy-done.6) | copy-start | bytes 3932164
  220.2 3.4 %copy-start.17 = (f32[128,640]{0,1:T(8,128)S(1)}, f32[128,640]{0,1:T(8,128)}, u32[]{:S(2)}) copy-start(f32[128,640]{0,1:T(8,128)} %copy-done.16) | copy-start | bytes 983044
  223.7 1.5 copy-start.18

commit v4 on v3

--- a/solution.py
+++ b/solution.py
@@ -124,23 +124,16 @@
     slot_id = jnp.sum(before * one_hot, axis=1)
     target = flat_ids * capacity + slot_id
     slots_all = owners * capacity
-    source = (
-        jnp.full((slots_all,), assigned, jnp.int32)
-        .at[target]
-        .set(jnp.arange(assigned, dtype=jnp.int32))
-    )
-    is_live = source < assigned
-    source_row = jnp.minimum(source, assigned - 1)
-    source_tok = source_row // top_count
-
-    live_f = is_live.astype(jnp.float32)
-    slot_share = jnp.where(is_live, share_flat[source_row], 0.0)
+    hit = target[None, :] == jnp.arange(slots_all, dtype=jnp.int32)[:, None]
+    hit_tok = jnp.any(hit.reshape(slots_all, tok_rows, top_count), axis=2)
+
+    slot_share = jnp.sum(jnp.where(hit, share_flat[None, :], 0.0), axis=1)
     share_hi = lax.reduce_precision(slot_share, exponent_bits=8, mantissa_bits=7)
     rest = slot_share - share_hi
     share_mid = lax.reduce_precision(rest, exponent_bits=8, mantissa_bits=7)
     share_lo = rest - share_mid
-    slot_forget = live_f * forget[source_tok].astype(jnp.float32)
-    slot_retain = live_f * retain[source_tok].astype(jnp.float32)
+    slot_forget = jnp.sum(jnp.where(hit_tok, forget[None, :], 0), axis=1).astype(jnp.float32)
+    slot_retain = jnp.sum(jnp.where(hit_tok, retain[None, :], 0), axis=1).astype(jnp.float32)
     per_slot = jnp.stack([share_hi, share_mid, share_lo, slot_forget, slot_retain], axis=1)
     per_slot = per_slot.reshape(owners, capacity * 5)
     local_counts = jnp.stack([jnp.sum(forget), jnp.sum(retain)]).astype(jnp.float32)
@@ -155,7 +148,7 @@
     my_tokens = lax.dynamic_slice_in_dim(tokens, core * half, half, axis=1)
     my_cotan = lax.dynamic_slice_in_dim(cotangent, core * half, half, axis=1)
     both = jnp.concatenate([my_tokens, my_cotan], axis=1)
-    send = jnp.where(is_live[:, None], both[source_tok], jnp.zeros((), tokens.dtype))
+    send = jnp.dot(hit_tok.astype(both.dtype), both, preferred_element_type=jnp.float32).astype(both.dtype)
     lanes = 128
     send = jnp.concatenate(
         [send.reshape(owners, capacity * features // lanes, lanes), meta.reshape(owners, features // lanes, lanes)],
@@ -197,7 +190,11 @@
     give = jnp.where(is_first, pieces[:, :, 1, :], pieces[:, :, 0, :])
     pair_sum = (keep.astype(jnp.float32) + _swap_pair(give).astype(jnp.float32)).astype(jnp.bfloat16)
     returned = _exchange(pair_sum.reshape(owners, capacity * groups * block // lanes, lanes), 1)
-    picked = returned.reshape(slots_all, groups * block)[target].astype(jnp.float32) * share_flat[:, None]
+    picked = jnp.dot(
+        hit.T.astype(returned.dtype),
+        returned.reshape(slots_all, groups * block),
+        preferred_element_type=jnp.float32,
+    ) * share_flat[:, None]
     token_terms = jnp.sum(picked.reshape(tok_rows, top_count, groups, block), axis=1)
     spread = lax.all_to_all(
         jnp.transpose(token_terms, (1, 0, 2)), "zh", split_axis=0, concat_axis=0, tiled=True

time: 238 us -> 220 us (0.924)
  local copies, waits for them, and re-layouts: 58.4 us -> 35 us
  matrix products: 12.4 us -> 16.3 us
    gather x6 -> x0, local copies, waits for them, and re-layouts: 23.3 us -> none  [the longest x2 7.96 us: body(): both[source_tok]]
    reshape x2 -> x4, local copies, waits for them, and re-layouts: 2.47 us -> 7.83 us  [the longest x1 3.16 us: body(): send.reshape(owners, capacity * features // lanes, lanes)]
    dot_general x0 -> x2, matrix products: none -> 3.19 us  [the longest x1 2.36 us: body(): jnp.dot(hit.T.astype(returned.dtype), returned.reshape(slots_all, groups...]
    scatter x1 -> x0, local copies, waits for them, and re-layouts: 2.45 us -> none  [body(): source = jnp.full((slots_all,), assigned, jnp.int32).at[target].set(jnp.a...]
where the time goes in v4:
time: 220 us; the launch traced here: 217 us
  Pallas kernels  114 us (52%)
  local copies, waits for them, and re-layouts  35 us (16%)
  other arithmetic  24.6 us (11%)
  matrix products  16.3 us (7%)
  starting transfers between devices  13.6 us (6%)
  waiting for transfers between devices  13 us (6%)
    pallas_call x2, Pallas kernels, _exchange(): pl.pallas_call(functools.partial(_exchange_kernel, n), out_shape=jax.Shap...  114 us
    all_to_all x1, starting transfers between devices, body(): lax.all_to_all(jnp.transpose(token_terms, (1, 0, 2)), 'zh', split_axis=0,...  9.31 us
    all_to_all x1, waiting for transfers between devices, body(): lax.all_to_all(jnp.transpose(token_terms, (1, 0, 2)), 'zh', split_axis=0,...  7.95 us
    slice x1, local copies, waits for them, and re-layouts, body(): keep = jnp.where(is_first, pieces[:, :, 0, :], pieces[:, :, 1, :])  6.89 us
    ppermute x2, waiting for transfers between devices, _swap_pair(): return lax.ppermute(x, 'core', [(0, 1), (1, 0)])  5.08 us
  transfers between devices with their start and end apart: 3, of which 2 were waited for; matrix products, arithmetic and copies ran while one was open for 6% of the time, Pallas kernels for 0%

profile of v4, /device:TPU:6, one launch (start us, length us, event | category | flops | bytes accessed | tf_op | source)
XLA Modules:
  0.0 217.1 jit_solution(1398371454250151007)
XLA Ops:
  0.7 0.9 copy.55
  1.8 1.2 reduce-window.6
  3.6 0.7 fusion.24
  4.3 1.3 fusion.31
  5.6 0.6 fusion.32
  6.3 0.7 reduce_sum.114
  7.0 0.7 broadcast_divide_fusion
  8.2 0.7 multiply_add_fusion
  9.0 0.2 select_reduce_fusion.1
  9.7 1.4 fusion.25
  11.5 0.8 convolution_convert_fusion.1
  12.3 3.2 %reshape.169 = bf16[64,160,128]{2,1,0:T(8,128)(2,1)} reshape(bf16[640,2048]{1,0:T(8,128)(2,1)S(1)} %convolution_convert_fusion.1) | data formatting | bytes 5242880 | tf_op jit(solution)/shard_map/reshape | solution.py:154
  15.5 3.5 %pad_maximum_fusion.x_ref = bf16[64,176,128]{2,1,0:T(8,128)(2,1)} fusion(bf16[64,16,128]{2,1,0:T(8,128)(2,1)S(1)} %bitcast.64, bf16[64,160,128]{2,1,0:T(8,128)(2,1)} %reshape.169), kind=kLoop, calls=%fused_computation.3 | loop fusion | flops 5767168 | bytes 5767168 | tf_op jit(solution)/shard_map/concatenate | solution.py:153
  19.0 73.5 %shard_map.120 = bf16[64,176,128]{2,1,0:T(8,128)(2,1)} custom-call(bf16[64,176,128]{2,1,0:T(8,128)(2,1)} %pad_maximum_fusion.x_ref), custom_call_target="tpu_custom_call" | custom-call | tf_op jit(solution)/shard_map/pallas_call | solution.py:67
  92.5 1.7 slice-done
  94.3 3.1 %reshape.171 = bf16[640,2048]{1,0:T(8,128)(2,1)} reshape(bf16[64,160,128]{2,1,0:T(8,128)(2,1)S(1)} %slice-done) | data formatting | bytes 5242880 | tf_op jit(solution)/shard_map/reshape | solution.py:158
  97.3 1.9 collective-permute-start
  99.3 5.1 %collective-permute-done = bf16[640,2048]{1,0:T(8,128)(2,1)S(1)} collective-permute-done((bf16[640,2048]{1,0:T(8,128)(2,1)}, bf16[640,2048]{1,0:T(8,128)(2,1)S(1)}, u32[]{:S(2)}, u32[]{:S(2)}) %collective-permute-start) | collective-permute-done | bytes 2621472 | tf_op jit(solution)/shard_map/ppermute | solution.py:82
  104.3 2.1 broadcast_select_fusion.1
  106.4 1.3 fusion.33
  107.8 1.3 fusion.34
  109.2 0.8 convolution_bitcast_fusion.2
  110.2 0.4 copy-done.14
  110.6 1.6 multiply_convert_fusion.3
  112.2 0.7 copy-done.9
  112.8 0.8 convolution_convert_fusion
  113.7 3.6 %reshape.172 = bf16[640,4,2,256]{3,2,1,0:T(2,128)(2,1)} reshape(bf16[640,2048]{1,0:T(8,128)(2,1)S(1)} %convolution_convert_fusion) | data formatting | bytes 5242880 | tf_op jit(solution)/shard_map/reshape | solution.py:188
  117.3 6.9 %fusion.35 = (bf16[640,4,1,256]{3,2,1,0:T(2,128)(2,1)S(1)}, bf16[640,4,1,256]{3,2,1,0:T(2,128)(2,1)S(1)}) fusion(bf16[640,4,2,256]{3,2,1,0:T(2,128)(2,1)} %reshape.172), kind=kLoop, calls=%fused_computation.94 | loop fusion | bytes 5242880 | tf_op jit(solution)/shard_map/slice | solution.py:189
  124.2 2.1 select_bitcast_fusion
  126.4 2.3 %collective-permute-start.1 = (bf16[640,4,256]{2,1,0:T(4,128)(2,1)}, bf16[640,4,256]{2,1,0:T(4,128)(2,1)}, u32[]{:S(2)}, u32[]{:S(2)}) collective-permute-start(bf16[640,4,256]{2,1,0:T(4,128)(2,1)} %select_bitcast_fusion), channel_id=1, source_target_pairs={{0,1},{1,0},{2,3},{3,2},{4,5},{5,4},{6,7},{7,6},{8,9},{9,8},{10,11... | collective-permute-start | bytes 3932168 | tf_op jit(solution)/shard_map/ppermute | solution.py:82
  129.0 0.8 copy-done.8
  129.9 1.5 slice_reduce_fusion.2
  131.4 1.7 fusion.14
  133.2 3.5 %convolution_bitcast_fusion = f32[128,640]{0,1:T(8,128)} fusion(bf16[1,128,2048]{2,1,0:T(8,128)(2,1)S(1)} %copy-done, bf16[640,1024]{1,0:T(8,128)(2,1)} %get-tuple-element.16, bf16[640,1024]{1,0:T(8,128)(2,1)} %get-tuple-element.14, f32[640]{0:T(1024)S(1)} %fusion.14), kind=kOutput, calls=%fused_computation.21 | convolution fusion | flops 343408640 | bytes 3475968 | tf_op jit(solution)/shard_map/dot_general | solution.py:205
  136.7 3.7 %fusion = bf16[640,4,256]{2,1,0:T(4,128)(2,1)} fusion(bf16[640,4,256]{2,1,0:T(4,128)(2,1)} %collective-permute-done.1, pred[]{:T(512)S(6)} %eq.69, bf16[640,4,1,256]{3,2,1,0:T(2,128)(2,1)S(1)} %copy-done.2, bf16[640,4,1,256]{3,2,1,0:T(2,128)(2,1)S(1)} %get-tuple-element.18), kind=kLoop, calls=%fused_computation.6 | loop fusion | flops 3276800 | bytes 5242881 | tf_op jit(solution)/shard_map/convert_element_type | solution.py:191
  140.4 3.5 %reshape.173.x_ref = bf16[64,80,128]{2,1,0:T(8,128)(2,1)} reshape(bf16[640,4,256]{2,1,0:T(4,128)(2,1)} %fusion) | data formatting | bytes 2621440 | tf_op jit(solution)/shard_map/reshape | solution.py:192
  143.9 40.1 %shard_map.121 = bf16[64,80,128]{2,1,0:T(8,128)(2,1)} custom-call(bf16[64,80,128]{2,1,0:T(8,128)(2,1)} %reshape.173.x_ref), custom_call_target="tpu_custom_call" | custom-call | tf_op jit(solution)/shard_map/pallas_call | solution.py:67
  184.0 2.4 %reshape.174 = bf16[640,1024]{1,0:T(8,128)(2,1)S(1)} reshape(bf16[64,80,128]{2,1,0:T(8,128)(2,1)} %shard_map.121) | data formatting | bytes 2621440 | tf_op jit(solution)/shard_map/reshape | solution.py:195
  186.4 2.4 %convolution_multiply_fusion = f32[512,1024]{1,0:T(8,128)} fusion(bf16[640,1024]{1,0:T(8,128)(2,1)S(1)} %reshape.174, f32[512]{0:T(512)S(1)} %broadcast_in_dim.72, s32[512]{0:T(512)S(1)} %multiply_add_fusion.1), kind=kOutput, calls=%fused_computation.15 | convolution fusion | flops 671940608 | bytes 3411968 | tf_op jit(solution)/shard_map/dot_general | solution.py:193
  188.7 2.2 %reshape.175 = f32[128,4,4,256]{3,2,1,0:T(4,128)S(1)} reshape(f32[512,1024]{1,0:T(8,128)} %convolution_multiply_fusion) | data formatting | bytes 4194304 | tf_op jit(solution)/shard_map/reshape | solution.py:198
  190.9 1.0 reduce_sum.122
  191.9 0.9 copy.63
  192.8 9.3 %all-to-all-start = ((f32[4,128,256]{2,1,0:T(8,128)}), f32[4,128,256]{2,1,0:T(8,128)S(1)}, u32[]{:S(2)}, u32[]{:S(2)}) async-start(f32[4,128,256]{2,1,0:T(8,128)} %copy.63), calls=%async_computation | async-start | bytes 1048576 | tf_op jit(solution)/shard_map/all_to_all | solution.py:199
  202.1 3.4 %fusion.3 = bf16[1,128,2048]{2,1,0:T(8,128)(2,1)} fusion(bf16[128,640]{0,1:T(8,128)(2,1)S(1)} %copy-done.10, bf16[640,1024]{1,0:T(8,128)(2,1)} %get-tuple-element.16, bf16[640,1024]{1,0:T(8,128)(2,1)} %get-tuple-element.14, f32[640]{0:T(1024)S(1)} %fusion.14), kind=kOutput, calls=%fused_computation.14 | convolution fusion | flops 343670784 | bytes 3312128 | tf_op jit(solution)/shard_map/dot_general | solution.py:204
  205.6 1.4 fusion.2
  207.0 1.5 fusion.1
  208.5 8.0 %all-to-all-done = f32[4,128,256]{2,1,0:T(8,128)S(1)} async-done(((f32[4,128,256]{2,1,0:T(8,128)}), f32[4,128,256]{2,1,0:T(8,128)S(1)}, u32[]{:S(2)}, u32[]{:S(2)}) %all-to-all-start) | async-done | bytes 524320 | tf_op jit(solution)/shard_map/all_to_all | solution.py:199
  216.5 0.7 reduce_sum.123
  (68 shorter events, 2.8 us)
Async XLA Ops:
  0.6 112.2 %copy-start = (bf16[1,128,2048]{2,1,0:T(8,128)(2,1)S(1)}, bf16[1,128,2048]{2,1,0:T(8,128)(2,1)}, u32[]{:S(2)}) copy-start(bf16[1,128,2048]{2,1,0:T(8,128)(2,1)} %param.17) | copy-start | bytes 1572868
  0.6 10.7 %copy-start.11 = (bf16[128,2048]{1,0:T(8,128)(2,1)S(1)}, bf16[128,2048]{1,0:T(8,128)(2,1)}, u32[]{:S(2)}) copy-start(bf16[128,2048]{1,0:T(8,128)(2,1)} %param.10) | copy-start | bytes 1572868
  0.7 10.7 %copy-start.12 = (bf16[128,2048]{1,0:T(8,128)(2,1)S(1)}, bf16[128,2048]{1,0:T(8,128)(2,1)}, u32[]{:S(2)}) copy-start(bf16[128,2048]{1,0:T(8,128)(2,1)} %param.9) | copy-start | bytes 1572868
  92.5 1.7 slice-start
  97.3 7.0 %collective-permute-start = (bf16[640,2048]{1,0:T(8,128)(2,1)}, bf16[640,2048]{1,0:T(8,128)(2,1)S(1)}, u32[]{:S(2)}, u32[]{:S(2)}) collective-permute-start(bf16[640,2048]{1,0:T(8,128)(2,1)} %reshape.171), channel_id=1, source_target_pairs={{0,1},{1,0},{2,3},{3,2},{4,5},{5,4},{6,7},{7,6},{8,9},{9,8},{10,11... | collective-permute-start | bytes 7864328 | tf_op jit(solution)/shard_map/ppermute | solution.py:82
  107.8 2.3 %copy-start.4 = (bf16[640,1024]{1,0:T(8,128)(2,1)}, bf16[640,1024]{1,0:T(8,128)(2,1)S(1)}, u32[]{:S(2)}) copy-start(bf16[640,1024]{1,0:T(8,128)(2,1)S(1)} %get-tuple-element.15) | copy-start | bytes 3932164
  107.8 1.4 copy-start.13
  109.1 1.1 copy-start.6
  109.2 1.4 copy-start.14
  110.6 1.6 copy-start.15
  112.2 0.7 copy-start.9
  124.2 2.2 copy-start.1
  124.2 4.5 %copy-start.3 = (bf16[64,176,128]{2,1,0:T(8,128)(2,1)S(1)}, bf16[64,176,128]{2,1,0:T(8,128)(2,1)}, u32[]{:S(2)}) copy-start(bf16[64,176,128]{2,1,0:T(8,128)(2,1)} %shard_map.120) | copy-start | bytes 8650756
  126.4 10.3 %collective-permute-start.1 = (bf16[640,4,256]{2,1,0:T(4,128)(2,1)}, bf16[640,4,256]{2,1,0:T(4,128)(2,1)}, u32[]{:S(2)}, u32[]{:S(2)}) collective-permute-start(bf16[640,4,256]{2,1,0:T(4,128)(2,1)} %select_bitcast_fusion), channel_id=1, source_target_pairs={{0,1},{1,0},{2,3},{3,2},{4,5},{5,4},{6,7},{7,6},{8,9},{9,8},{10,11... | collective-permute-start | bytes 3932168 | tf_op jit(solution)/shard_map/ppermute | solution.py:82
  128.9 0.8 copy-start.8
  133.2 3.5 %copy-start.2 = (bf16[640,4,1,256]{3,2,1,0:T(2,128)(2,1)S(1)}, bf16[640,4,1,256]{3,2,1,0:T(2,128)(2,1)}, u32[]{:S(2)}) copy-start(bf16[640,4,1,256]{3,2,1,0:T(2,128)(2,1)} %copy-done.1) | copy-start | bytes 3932164
  190.9 11.2 %copy-start.10 = (bf16[128,640]{0,1:T(8,128)(2,1)S(1)}, bf16[128,640]{0,1:T(8,128)(2,1)}, u32[]{:S(2)}) copy-start(bf16[128,640]{0,1:T(8,128)(2,1)} %copy-done.9) | copy-start | bytes 491524
  192.8 23.7 %all-to-all-start = ((f32[4,128,256]{2,1,0:T(8,128)}), f32[4,128,256]{2,1,0:T(8,128)S(1)}, u32[]{:S(2)}, u32[]{:S(2)}) async-start(f32[4,128,256]{2,1,0:T(8,128)} %copy.63), calls=%async_computation | async-start | bytes 1048576 | tf_op jit(solution)/shard_map/all_to_all | solution.py:199
  202.1 3.4 %copy-start.5 = (bf16[640,1024]{1,0:T(8,128)(2,1)S(1)}, bf16[640,1024]{1,0:T(8,128)(2,1)}, u32[]{:S(2)}) copy-start(bf16[640,1024]{1,0:T(8,128)(2,1)} %copy-done.4) | copy-start | bytes 3932164
  202.1 3.4 %copy-start.7 = (bf16[640,1024]{1,0:T(8,128)(2,1)S(1)}, bf16[640,1024]{1,0:T(8,128)(2,1)}, u32[]{:S(2)}) copy-start(bf16[640,1024]{1,0:T(8,128)(2,1)} %copy-done.6) | copy-start | bytes 3932164
  202.1 3.4 %copy-start.16 = (f32[128,640]{0,1:T(8,128)S(1)}, f32[128,640]{0,1:T(8,128)}, u32[]{:S(2)}) copy-start(f32[128,640]{0,1:T(8,128)} %copy-done.15) | copy-start | bytes 983044
  202.1 3.4 %copy-start.18 = (f32[128,640]{0,1:T(8,128)S(1)}, f32[128,640]{0,1:T(8,128)}, u32[]{:S(2)}) copy-start(f32[128,640]{0,1:T(8,128)} %convolution_bitcast_fusion) | copy-start | bytes 983044
  205.6 1.5 copy-start.17

commit v5 on v4

--- a/solution.py
+++ b/solution.py
@@ -13,8 +13,8 @@
 MESH = pl.DeviceIdType.MESH
 
 
-def _exchange_kernel(n, x_ref, y_ref, send_sem, recv_sem, own_sem):
-    me = lax.axis_index("dp")
+def _exchange_kernel(n, axis, x_ref, y_ref, send_sem, recv_sem, own_sem):
+    me = lax.axis_index(axis)
 
     def copy_to(peer):
         return pltpu.make_async_remote_copy(
@@ -22,7 +22,7 @@
             dst_ref=y_ref.at[me],
             send_sem=send_sem.at[peer],
             recv_sem=recv_sem.at[me],
-            device_id={"dp": peer},
+            device_id={axis: peer},
             device_id_type=MESH,
         )
 
@@ -32,14 +32,14 @@
             dst_ref=y_ref.at[source],
             send_sem=send_sem.at[source],
             recv_sem=recv_sem.at[source],
-            device_id={"dp": source},
+            device_id={axis: source},
             device_id_type=MESH,
         )
 
     barrier = pltpu.get_barrier_semaphore()
 
     def greet(i, carry):
-        pl.semaphore_signal(barrier, inc=1, device_id={"dp": lax.rem(me + i, n)}, device_id_type=MESH)
+        pl.semaphore_signal(barrier, inc=1, device_id={axis: lax.rem(me + i, n)}, device_id_type=MESH)
         return carry
 
     lax.fori_loop(1, n, greet, 0)
@@ -62,10 +62,10 @@
     own.wait()
 
 
-def _exchange(x, collective_id):
+def _exchange(x, collective_id, axis="dp"):
     n = x.shape[0]
     return pl.pallas_call(
-        functools.partial(_exchange_kernel, n),
+        functools.partial(_exchange_kernel, n, axis),
         out_shape=jax.ShapeDtypeStruct(x.shape, x.dtype),
         in_specs=[pl.BlockSpec(memory_space=pl.ANY)],
         out_specs=pl.BlockSpec(memory_space=pl.ANY),
@@ -189,17 +189,15 @@
     keep = jnp.where(is_first, pieces[:, :, 0, :], pieces[:, :, 1, :])
     give = jnp.where(is_first, pieces[:, :, 1, :], pieces[:, :, 0, :])
     pair_sum = (keep.astype(jnp.float32) + _swap_pair(give).astype(jnp.float32)).astype(jnp.bfloat16)
-    returned = _exchange(pair_sum.reshape(owners, capacity * groups * block // lanes, lanes), 1)
+    by_group = _exchange(jnp.transpose(pair_sum, (1, 0, 2)), 2, axis="zh")
+    slice_sum = jnp.sum(by_group.astype(jnp.float32), axis=0).astype(jnp.bfloat16)
+    returned = _exchange(slice_sum.reshape(owners, capacity * block // lanes, lanes), 1)
     picked = jnp.dot(
         hit.T.astype(returned.dtype),
-        returned.reshape(slots_all, groups * block),
+        returned.reshape(slots_all, block),
         preferred_element_type=jnp.float32,
     ) * share_flat[:, None]
-    token_terms = jnp.sum(picked.reshape(tok_rows, top_count, groups, block), axis=1)
-    spread = lax.all_to_all(
-        jnp.transpose(token_terms, (1, 0, 2)), "zh", split_axis=0, concat_axis=0, tiled=True
-    )
-    mixed_out = jnp.sum(spread, axis=0).astype(jnp.bfloat16)
+    mixed_out = jnp.sum(picked.reshape(tok_rows, top_count, block), axis=1).astype(jnp.bfloat16)
 
     grad_down = jnp.dot(hidden, routed, preferred_element_type=jnp.float32)
     dhidden = lax.dot_general(

time: 220 us -> 209 us (0.950)
  Pallas kernels: 114 us -> 134 us
  waiting for transfers between devices: 13 us -> 3.12 us
  starting transfers between devices: 13.6 us -> 4.12 us
  local copies, waits for them, and re-layouts: 35 us -> 27.4 us
  matrix products: 16.3 us -> 13.4 us
    pallas_call x2 -> x3, Pallas kernels: 114 us -> 134 us  [_exchange(): pl.pallas_call(functools.partial(_exchange_kernel, n, axis), out_shape=ja...]
    reshape x4 -> x3, local copies, waits for them, and re-layouts: 11.7 us -> 2.19 us  [the longest x1 1.15 us: body(): returned.reshape(slots_all, block)]
    all_to_all x1 -> x0, starting transfers between devices: 9.31 us -> none  [body(): lax.all_to_all(jnp.transpose(token_terms, (1, 0, 2)), 'zh', split_axis=0,...]
    all_to_all x1 -> x0, waiting for transfers between devices: 7.95 us -> none  [body(): lax.all_to_all(jnp.transpose(token_terms, (1, 0, 2)), 'zh', split_axis=0,...]
    slice x1, local copies, waits for them, and re-layouts: 6.89 us -> 1.73 us  [body(): keep = jnp.where(is_first, pieces[:, :, 0, :], pieces[:, :, 1, :])]
    unnamed x41 -> x35, local copies, waits for them, and re-layouts: 3.24 us -> 7.25 us
    convert_element_type x1 -> x0, other arithmetic: 3.74 us -> none  [body(): (keep.astype(jnp.float32) + _swap_pair(give).astype(jnp.float32)).astype(...]
    convert_element_type x0 -> x1, local copies, waits for them, and re-layouts: none -> 3.13 us  [body(): partial_out = lax.dot_general(hidden, down_weight[0], contract_first, pre...]
  transfers between devices with their start and end apart: 3 -> 2, of which waited for: 2 -> 1; matrix products, arithmetic and copies ran while one was open for 6% -> 7% of each run, Pallas kernels for 0% -> 0%
where the time goes in v5:
time: 209 us; the launch traced here: 207 us
  Pallas kernels  134 us (64%)
  local copies, waits for them, and re-layouts  27.4 us (13%)
  other arithmetic  24.8 us (12%)
  matrix products  13.4 us (6%)
  starting transfers between devices  4.12 us (2%)
  waiting for transfers between devices  3.12 us (1%)
    pallas_call x3, Pallas kernels, _exchange(): pl.pallas_call(functools.partial(_exchange_kernel, n, axis), out_shape=ja...  134 us
    unnamed x35, local copies, waits for them, and re-layouts  7.25 us
  transfers between devices with their start and end apart: 2, of which 1 were waited for; matrix products, arithmetic and copies ran while one was open for 7% of the time, Pallas kernels for 0%

profile of v5, /device:TPU:6, one launch (start us, length us, event | category | flops | bytes accessed | tf_op | source)
XLA Modules:
  0.0 207.5 jit_solution(13158466506448299553)
XLA Ops:
  0.7 0.9 copy.35
  1.8 1.2 reduce-window.6
  3.6 0.7 fusion.27
  4.3 1.3 fusion.34
  5.6 0.6 fusion.35
  6.3 0.7 reduce_sum.117
  7.0 0.7 broadcast_divide_fusion
  8.2 0.7 multiply_add_fusion
  9.7 1.4 fusion.28
  11.5 0.8 convolution_convert_fusion.1
  12.3 3.2 %reshape.169 = bf16[64,160,128]{2,1,0:T(8,128)(2,1)} reshape(bf16[640,2048]{1,0:T(8,128)(2,1)S(1)} %convolution_convert_fusion.1) | data formatting | bytes 5242880 | tf_op jit(solution)/shard_map/reshape | solution.py:154
  15.5 3.5 %pad_maximum_fusion.x_ref = bf16[64,176,128]{2,1,0:T(8,128)(2,1)} fusion(bf16[64,16,128]{2,1,0:T(8,128)(2,1)S(1)} %bitcast.66, bf16[64,160,128]{2,1,0:T(8,128)(2,1)} %reshape.169), kind=kLoop, calls=%fused_computation.3 | loop fusion | flops 5767168 | bytes 5767168 | tf_op jit(solution)/shard_map/concatenate | solution.py:153
  19.0 73.5 %shard_map.120 = bf16[64,176,128]{2,1,0:T(8,128)(2,1)} custom-call(bf16[64,176,128]{2,1,0:T(8,128)(2,1)} %pad_maximum_fusion.x_ref), custom_call_target="tpu_custom_call" | custom-call | tf_op jit(solution)/shard_map/pallas_call | solution.py:67
  92.5 1.7 slice-done
  94.3 3.1 %reshape.171 = bf16[640,2048]{1,0:T(8,128)(2,1)} reshape(bf16[64,160,128]{2,1,0:T(8,128)(2,1)S(1)} %slice-done) | data formatting | bytes 5242880 | tf_op jit(solution)/shard_map/reshape | solution.py:158
  97.3 1.9 collective-permute-start
  99.3 1.0 slice_convert_fusion
  100.3 1.0 copy.51
  101.2 3.1 %collective-permute-done = bf16[640,2048]{1,0:T(8,128)(2,1)S(1)} collective-permute-done((bf16[640,2048]{1,0:T(8,128)(2,1)}, bf16[640,2048]{1,0:T(8,128)(2,1)S(1)}, u32[]{:S(2)}, u32[]{:S(2)}) %collective-permute-start) | collective-permute-done | bytes 2621472 | tf_op jit(solution)/shard_map/ppermute | solution.py:82
  104.3 2.1 %broadcast_select_fusion.1 = (bf16[640,2048]{1,0:T(8,128)(2,1)S(1)}, bf16[640,2048]{1,0:T(8,128)(2,1)S(1)}) fusion(bf16[640,2048]{1,0:T(8,128)(2,1)} %reshape.171, bf16[640,2048]{1,0:T(8,128)(2,1)S(1)} %collective-permute-done, pred[]{:T(512)S(6)} %eq.69), kind=kLoop, calls=%fused_computation.8 | loop fusion | flops 2621440 | bytes 10485761 | tf_op jit(solution)/shard_map/jit(_where)/select_n | solution.py:161
  106.4 1.3 fusion.36
  107.8 1.3 fusion.37
  109.2 0.8 convolution_bitcast_fusion.2
  110.2 0.4 copy-done.11
  110.6 1.6 multiply_convert_fusion.3
  112.2 0.7 copy-done.7
  112.8 2.3 %convolution_convert_fusion = bf16[640,2048]{1,0:T(8,128)(2,1)} fusion(bf16[128,640]{0,1:T(8,128)(2,1)S(1)} %get-tuple-element.23, bf16[1,128,2048]{2,1,0:T(8,128)(2,1)S(1)} %copy-done), kind=kOutput, calls=%fused_computation.1 | convolution fusion | flops 336855040 | bytes 3309568 | tf_op jit(solution)/shard_map/dot_general | solution.py:185
  115.2 3.1 %copy.41 = bf16[640,2048]{0,1:T(8,128)(2,1)S(1)} copy(bf16[640,2048]{1,0:T(8,128)(2,1)} %convolution_convert_fusion) | data formatting | bytes 5242880 | tf_op jit(solution)/shard_map/convert_element_type | solution.py:187
  118.3 1.7 fusion.38
  120.0 1.6 copy.44
  121.6 1.6 copy.45
  123.2 1.2 select_bitcast_fusion
  124.5 2.2 %collective-permute-start.1 = (bf16[640,4,256]{2,0,1:T(8,128)(2,1)}, bf16[640,4,256]{2,0,1:T(8,128)(2,1)}, u32[]{:S(2)}, u32[]{:S(2)}) collective-permute-start(bf16[640,4,256]{2,0,1:T(8,128)(2,1)} %select_bitcast_fusion), channel_id=1, source_target_pairs={{0,1},{1,0},{2,3},{3,2},{4,5},{5,4},{6,7},{7,6},{8,9},{9,8},{10,11... | collective-permute-start | bytes 3932168 | tf_op jit(solution)/shard_map/ppermute | solution.py:82
  126.7 1.6 slice_reduce_fusion.2
  128.2 0.8 slice.79
  129.1 1.8 fusion.17
  131.0 3.5 %fusion.3 = bf16[1,128,2048]{2,1,0:T(8,128)(2,1)} fusion(bf16[128,640]{0,1:T(8,128)(2,1)} %copy-done.7, bf16[640,1024]{1,0:T(8,128)(2,1)} %get-tuple-element.16, bf16[640,1024]{1,0:T(8,128)(2,1)} %get-tuple-element.14, f32[640]{0:T(1024)S(1)} %fusion.17), kind=kOutput, calls=%fused_computation.14 | convolution fusion | flops 343670784 | bytes 3312128 | tf_op jit(solution)/shard_map/dot_general | solution.py:202
  134.5 0.9 convolution_bitcast_fusion
  136.2 1.4 fusion.2
  137.7 1.5 fusion.1
  139.2 2.9 %fusion.4.x_ref = bf16[4,640,256]{2,1,0:T(8,128)(2,1)} fusion(bf16[640,4,256]{2,0,1:T(8,128)(2,1)} %collective-permute-done.1, bf16[640,4,1,256]{3,0,1,2:T(8,128)(2,1)S(1)} %copy.44, bf16[640,4,1,256]{3,0,1,2:T(8,128)(2,1)S(1)} %copy.45, pred[]{:T(512)S(6)} %eq.69), kind=kLoop, calls=%fused_computation.15 | loop fusion | flops 3276800 | bytes 5242881 | tf_op jit(solution)/shard_map/transpose | solution.py:192
  142.0 30.8 %shard_map.121 = bf16[4,640,256]{2,1,0:T(8,128)(2,1)} custom-call(bf16[4,640,256]{2,1,0:T(8,128)(2,1)} %fusion.4.x_ref), custom_call_target="tpu_custom_call" | custom-call | tf_op jit(solution)/shard_map/pallas_call | solution.py:67
  172.9 1.6 reduce_sum.125
  174.5 0.9 reshape.173.x_ref
  175.4 29.3 %shard_map.122 = bf16[64,20,128]{2,1,0:T(8,128)(2,1)} custom-call(bf16[64,20,128]{2,1,0:T(8,128)(2,1)} %reshape.173.x_ref), custom_call_target="tpu_custom_call" | custom-call | tf_op jit(solution)/shard_map/pallas_call | solution.py:67
  204.7 1.2 reshape.174
  205.8 0.5 fusion.7
  206.5 0.9 reduce_sum.126
  (60 shorter events, 3.8 us)
Async XLA Ops:
  0.6 112.2 %copy-start = (bf16[1,128,2048]{2,1,0:T(8,128)(2,1)S(1)}, bf16[1,128,2048]{2,1,0:T(8,128)(2,1)}, u32[]{:S(2)}) copy-start(bf16[1,128,2048]{2,1,0:T(8,128)(2,1)} %param.17) | copy-start | bytes 1572868
  0.6 10.7 %copy-start.8 = (bf16[128,2048]{1,0:T(8,128)(2,1)S(1)}, bf16[128,2048]{1,0:T(8,128)(2,1)}, u32[]{:S(2)}) copy-start(bf16[128,2048]{1,0:T(8,128)(2,1)} %param.10) | copy-start | bytes 1572868
  0.7 10.7 %copy-start.9 = (bf16[128,2048]{1,0:T(8,128)(2,1)S(1)}, bf16[128,2048]{1,0:T(8,128)(2,1)}, u32[]{:S(2)}) copy-start(bf16[128,2048]{1,0:T(8,128)(2,1)} %param.9) | copy-start | bytes 1572868
  92.5 1.7 slice-start
  97.3 7.0 %collective-permute-start = (bf16[640,2048]{1,0:T(8,128)(2,1)}, bf16[640,2048]{1,0:T(8,128)(2,1)S(1)}, u32[]{:S(2)}, u32[]{:S(2)}) collective-permute-start(bf16[640,2048]{1,0:T(8,128)(2,1)} %reshape.171), channel_id=1, source_target_pairs={{0,1},{1,0},{2,3},{3,2},{4,5},{5,4},{6,7},{7,6},{8,9},{9,8},{10,11... | collective-permute-start | bytes 7864328 | tf_op jit(solution)/shard_map/ppermute | solution.py:82
  107.8 2.3 %copy-start.1 = (bf16[640,1024]{1,0:T(8,128)(2,1)}, bf16[640,1024]{1,0:T(8,128)(2,1)S(1)}, u32[]{:S(2)}) copy-start(bf16[640,1024]{1,0:T(8,128)(2,1)S(1)} %get-tuple-element.15) | copy-start | bytes 3932164
  107.8 1.4 copy-start.10
  109.1 1.1 copy-start.3
  109.2 1.4 copy-start.11
  110.6 1.6 copy-start.12
  112.2 0.7 copy-start.7
  124.5 14.7 %collective-permute-start.1 = (bf16[640,4,256]{2,0,1:T(8,128)(2,1)}, bf16[640,4,256]{2,0,1:T(8,128)(2,1)}, u32[]{:S(2)}, u32[]{:S(2)}) collective-permute-start(bf16[640,4,256]{2,0,1:T(8,128)(2,1)} %select_bitcast_fusion), channel_id=1, source_target_pairs={{0,1},{1,0},{2,3},{3,2},{4,5},{5,4},{6,7},{7,6},{8,9},{9,8},{10,11... | collective-permute-start | bytes 3932168 | tf_op jit(solution)/shard_map/ppermute | solution.py:82
  130.9 3.5 %copy-start.5 = (bf16[640,1024]{1,0:T(8,128)(2,1)S(1)}, bf16[640,1024]{1,0:T(8,128)(2,1)}, u32[]{:S(2)}) copy-start(bf16[640,1024]{1,0:T(8,128)(2,1)} %get-tuple-element.14) | copy-start | bytes 3932164
  131.0 3.5 %copy-start.6 = (bf16[640,1024]{1,0:T(8,128)(2,1)S(1)}, bf16[640,1024]{1,0:T(8,128)(2,1)}, u32[]{:S(2)}) copy-start(bf16[640,1024]{1,0:T(8,128)(2,1)} %get-tuple-element.16) | copy-start | bytes 3932164
  134.4 1.3 copy-start.2
  134.5 1.7 copy-start.4
  134.5 1.7 copy-start.13
  136.2 1.4 copy-start.14

commit v6 on v5

--- a/solution.py
+++ b/solution.py
@@ -189,15 +189,15 @@
     keep = jnp.where(is_first, pieces[:, :, 0, :], pieces[:, :, 1, :])
     give = jnp.where(is_first, pieces[:, :, 1, :], pieces[:, :, 0, :])
     pair_sum = (keep.astype(jnp.float32) + _swap_pair(give).astype(jnp.float32)).astype(jnp.bfloat16)
-    by_group = _exchange(jnp.transpose(pair_sum, (1, 0, 2)), 2, axis="zh")
-    slice_sum = jnp.sum(by_group.astype(jnp.float32), axis=0).astype(jnp.bfloat16)
-    returned = _exchange(slice_sum.reshape(owners, capacity * block // lanes, lanes), 1)
+    returned = _exchange(pair_sum.reshape(owners, capacity * groups * block // lanes, lanes), 1)
     picked = jnp.dot(
         hit.T.astype(returned.dtype),
-        returned.reshape(slots_all, block),
+        returned.reshape(slots_all, groups * block),
         preferred_element_type=jnp.float32,
     ) * share_flat[:, None]
-    mixed_out = jnp.sum(picked.reshape(tok_rows, top_count, block), axis=1).astype(jnp.bfloat16)
+    token_terms = jnp.sum(picked.reshape(tok_rows, top_count, groups, block), axis=1)
+    by_group = _exchange(jnp.transpose(token_terms, (1, 0, 2)), 2, axis="zh")
+    mixed_out = jnp.sum(by_group, axis=0).astype(jnp.bfloat16)
 
     grad_down = jnp.dot(hidden, routed, preferred_element_type=jnp.float32)
     dhidden = lax.dot_general(

time: 209 us -> 224 us (1.072)
  the two profiles are of different devices: /device:TPU:6 before, /device:TPU:16 now
where the time goes in v6:
time: 224 us; the launch traced here: 223 us
  Pallas kernels  138 us (62%)
  local copies, waits for them, and re-layouts  36.6 us (16%)
  other arithmetic  26.5 us (12%)
  matrix products  13.8 us (6%)
  starting transfers between devices  4.13 us (2%)
  waiting for transfers between devices  3.12 us (1%)
    pallas_call x3, Pallas kernels, _exchange(): pl.pallas_call(functools.partial(_exchange_kernel, n, axis), out_shape=ja...  138 us
    slice x1, local copies, waits for them, and re-layouts, body(): keep = jnp.where(is_first, pieces[:, :, 0, :], pieces[:, :, 1, :])  6.64 us
  transfers between devices with their start and end apart: 2, of which 1 were waited for; matrix products, arithmetic and copies ran while one was open for 6% of the time, Pallas kernels for 0%

profile of v6, /device:TPU:16, one launch (start us, length us, event | category | flops | bytes accessed | tf_op | source)
XLA Modules:
  0.0 222.9 jit_solution(7582248003869455017)
XLA Ops:
  0.7 0.9 copy.46
  1.8 1.2 reduce-window.6
  3.6 0.7 fusion.24
  4.3 1.3 fusion.31
  5.6 0.6 fusion.32
  6.3 0.7 reduce_sum.114
  7.0 0.7 broadcast_divide_fusion
  8.2 0.7 multiply_add_fusion
  9.7 1.4 fusion.25
  11.5 0.8 convolution_convert_fusion.1
  12.3 3.2 %reshape.169 = bf16[64,160,128]{2,1,0:T(8,128)(2,1)} reshape(bf16[640,2048]{1,0:T(8,128)(2,1)S(1)} %convolution_convert_fusion.1) | data formatting | bytes 5242880 | tf_op jit(solution)/shard_map/reshape | solution.py:154
  15.5 3.5 %pad_maximum_fusion.x_ref = bf16[64,176,128]{2,1,0:T(8,128)(2,1)} fusion(bf16[64,16,128]{2,1,0:T(8,128)(2,1)S(1)} %bitcast.66, bf16[64,160,128]{2,1,0:T(8,128)(2,1)} %reshape.169), kind=kLoop, calls=%fused_computation.3 | loop fusion | flops 5767168 | bytes 5767168 | tf_op jit(solution)/shard_map/concatenate | solution.py:153
  19.0 75.3 %shard_map.120 = bf16[64,176,128]{2,1,0:T(8,128)(2,1)} custom-call(bf16[64,176,128]{2,1,0:T(8,128)(2,1)} %pad_maximum_fusion.x_ref), custom_call_target="tpu_custom_call" | custom-call | tf_op jit(solution)/shard_map/pallas_call | solution.py:67
  94.3 1.7 slice-done
  96.0 3.1 %reshape.171 = bf16[640,2048]{1,0:T(8,128)(2,1)} reshape(bf16[64,160,128]{2,1,0:T(8,128)(2,1)S(1)} %slice-done) | data formatting | bytes 5242880 | tf_op jit(solution)/shard_map/reshape | solution.py:158
  99.1 1.9 collective-permute-start
  101.0 1.0 slice_convert_fusion
  102.0 1.0 copy.67
  103.0 3.1 %collective-permute-done = bf16[640,2048]{1,0:T(8,128)(2,1)S(1)} collective-permute-done((bf16[640,2048]{1,0:T(8,128)(2,1)}, bf16[640,2048]{1,0:T(8,128)(2,1)S(1)}, u32[]{:S(2)}, u32[]{:S(2)}) %collective-permute-start) | collective-permute-done | bytes 2621472 | tf_op jit(solution)/shard_map/ppermute | solution.py:82
  106.1 2.1 broadcast_select_fusion.1
  108.2 1.3 fusion.33
  109.5 1.3 fusion.34
  110.9 0.8 convolution_bitcast_fusion.2
  111.9 0.4 copy-done.13
  112.3 1.6 multiply_convert_fusion.3
  113.9 0.7 copy-done.9
  114.6 0.8 convolution_convert_fusion
  115.4 3.6 %reshape.172 = bf16[640,4,2,256]{3,2,1,0:T(2,128)(2,1)} reshape(bf16[640,2048]{1,0:T(8,128)(2,1)S(1)} %convolution_convert_fusion) | data formatting | bytes 5242880 | tf_op jit(solution)/shard_map/reshape | solution.py:188
  119.0 6.6 %fusion.35 = (bf16[640,4,1,256]{3,2,1,0:T(2,128)(2,1)S(1)}, bf16[640,4,1,256]{3,2,1,0:T(2,128)(2,1)S(1)}) fusion(bf16[640,4,2,256]{3,2,1,0:T(2,128)(2,1)} %reshape.172), kind=kLoop, calls=%fused_computation.95 | loop fusion | bytes 5242880 | tf_op jit(solution)/shard_map/slice | solution.py:189
  125.7 2.1 select_bitcast_fusion
  127.7 2.2 collective-permute-start.1
  130.0 1.5 slice_reduce_fusion.2
  131.5 0.8 slice.79
  132.4 1.7 fusion.14
  134.2 3.5 %fusion.3 = bf16[1,128,2048]{2,1,0:T(8,128)(2,1)} fusion(bf16[128,640]{0,1:T(8,128)(2,1)} %copy-done.9, bf16[640,1024]{1,0:T(8,128)(2,1)} %get-tuple-element.16, bf16[640,1024]{1,0:T(8,128)(2,1)} %get-tuple-element.14, f32[640]{0:T(1024)S(1)} %fusion.14), kind=kOutput, calls=%fused_computation.14 | convolution fusion | flops 343670784 | bytes 3312128 | tf_op jit(solution)/shard_map/dot_general | solution.py:202
  137.7 0.9 convolution_bitcast_fusion
  139.4 1.4 fusion.2
  140.9 1.5 fusion.1
  142.7 3.7 %fusion = bf16[640,4,256]{2,1,0:T(4,128)(2,1)} fusion(bf16[640,4,256]{2,1,0:T(4,128)(2,1)} %collective-permute-done.1, pred[]{:T(512)S(6)} %eq.69, bf16[640,4,1,256]{3,2,1,0:T(2,128)(2,1)S(1)} %copy-done.2, bf16[640,4,1,256]{3,2,1,0:T(2,128)(2,1)S(1)} %get-tuple-element.18), kind=kLoop, calls=%fused_computation.6 | loop fusion | flops 3276800 | bytes 5242881 | tf_op jit(solution)/shard_map/convert_element_type | solution.py:191
  146.5 3.5 %reshape.173.x_ref = bf16[64,80,128]{2,1,0:T(8,128)(2,1)} reshape(bf16[640,4,256]{2,1,0:T(4,128)(2,1)} %fusion) | data formatting | bytes 2621440 | tf_op jit(solution)/shard_map/reshape | solution.py:192
  149.9 39.8 %shard_map.121 = bf16[64,80,128]{2,1,0:T(8,128)(2,1)} custom-call(bf16[64,80,128]{2,1,0:T(8,128)(2,1)} %reshape.173.x_ref), custom_call_target="tpu_custom_call" | custom-call | tf_op jit(solution)/shard_map/pallas_call | solution.py:67
  189.8 2.4 %reshape.174 = bf16[640,1024]{1,0:T(8,128)(2,1)S(1)} reshape(bf16[64,80,128]{2,1,0:T(8,128)(2,1)} %shard_map.121) | data formatting | bytes 2621440 | tf_op jit(solution)/shard_map/reshape | solution.py:195
  192.2 2.4 %convolution_multiply_fusion = f32[512,1024]{1,0:T(8,128)} fusion(bf16[640,1024]{1,0:T(8,128)(2,1)S(1)} %reshape.174, f32[512]{0:T(512)S(1)} %broadcast_in_dim.72, s32[512]{0:T(512)S(1)} %multiply_add_fusion.1), kind=kOutput, calls=%fused_computation.15 | convolution fusion | flops 671940608 | bytes 3411968 | tf_op jit(solution)/shard_map/dot_general | solution.py:193
  194.5 2.2 reshape.175
  196.7 1.0 reduce_sum.122
  197.7 0.9 copy.68
  198.6 22.6 %shard_map.122 = f32[4,128,256]{2,1,0:T(8,128)} custom-call(f32[4,128,256]{2,1,0:T(8,128)} %bitcast.65), custom_call_target="tpu_custom_call" | custom-call | tf_op jit(solution)/shard_map/pallas_call | solution.py:67
  221.2 1.7 reduce_sum.123
  (63 shorter events, 4.0 us)
Async XLA Ops:
  0.6 114.0 %copy-start = (bf16[1,128,2048]{2,1,0:T(8,128)(2,1)S(1)}, bf16[1,128,2048]{2,1,0:T(8,128)(2,1)}, u32[]{:S(2)}) copy-start(bf16[1,128,2048]{2,1,0:T(8,128)(2,1)} %param.17) | copy-start | bytes 1572868
  0.6 10.7 %copy-start.10 = (bf16[128,2048]{1,0:T(8,128)(2,1)S(1)}, bf16[128,2048]{1,0:T(8,128)(2,1)}, u32[]{:S(2)}) copy-start(bf16[128,2048]{1,0:T(8,128)(2,1)} %param.10) | copy-start | bytes 1572868
  0.7 10.7 %copy-start.11 = (bf16[128,2048]{1,0:T(8,128)(2,1)S(1)}, bf16[128,2048]{1,0:T(8,128)(2,1)}, u32[]{:S(2)}) copy-start(bf16[128,2048]{1,0:T(8,128)(2,1)} %param.9) | copy-start | bytes 1572868
  94.3 1.7 slice-start
  99.1 7.0 %collective-permute-start = (bf16[640,2048]{1,0:T(8,128)(2,1)}, bf16[640,2048]{1,0:T(8,128)(2,1)S(1)}, u32[]{:S(2)}, u32[]{:S(2)}) collective-permute-start(bf16[640,2048]{1,0:T(8,128)(2,1)} %reshape.171), channel_id=1, source_target_pairs={{0,1},{1,0},{2,3},{3,2},{4,5},{5,4},{6,7},{7,6},{8,9},{9,8},{10,11... | collective-permute-start | bytes 7864328 | tf_op jit(solution)/shard_map/ppermute | solution.py:82
  109.5 2.3 %copy-start.3 = (bf16[640,1024]{1,0:T(8,128)(2,1)}, bf16[640,1024]{1,0:T(8,128)(2,1)S(1)}, u32[]{:S(2)}) copy-start(bf16[640,1024]{1,0:T(8,128)(2,1)S(1)} %get-tuple-element.15) | copy-start | bytes 3932164
  109.5 1.4 copy-start.12
  110.8 1.1 copy-start.5
  110.9 1.4 copy-start.13
  112.3 1.6 copy-start.14
  113.9 0.7 copy-start.9
  125.6 2.1 copy-start.1
  127.7 14.6 %collective-permute-start.1 = (bf16[640,4,256]{2,1,0:T(4,128)(2,1)}, bf16[640,4,256]{2,1,0:T(4,128)(2,1)}, u32[]{:S(2)}, u32[]{:S(2)}) collective-permute-start(bf16[640,4,256]{2,1,0:T(4,128)(2,1)} %select_bitcast_fusion), channel_id=1, source_target_pairs={{0,1},{1,0},{2,3},{3,2},{4,5},{5,4},{6,7},{7,6},{8,9},{9,8},{10,11... | collective-permute-start | bytes 3932168 | tf_op jit(solution)/shard_map/ppermute | solution.py:82
  134.1 3.5 %copy-start.7 = (bf16[640,1024]{1,0:T(8,128)(2,1)S(1)}, bf16[640,1024]{1,0:T(8,128)(2,1)}, u32[]{:S(2)}) copy-start(bf16[640,1024]{1,0:T(8,128)(2,1)} %get-tuple-element.14) | copy-start | bytes 3932164
  134.2 3.5 %copy-start.8 = (bf16[640,1024]{1,0:T(8,128)(2,1)S(1)}, bf16[640,1024]{1,0:T(8,128)(2,1)}, u32[]{:S(2)}) copy-start(bf16[640,1024]{1,0:T(8,128)(2,1)} %get-tuple-element.16) | copy-start | bytes 3932164
  137.6 1.3 copy-start.4
  137.7 1.7 copy-start.6
  137.7 1.7 copy-start.15
  139.4 1.4 copy-start.16
  140.8 1.9 copy-start.2

commit v7 on v5

--- a/solution.py
+++ b/solution.py
@@ -189,8 +189,9 @@
     keep = jnp.where(is_first, pieces[:, :, 0, :], pieces[:, :, 1, :])
     give = jnp.where(is_first, pieces[:, :, 1, :], pieces[:, :, 0, :])
     pair_sum = (keep.astype(jnp.float32) + _swap_pair(give).astype(jnp.float32)).astype(jnp.bfloat16)
-    by_group = _exchange(jnp.transpose(pair_sum, (1, 0, 2)), 2, axis="zh")
-    slice_sum = jnp.sum(by_group.astype(jnp.float32), axis=0).astype(jnp.bfloat16)
+    slice_sum = lax.psum_scatter(
+        jnp.transpose(pair_sum, (1, 0, 2)), "zh", scatter_dimension=0, tiled=True
+    ).reshape(slots_all, block)
     returned = _exchange(slice_sum.reshape(owners, capacity * block // lanes, lanes), 1)
     picked = jnp.dot(
         hit.T.astype(returned.dtype),

time: 209 us -> 215 us (1.029)
  Pallas kernels: 134 us -> 93.5 us
  waiting for transfers between devices: 3.12 us -> 40.1 us
  between operations: 1 us -> 14.4 us
  other arithmetic: 24.8 us -> 20.9 us
    pallas_call x3 -> x2, Pallas kernels: 134 us -> 93.5 us  [_exchange(): pl.pallas_call(functools.partial(_exchange_kernel, n, axis), out_shape=ja...]
    reduce_scatter x0 -> x1, waiting for transfers between devices: none -> 32.3 us  [body(): lax.psum_scatter(jnp.transpose(pair_sum, (1, 0, 2)), 'zh', scatter_dimens...]
    ppermute x2, waiting for transfers between devices: 3.12 us -> 7.78 us  [_swap_pair(): return lax.ppermute(x, 'core', [(0, 1), (1, 0)])]
    reshape x1, local copies, waits for them, and re-layouts: 0.89 us -> 4.29 us  [body(): pieces = partial_out.reshape(slots_all, groups, 2, block)]
    unnamed x35 -> x37, local copies, waits for them, and re-layouts: 7.25 us -> 4.08 us
    convert_element_type x1 -> x0, local copies, waits for them, and re-layouts: 3.13 us -> none  [body(): partial_out = lax.dot_general(hidden, down_weight[0], contract_first, pre...]
  transfers between devices with their start and end apart: 2 -> 3, of which waited for: 1 -> 3; matrix products, arithmetic and copies ran while one was open for 7% -> 5% of each run, Pallas kernels for 0% -> 0%
where the time goes in v7:
time: 215 us; the launch traced here: 213 us
  Pallas kernels  93.5 us (43%)
  waiting for transfers between devices  40.1 us (19%)
  local copies, waits for them, and re-layouts  27.6 us (13%)
  other arithmetic  20.9 us (10%)
  between operations  14.4 us (7%)
  matrix products  12.5 us (6%)
  starting transfers between devices  4.43 us (2%)
    pallas_call x2, Pallas kernels, _exchange(): pl.pallas_call(functools.partial(_exchange_kernel, n, axis), out_shape=ja...  93.5 us
    reduce_scatter x1, waiting for transfers between devices, body(): lax.psum_scatter(jnp.transpose(pair_sum, (1, 0, 2)), 'zh', scatter_dimens...  32.3 us
    ppermute x2, waiting for transfers between devices, _swap_pair(): return lax.ppermute(x, 'core', [(0, 1), (1, 0)])  7.78 us
    ppermute x2, starting transfers between devices, _swap_pair(): return lax.ppermute(x, 'core', [(0, 1), (1, 0)])  4.39 us
  transfers between devices with their start and end apart: 3, of which 3 were waited for; matrix products, arithmetic and copies ran while one was open for 5% of the time, Pallas kernels for 0%

profile of v7, /device:TPU:6, one launch (start us, length us, event | category | flops | bytes accessed | tf_op | source)
XLA Modules:
  0.0 213.5 jit_solution(202766884566158179)
XLA Ops:
  7.2 0.9 copy.35
  8.4 1.2 reduce-window.6
  9.6 0.2 slice_reduce_fusion
  10.1 0.7 fusion.27
  10.9 1.3 fusion.34
  12.2 0.6 fusion.35
  12.8 0.7 reduce_sum.105
  13.5 0.7 broadcast_divide_fusion
  14.7 0.7 multiply_add_fusion
  15.6 0.2 select_reduce_fusion.1
  16.3 1.4 fusion.28
  18.0 0.8 convolution_convert_fusion.1
  18.9 3.2 %reshape.166 = bf16[64,160,128]{2,1,0:T(8,128)(2,1)} reshape(bf16[640,2048]{1,0:T(8,128)(2,1)S(1)} %convolution_convert_fusion.1) | data formatting | bytes 5242880 | tf_op jit(solution)/shard_map/reshape | solution.py:154
  22.0 3.5 %pad_maximum_fusion.x_ref = bf16[64,176,128]{2,1,0:T(8,128)(2,1)} fusion(bf16[64,16,128]{2,1,0:T(8,128)(2,1)S(1)} %bitcast.64, bf16[64,160,128]{2,1,0:T(8,128)(2,1)} %reshape.166), kind=kLoop, calls=%fused_computation.3 | loop fusion | flops 5767168 | bytes 5767168 | tf_op jit(solution)/shard_map/concatenate | solution.py:153
  25.6 73.5 %shard_map.120 = bf16[64,176,128]{2,1,0:T(8,128)(2,1)} custom-call(bf16[64,176,128]{2,1,0:T(8,128)(2,1)} %pad_maximum_fusion.x_ref), custom_call_target="tpu_custom_call" | custom-call | tf_op jit(solution)/shard_map/pallas_call | solution.py:67
  99.1 1.7 slice-done
  100.9 3.1 %reshape.168 = bf16[640,2048]{1,0:T(8,128)(2,1)} reshape(bf16[64,160,128]{2,1,0:T(8,128)(2,1)S(1)} %slice-done) | data formatting | bytes 5242880 | tf_op jit(solution)/shard_map/reshape | solution.py:158
  104.0 1.9 collective-permute-start
  105.9 5.1 %collective-permute-done = bf16[640,2048]{1,0:T(8,128)(2,1)S(1)} collective-permute-done((bf16[640,2048]{1,0:T(8,128)(2,1)}, bf16[640,2048]{1,0:T(8,128)(2,1)S(1)}, u32[]{:S(2)}, u32[]{:S(2)}) %collective-permute-start) | collective-permute-done | bytes 2621472 | tf_op jit(solution)/shard_map/ppermute | solution.py:82
  111.0 2.1 broadcast_select_fusion.1
  113.0 1.4 fusion.36
  114.5 1.3 fusion.37
  115.8 0.9 convolution_bitcast_fusion.2
  116.8 0.5 copy-done.13
  117.3 1.6 multiply_convert_fusion.3
  118.9 0.7 copy-done.9
  119.6 2.4 %convolution_convert_fusion = bf16[640,2048]{1,0:T(8,128)(2,1)} fusion(bf16[128,640]{0,1:T(8,128)(2,1)S(1)} %get-tuple-element.23, bf16[1,128,2048]{2,1,0:T(8,128)(2,1)S(1)} %copy-done), kind=kOutput, calls=%fused_computation.1 | convolution fusion | flops 336855040 | bytes 3309568 | tf_op jit(solution)/shard_map/dot_general | solution.py:185
  121.9 4.3 %reshape.169 = bf16[640,4,2,256]{3,2,1,0:T(2,128)(2,1)S(1)} reshape(bf16[640,2048]{1,0:T(8,128)(2,1)} %convolution_convert_fusion) | data formatting | bytes 5242880 | tf_op jit(solution)/shard_map/reshape | solution.py:188
  126.2 3.7 %fusion.38 = (bf16[640,4,1,256]{3,2,1,0:T(2,128)(2,1)S(1)}, bf16[640,4,1,256]{3,2,1,0:T(2,128)(2,1)S(1)}) fusion(bf16[640,4,2,256]{3,2,1,0:T(2,128)(2,1)S(1)} %reshape.169), kind=kLoop, calls=%fused_computation.96 | loop fusion | bytes 5242880 | tf_op jit(solution)/shard_map/slice | solution.py:189
  129.9 0.8 select_bitcast_fusion
  130.7 2.5 %collective-permute-start.1 = (bf16[640,4,256]{2,0,1:T(8,128)(2,1)S(1)}, bf16[640,4,256]{2,0,1:T(8,128)(2,1)S(1)}, u32[]{:S(2)}, u32[]{:S(2)}) collective-permute-start(bf16[640,4,256]{2,0,1:T(8,128)(2,1)S(1)} %select_bitcast_fusion), channel_id=1, source_target_pairs={{0,1},{1,0},{2,3},{3,2},{4,5},{5,4},{6,7},{7,6},{8,9},{9,8},{10,11... | collective-permute-start | bytes 3932168 | tf_op jit(solution)/shard_map/ppermute | solution.py:82
  133.2 2.7 %collective-permute-done.1 = bf16[640,4,256]{2,0,1:T(8,128)(2,1)S(1)} collective-permute-done((bf16[640,4,256]{2,0,1:T(8,128)(2,1)S(1)}, bf16[640,4,256]{2,0,1:T(8,128)(2,1)S(1)}, u32[]{:S(2)}, u32[]{:S(2)}) %collective-permute-start.1) | collective-permute-done | bytes 1310752 | tf_op jit(solution)/shard_map/ppermute | solution.py:82
  135.9 2.0 fusion.4
  138.2 0.8 copy-done.8
  139.1 1.6 slice_reduce_fusion.2
  140.7 1.8 fusion.17
  142.5 2.5 %fusion.3 = bf16[1,128,2048]{2,1,0:T(8,128)(2,1)} fusion(bf16[128,640]{0,1:T(8,128)(2,1)} %copy-done.9, bf16[640,1024]{1,0:T(8,128)(2,1)S(1)} %copy-done.7, bf16[640,1024]{1,0:T(8,128)(2,1)S(1)} %copy-done.6, f32[640]{0:T(1024)S(1)} %fusion.17), kind=kOutput, calls=%fused_computation.14 | convolution fusion | flops 343670784 | bytes 3312128 | tf_op jit(solution)/shard_map/dot_general | solution.py:203
  145.0 0.9 convolution_bitcast_fusion
  145.9 0.4 copy-done.3
  146.3 0.4 copy-done.5
  146.7 1.4 fusion.2
  148.2 1.5 fusion.1
  149.7 32.3 %reduce-scatter.2.cloned.1.call-done = bf16[1,640,256]{2,1,0:T(8,128)(2,1)} async-done(((bf16[4,640,256]{2,1,0:T(8,128)(2,1)}), bf16[1,640,256]{2,1,0:T(8,128)(2,1)}) %reduce-scatter.2.cloned.1.call-update) | async-done | bytes 327696 | tf_op jit(solution)/shard_map/reduce_scatter | solution.py:192
  182.0 1.9 reshape_reshape.3.x_ref
  183.8 20.0 %shard_map.121 = bf16[64,20,128]{2,1,0:T(8,128)(2,1)} custom-call(bf16[64,20,128]{2,1,0:T(8,128)(2,1)} %reshape_reshape.3.x_ref), custom_call_target="tpu_custom_call" | custom-call | tf_op jit(solution)/shard_map/pallas_call | solution.py:67
  203.8 1.2 reshape.170
  205.0 0.5 fusion.7
  205.7 0.9 reduce_sum.113
  (63 shorter events, 2.7 us)
Async XLA Ops:
  7.2 112.4 %copy-start = (bf16[1,128,2048]{2,1,0:T(8,128)(2,1)S(1)}, bf16[1,128,2048]{2,1,0:T(8,128)(2,1)}, u32[]{:S(2)}) copy-start(bf16[1,128,2048]{2,1,0:T(8,128)(2,1)} %param.17) | copy-start | bytes 1572868
  7.2 10.8 %copy-start.10 = (bf16[128,2048]{1,0:T(8,128)(2,1)S(1)}, bf16[128,2048]{1,0:T(8,128)(2,1)}, u32[]{:S(2)}) copy-start(bf16[128,2048]{1,0:T(8,128)(2,1)} %param.10) | copy-start | bytes 1572868
  7.2 10.8 %copy-start.11 = (bf16[128,2048]{1,0:T(8,128)(2,1)S(1)}, bf16[128,2048]{1,0:T(8,128)(2,1)}, u32[]{:S(2)}) copy-start(bf16[128,2048]{1,0:T(8,128)(2,1)} %param.9) | copy-start | bytes 1572868
  7.2 174.8 %reduce-scatter.2.cloned.1.call-start = ((), (), s32[]{:S(2)}) async-start(), calls=%async_computation.1 | async-start | bytes 1638400 | tf_op jit(solution)/shard_map/reduce_scatter | solution.py:192
  99.1 1.7 slice-start
  104.0 7.0 %collective-permute-start = (bf16[640,2048]{1,0:T(8,128)(2,1)}, bf16[640,2048]{1,0:T(8,128)(2,1)S(1)}, u32[]{:S(2)}, u32[]{:S(2)}) collective-permute-start(bf16[640,2048]{1,0:T(8,128)(2,1)} %reshape.168), channel_id=1, source_target_pairs={{0,1},{1,0},{2,3},{3,2},{4,5},{5,4},{6,7},{7,6},{8,9},{9,8},{10,11... | collective-permute-start | bytes 7864328 | tf_op jit(solution)/shard_map/ppermute | solution.py:82
  114.4 2.3 %copy-start.2 = (bf16[640,1024]{1,0:T(8,128)(2,1)}, bf16[640,1024]{1,0:T(8,128)(2,1)S(1)}, u32[]{:S(2)}) copy-start(bf16[640,1024]{1,0:T(8,128)(2,1)S(1)} %get-tuple-element.15) | copy-start | bytes 3932164
  114.4 1.4 copy-start.12
  115.8 1.1 copy-start.4
  115.8 1.4 copy-start.13
  117.3 1.6 copy-start.14
  118.9 0.7 copy-start.9
  130.7 7.2 %copy-start.1 = (bf16[64,176,128]{2,1,0:T(8,128)(2,1)S(1)}, bf16[64,176,128]{2,1,0:T(8,128)(2,1)}, u32[]{:S(2)}) copy-start(bf16[64,176,128]{2,1,0:T(8,128)(2,1)} %shard_map.120) | copy-start | bytes 8650756
  130.7 5.2 %collective-permute-start.1 = (bf16[640,4,256]{2,0,1:T(8,128)(2,1)S(1)}, bf16[640,4,256]{2,0,1:T(8,128)(2,1)S(1)}, u32[]{:S(2)}, u32[]{:S(2)}) collective-permute-start(bf16[640,4,256]{2,0,1:T(8,128)(2,1)S(1)} %select_bitcast_fusion), channel_id=1, source_target_pairs={{0,1},{1,0},{2,3},{3,2},{4,5},{5,4},{6,7},{7,6},{8,9},{9,8},{10,11... | collective-permute-start | bytes 3932168 | tf_op jit(solution)/shard_map/ppermute | solution.py:82
  138.0 4.5 %copy-start.6 = (bf16[640,1024]{1,0:T(8,128)(2,1)S(1)}, bf16[640,1024]{1,0:T(8,128)(2,1)}, u32[]{:S(2)}) copy-start(bf16[640,1024]{1,0:T(8,128)(2,1)} %get-tuple-element.14) | copy-start | bytes 3932164
  138.0 4.5 %copy-start.7 = (bf16[640,1024]{1,0:T(8,128)(2,1)S(1)}, bf16[640,1024]{1,0:T(8,128)(2,1)}, u32[]{:S(2)}) copy-start(bf16[640,1024]{1,0:T(8,128)(2,1)} %get-tuple-element.16) | copy-start | bytes 3932164
  138.2 0.8 copy-start.8
  145.0 1.3 copy-start.3
  145.0 1.7 copy-start.5
  145.0 1.8 copy-start.15
  146.7 1.4 copy-start.16
Sparse Core Ops, SparseCore 0:
  138.0 43.8 reduce-scatter.1

commit v8 on v5

--- a/solution.py
+++ b/solution.py
@@ -72,6 +72,67 @@
         scratch_shapes=[
             pltpu.SemaphoreType.DMA((n,)),
             pltpu.SemaphoreType.DMA((n,)),
+            pltpu.SemaphoreType.DMA(()),
+        ],
+        compiler_params=pltpu.CompilerParams(collective_id=collective_id, has_side_effects=True),
+    )(x)
+
+
+def _ring4_kernel(axis, x_ref, y_ref, relay_up, relay_down, send_sem, recv_sem, own_sem):
+    me = lax.axis_index(axis)
+    up, down, across = lax.rem(me + 1, 4), lax.rem(me + 3, 4), lax.rem(me + 2, 4)
+    rows = x_ref.shape[1] // 2
+
+    def remote(src, dst, slot, peer):
+        return pltpu.make_async_remote_copy(
+            src_ref=src,
+            dst_ref=dst,
+            send_sem=send_sem.at[slot],
+            recv_sem=recv_sem.at[slot],
+            device_id={axis: peer},
+            device_id_type=MESH,
+        )
+
+    barrier = pltpu.get_barrier_semaphore()
+    for peer in (up, down):
+        pl.semaphore_signal(barrier, inc=1, device_id={axis: peer}, device_id_type=MESH)
+    pl.semaphore_wait(barrier, 2)
+
+    own = pltpu.make_async_copy(x_ref.at[me], y_ref.at[me], own_sem)
+    own.start()
+    to_up = remote(x_ref.at[up], y_ref.at[me], 0, up)
+    to_down = remote(x_ref.at[down], y_ref.at[me], 1, down)
+    lift = remote(x_ref.at[across, pl.ds(0, rows)], relay_up, 2, up)
+    drop = remote(x_ref.at[across, pl.ds(rows, rows)], relay_down, 3, down)
+    for copy in (to_up, to_down, lift, drop):
+        copy.start()
+    lift.wait_recv()
+    pass_up = remote(relay_up, y_ref.at[down, pl.ds(0, rows)], 4, up)
+    pass_up.start()
+    drop.wait_recv()
+    pass_down = remote(relay_down, y_ref.at[up, pl.ds(rows, rows)], 5, down)
+    pass_down.start()
+    for copy in (to_up, to_down, lift, drop, pass_up, pass_down):
+        copy.wait_send()
+    to_up.wait_recv()
+    to_down.wait_recv()
+    pass_up.wait_recv()
+    pass_down.wait_recv()
+    own.wait()
+
+
+def _ring4_exchange(x, collective_id, axis):
+    rows = x.shape[1] // 2
+    return pl.pallas_call(
+        functools.partial(_ring4_kernel, axis),
+        out_shape=jax.ShapeDtypeStruct(x.shape, x.dtype),
+        in_specs=[pl.BlockSpec(memory_space=pl.ANY)],
+        out_specs=pl.BlockSpec(memory_space=pl.ANY),
+        scratch_shapes=[
+            pltpu.VMEM((rows,) + x.shape[2:], x.dtype),
+            pltpu.VMEM((rows,) + x.shape[2:], x.dtype),
+            pltpu.SemaphoreType.DMA((6,)),
+            pltpu.SemaphoreType.DMA((6,)),
             pltpu.SemaphoreType.DMA(()),
         ],
         compiler_params=pltpu.CompilerParams(collective_id=collective_id, has_side_effects=True),
@@ -189,7 +250,7 @@
     keep = jnp.where(is_first, pieces[:, :, 0, :], pieces[:, :, 1, :])
     give = jnp.where(is_first, pieces[:, :, 1, :], pieces[:, :, 0, :])
     pair_sum = (keep.astype(jnp.float32) + _swap_pair(give).astype(jnp.float32)).astype(jnp.bfloat16)
-    by_group = _exchange(jnp.transpose(pair_sum, (1, 0, 2)), 2, axis="zh")
+    by_group = _ring4_exchange(jnp.transpose(pair_sum, (1, 0, 2)), 2, "zh")
     slice_sum = jnp.sum(by_group.astype(jnp.float32), axis=0).astype(jnp.bfloat16)
     returned = _exchange(slice_sum.reshape(owners, capacity * block // lanes, lanes), 1)
     picked = jnp.dot(

time: 209 us -> 211 us (level)
    pallas_call x0 -> x1, Pallas kernels: none -> 37.3 us  [_ring4_exchange(): pl.pallas_call(functools.partial(_ring4_kernel, axis), out_shape=jax.Shap...]
    pallas_call x3 -> x2, Pallas kernels: 134 us -> 97.6 us  [_exchange(): pl.pallas_call(functools.partial(_exchange_kernel, n, axis), out_shape=ja...]
  transfers between devices with their start and end apart: 2 -> 2, of which waited for: 1 -> 1; matrix products, arithmetic and copies ran while one was open for 7% -> 6% of each run, Pallas kernels for 0% -> 0%
where the time goes in v8:
time: 211 us; the launch traced here: 209 us
  Pallas kernels  135 us (64%)
  local copies, waits for them, and re-layouts  27.4 us (13%)
  other arithmetic  24.8 us (12%)
  matrix products  13.4 us (6%)
  starting transfers between devices  4.12 us (2%)
  waiting for transfers between devices  3.12 us (1%)
    pallas_call x2, Pallas kernels, _exchange(): pl.pallas_call(functools.partial(_exchange_kernel, n, axis), out_shape=ja...  97.6 us
    pallas_call x1, Pallas kernels, _ring4_exchange(): pl.pallas_call(functools.partial(_ring4_kernel, axis), out_shape=jax.Shap...  37.3 us
    unnamed x35, local copies, waits for them, and re-layouts  7.25 us
  transfers between devices with their start and end apart: 2, of which 1 were waited for; matrix products, arithmetic and copies ran while one was open for 6% of the time, Pallas kernels for 0%

profile of v8, /device:TPU:6, one launch (start us, length us, event | category | flops | bytes accessed | tf_op | source)
XLA Modules:
  0.0 208.7 jit_solution(2446300581189785035)
XLA Ops:
  0.7 0.9 copy.35
  1.8 1.2 reduce-window.6
  3.6 0.7 fusion.27
  4.3 1.3 fusion.34
  5.6 0.6 fusion.35
  6.3 0.7 reduce_sum.117
  7.0 0.7 broadcast_divide_fusion
  8.2 0.7 multiply_add_fusion
  9.7 1.4 fusion.28
  11.5 0.8 convolution_convert_fusion.1
  12.3 3.2 %reshape.169 = bf16[64,160,128]{2,1,0:T(8,128)(2,1)} reshape(bf16[640,2048]{1,0:T(8,128)(2,1)S(1)} %convolution_convert_fusion.1) | data formatting | bytes 5242880 | tf_op jit(solution)/shard_map/reshape | solution.py:215
  15.5 3.5 %pad_maximum_fusion.x_ref = bf16[64,176,128]{2,1,0:T(8,128)(2,1)} fusion(bf16[64,16,128]{2,1,0:T(8,128)(2,1)S(1)} %bitcast.66, bf16[64,160,128]{2,1,0:T(8,128)(2,1)} %reshape.169), kind=kLoop, calls=%fused_computation.3 | loop fusion | flops 5767168 | bytes 5767168 | tf_op jit(solution)/shard_map/concatenate | solution.py:214
  19.0 73.5 %shard_map.120 = bf16[64,176,128]{2,1,0:T(8,128)(2,1)} custom-call(bf16[64,176,128]{2,1,0:T(8,128)(2,1)} %pad_maximum_fusion.x_ref), custom_call_target="tpu_custom_call" | custom-call | tf_op jit(solution)/shard_map/pallas_call | solution.py:67
  92.5 1.7 slice-done
  94.3 3.1 %reshape.171 = bf16[640,2048]{1,0:T(8,128)(2,1)} reshape(bf16[64,160,128]{2,1,0:T(8,128)(2,1)S(1)} %slice-done) | data formatting | bytes 5242880 | tf_op jit(solution)/shard_map/reshape | solution.py:219
  97.3 1.9 collective-permute-start
  99.3 1.0 slice_convert_fusion
  100.3 1.0 copy.51
  101.2 3.1 %collective-permute-done = bf16[640,2048]{1,0:T(8,128)(2,1)S(1)} collective-permute-done((bf16[640,2048]{1,0:T(8,128)(2,1)}, bf16[640,2048]{1,0:T(8,128)(2,1)S(1)}, u32[]{:S(2)}, u32[]{:S(2)}) %collective-permute-start) | collective-permute-done | bytes 2621472 | tf_op jit(solution)/shard_map/ppermute | solution.py:143
  104.3 2.1 broadcast_select_fusion.1
  106.4 1.3 fusion.36
  107.8 1.3 fusion.37
  109.2 0.8 convolution_bitcast_fusion.2
  110.2 0.4 copy-done.11
  110.6 1.6 multiply_convert_fusion.3
  112.2 0.7 copy-done.7
  112.8 2.3 %convolution_convert_fusion = bf16[640,2048]{1,0:T(8,128)(2,1)} fusion(bf16[128,640]{0,1:T(8,128)(2,1)S(1)} %get-tuple-element.23, bf16[1,128,2048]{2,1,0:T(8,128)(2,1)S(1)} %copy-done), kind=kOutput, calls=%fused_computation.1 | convolution fusion | flops 336855040 | bytes 3309568 | tf_op jit(solution)/shard_map/dot_general | solution.py:246
  115.2 3.1 %copy.41 = bf16[640,2048]{0,1:T(8,128)(2,1)S(1)} copy(bf16[640,2048]{1,0:T(8,128)(2,1)} %convolution_convert_fusion) | data formatting | bytes 5242880 | tf_op jit(solution)/shard_map/convert_element_type | solution.py:248
  118.3 1.7 fusion.38
  120.0 1.6 copy.44
  121.6 1.6 copy.45
  123.2 1.2 select_bitcast_fusion
  124.5 2.2 %collective-permute-start.1 = (bf16[640,4,256]{2,0,1:T(8,128)(2,1)}, bf16[640,4,256]{2,0,1:T(8,128)(2,1)}, u32[]{:S(2)}, u32[]{:S(2)}) collective-permute-start(bf16[640,4,256]{2,0,1:T(8,128)(2,1)} %select_bitcast_fusion), channel_id=1, source_target_pairs={{0,1},{1,0},{2,3},{3,2},{4,5},{5,4},{6,7},{7,6},{8,9},{9,8},{10,11... | collective-permute-start | bytes 3932168 | tf_op jit(solution)/shard_map/ppermute | solution.py:143
  126.7 1.6 slice_reduce_fusion.2
  128.2 0.8 slice.79
  129.1 1.8 fusion.17
  131.0 3.5 %fusion.3 = bf16[1,128,2048]{2,1,0:T(8,128)(2,1)} fusion(bf16[128,640]{0,1:T(8,128)(2,1)} %copy-done.7, bf16[640,1024]{1,0:T(8,128)(2,1)} %get-tuple-element.16, bf16[640,1024]{1,0:T(8,128)(2,1)} %get-tuple-element.14, f32[640]{0:T(1024)S(1)} %fusion.17), kind=kOutput, calls=%fused_computation.14 | convolution fusion | flops 343670784 | bytes 3312128 | tf_op jit(solution)/shard_map/dot_general | solution.py:263
  134.5 0.9 convolution_bitcast_fusion
  136.2 1.4 fusion.2
  137.7 1.5 fusion.1
  139.2 2.9 %fusion.4.x_ref = bf16[4,640,256]{2,1,0:T(8,128)(2,1)} fusion(bf16[640,4,256]{2,0,1:T(8,128)(2,1)} %collective-permute-done.1, bf16[640,4,1,256]{3,0,1,2:T(8,128)(2,1)S(1)} %copy.44, bf16[640,4,1,256]{3,0,1,2:T(8,128)(2,1)S(1)} %copy.45, pred[]{:T(512)S(6)} %eq.69), kind=kLoop, calls=%fused_computation.15 | loop fusion | flops 3276800 | bytes 5242881 | tf_op jit(solution)/shard_map/transpose | solution.py:253
  142.0 37.3 %shard_map.121 = bf16[4,640,256]{2,1,0:T(8,128)(2,1)} custom-call(bf16[4,640,256]{2,1,0:T(8,128)(2,1)} %fusion.4.x_ref), custom_call_target="tpu_custom_call" | custom-call | tf_op jit(solution)/shard_map/pallas_call | solution.py:126
  179.3 1.6 reduce_sum.125
  181.0 0.9 reshape.173.x_ref
  181.9 24.1 %shard_map.122 = bf16[64,20,128]{2,1,0:T(8,128)(2,1)} custom-call(bf16[64,20,128]{2,1,0:T(8,128)(2,1)} %reshape.173.x_ref), custom_call_target="tpu_custom_call" | custom-call | tf_op jit(solution)/shard_map/pallas_call | solution.py:67
  205.9 1.2 reshape.174
  207.1 0.5 fusion.7
  207.8 0.9 reduce_sum.126
  (60 shorter events, 3.8 us)
Async XLA Ops:
  0.6 112.2 %copy-start = (bf16[1,128,2048]{2,1,0:T(8,128)(2,1)S(1)}, bf16[1,128,2048]{2,1,0:T(8,128)(2,1)}, u32[]{:S(2)}) copy-start(bf16[1,128,2048]{2,1,0:T(8,128)(2,1)} %param.17) | copy-start | bytes 1572868
  0.6 10.7 %copy-start.8 = (bf16[128,2048]{1,0:T(8,128)(2,1)S(1)}, bf16[128,2048]{1,0:T(8,128)(2,1)}, u32[]{:S(2)}) copy-start(bf16[128,2048]{1,0:T(8,128)(2,1)} %param.10) | copy-start | bytes 1572868
  0.7 10.7 %copy-start.9 = (bf16[128,2048]{1,0:T(8,128)(2,1)S(1)}, bf16[128,2048]{1,0:T(8,128)(2,1)}, u32[]{:S(2)}) copy-start(bf16[128,2048]{1,0:T(8,128)(2,1)} %param.9) | copy-start | bytes 1572868
  92.5 1.7 slice-start
  97.3 7.0 %collective-permute-start = (bf16[640,2048]{1,0:T(8,128)(2,1)}, bf16[640,2048]{1,0:T(8,128)(2,1)S(1)}, u32[]{:S(2)}, u32[]{:S(2)}) collective-permute-start(bf16[640,2048]{1,0:T(8,128)(2,1)} %reshape.171), channel_id=1, source_target_pairs={{0,1},{1,0},{2,3},{3,2},{4,5},{5,4},{6,7},{7,6},{8,9},{9,8},{10,11... | collective-permute-start | bytes 7864328 | tf_op jit(solution)/shard_map/ppermute | solution.py:143
  107.8 2.3 %copy-start.1 = (bf16[640,1024]{1,0:T(8,128)(2,1)}, bf16[640,1024]{1,0:T(8,128)(2,1)S(1)}, u32[]{:S(2)}) copy-start(bf16[640,1024]{1,0:T(8,128)(2,1)S(1)} %get-tuple-element.15) | copy-start | bytes 3932164
  107.8 1.4 copy-start.10
  109.1 1.1 copy-start.3
  109.2 1.4 copy-start.11
  110.6 1.6 copy-start.12
  112.2 0.7 copy-start.7
  124.5 14.7 %collective-permute-start.1 = (bf16[640,4,256]{2,0,1:T(8,128)(2,1)}, bf16[640,4,256]{2,0,1:T(8,128)(2,1)}, u32[]{:S(2)}, u32[]{:S(2)}) collective-permute-start(bf16[640,4,256]{2,0,1:T(8,128)(2,1)} %select_bitcast_fusion), channel_id=1, source_target_pairs={{0,1},{1,0},{2,3},{3,2},{4,5},{5,4},{6,7},{7,6},{8,9},{9,8},{10,11... | collective-permute-start | bytes 3932168 | tf_op jit(solution)/shard_map/ppermute | solution.py:143
  130.9 3.5 %copy-start.5 = (bf16[640,1024]{1,0:T(8,128)(2,1)S(1)}, bf16[640,1024]{1,0:T(8,128)(2,1)}, u32[]{:S(2)}) copy-start(bf16[640,1024]{1,0:T(8,128)(2,1)} %get-tuple-element.14) | copy-start | bytes 3932164
  131.0 3.5 %copy-start.6 = (bf16[640,1024]{1,0:T(8,128)(2,1)S(1)}, bf16[640,1024]{1,0:T(8,128)(2,1)}, u32[]{:S(2)}) copy-start(bf16[640,1024]{1,0:T(8,128)(2,1)} %get-tuple-element.16) | copy-start | bytes 3932164
  134.4 1.3 copy-start.2
  134.5 1.7 copy-start.4
  134.5 1.7 copy-start.13
  136.2 1.4 copy-start.14

commit v9 on v8

--- a/solution.py
+++ b/solution.py
@@ -243,14 +243,13 @@
     )
     sigmoid_gate = jax.nn.sigmoid(gate_pre)
     hidden = (gate_pre * sigmoid_gate * up_pre).astype(jnp.bfloat16)
-    partial_out = lax.dot_general(
-        hidden, down_weight[0], contract_first, preferred_element_type=jnp.float32
-    ).astype(jnp.bfloat16)
-    pieces = partial_out.reshape(slots_all, groups, 2, block)
-    keep = jnp.where(is_first, pieces[:, :, 0, :], pieces[:, :, 1, :])
-    give = jnp.where(is_first, pieces[:, :, 1, :], pieces[:, :, 0, :])
+    down_groups = down_weight[0].reshape(down_weight.shape[1], groups, 2, block)
+    keep_w = jnp.where(is_first, down_groups[:, :, 0, :], down_groups[:, :, 1, :])
+    give_w = jnp.where(is_first, down_groups[:, :, 1, :], down_groups[:, :, 0, :])
+    keep = jnp.einsum("hr,hzb->zrb", hidden, keep_w, preferred_element_type=jnp.float32).astype(jnp.bfloat16)
+    give = jnp.einsum("hr,hzb->zrb", hidden, give_w, preferred_element_type=jnp.float32).astype(jnp.bfloat16)
     pair_sum = (keep.astype(jnp.float32) + _swap_pair(give).astype(jnp.float32)).astype(jnp.bfloat16)
-    by_group = _ring4_exchange(jnp.transpose(pair_sum, (1, 0, 2)), 2, "zh")
+    by_group = _ring4_exchange(pair_sum, 2, "zh")
     slice_sum = jnp.sum(by_group.astype(jnp.float32), axis=0).astype(jnp.bfloat16)
     returned = _exchange(slice_sum.reshape(owners, capacity * block // lanes, lanes), 1)
     picked = jnp.dot(

time: 211 us -> 205 us (0.972)
  other arithmetic: 24.8 us -> 20.7 us
  waiting for transfers between devices: 3.12 us -> 0.01 us
  matrix products: 13.4 us -> 15.6 us
    convert_element_type x1 -> x0, local copies, waits for them, and re-layouts: 3.13 us -> none  [body(): partial_out = lax.dot_general(hidden, down_weight[0], contract_first, pre...]
    ppermute x2, waiting for transfers between devices: 3.12 us -> 0.01 us  [_swap_pair(): return lax.ppermute(x, 'core', [(0, 1), (1, 0)])]
    transpose x1 -> x0, other arithmetic: 2.88 us -> none  [body(): by_group = _ring4_exchange(jnp.transpose(pair_sum, (1, 0, 2)), 2, 'zh')]
    another operation x1 -> x2, local copies, waits for them, and re-layouts: 0.01 us -> 2.37 us  [the longest x1 2.36 us: body(): down_groups = down_weight[0].reshape(down_weight.shape[1], groups, 2, block)]
    dot_general x1 -> x2, matrix products: 2.34 us -> 4.49 us  [the longest x1 2.89 us: body(): jnp.einsum('hr,hzb->zrb', hidden, keep_w, preferred_element_type=jnp.floa...]
    unnamed x35 -> x33, local copies, waits for them, and re-layouts: 7.25 us -> 5.78 us
  transfers between devices with their start and end apart: 2 -> 2, of which waited for: 1 -> 0; matrix products, arithmetic and copies ran while one was open for 6% -> 11% of each run, Pallas kernels for 0% -> 0%
where the time goes in v9:
time: 205 us; the launch traced here: 203 us
  Pallas kernels  134 us (65%)
  local copies, waits for them, and re-layouts  26.5 us (13%)
  other arithmetic  20.7 us (10%)
  matrix products  15.6 us (8%)
  starting transfers between devices  4.48 us (2%)
    pallas_call x2, Pallas kernels, _exchange(): pl.pallas_call(functools.partial(_exchange_kernel, n, axis), out_shape=ja...  97.5 us
    pallas_call x1, Pallas kernels, _ring4_exchange(): pl.pallas_call(functools.partial(_ring4_kernel, axis), out_shape=jax.Shap...  36.9 us
    unnamed x33, local copies, waits for them, and re-layouts  5.78 us
    ppermute x2, starting transfers between devices, _swap_pair(): return lax.ppermute(x, 'core', [(0, 1), (1, 0)])  4.48 us
  transfers between devices with their start and end apart: 2, of which 0 were waited for; matrix products, arithmetic and copies ran while one was open for 11% of the time, Pallas kernels for 0%

profile of v9, /device:TPU:6, one launch (start us, length us, event | category | flops | bytes accessed | tf_op | source)
XLA Modules:
  0.0 202.7 jit_solution(7388520652513796850)
XLA Ops:
  0.7 0.9 copy.47
  1.8 1.2 reduce-window.6
  3.0 0.2 slice_reduce_fusion
  3.6 0.7 fusion.34
  4.3 1.3 fusion.41
  5.6 0.6 fusion.42
  6.3 0.7 multiply_add_fusion
  7.2 0.2 select_reduce_fusion.1
  7.5 0.7 reduce_sum.117
  8.2 0.7 broadcast_divide_fusion
  9.7 1.4 fusion.35
  11.1 0.2 concatenate.21
  11.5 0.8 convolution_convert_fusion
  12.3 3.2 %reshape.164 = bf16[64,160,128]{2,1,0:T(8,128)(2,1)} reshape(bf16[640,2048]{1,0:T(8,128)(2,1)S(1)} %convolution_convert_fusion) | data formatting | bytes 5242880 | tf_op jit(solution)/shard_map/reshape | solution.py:215
  15.4 3.5 %pad_maximum_fusion.x_ref = bf16[64,176,128]{2,1,0:T(8,128)(2,1)} fusion(bf16[64,16,128]{2,1,0:T(8,128)(2,1)S(1)} %bitcast.72, bf16[64,160,128]{2,1,0:T(8,128)(2,1)} %reshape.164), kind=kLoop, calls=%fused_computation.2 | loop fusion | flops 5767168 | bytes 5767168 | tf_op jit(solution)/shard_map/concatenate | solution.py:214
  19.0 73.5 %shard_map.120 = bf16[64,176,128]{2,1,0:T(8,128)(2,1)} custom-call(bf16[64,176,128]{2,1,0:T(8,128)(2,1)} %pad_maximum_fusion.x_ref), custom_call_target="tpu_custom_call" | custom-call | tf_op jit(solution)/shard_map/pallas_call | solution.py:67
  92.6 1.7 slice-done
  94.3 3.1 %reshape.166 = bf16[640,2048]{1,0:T(8,128)(2,1)} reshape(bf16[64,160,128]{2,1,0:T(8,128)(2,1)S(1)} %slice-done) | data formatting | bytes 5242880 | tf_op jit(solution)/shard_map/reshape | solution.py:219
  97.4 1.9 collective-permute-start
  99.3 1.0 slice_convert_fusion
  100.3 1.0 copy.72
  101.3 2.4 %reshape_squeeze.3 = bf16[128,4,2,256]{3,2,1,0:T(2,128)(2,1)} reshape(bf16[1,128,2048]{2,1,0:T(8,128)(2,1)} %param.17) | data formatting | bytes 1048576 | tf_op jit(solution)/shard_map/reshape;squeeze | solution.py:246
  103.6 3.1 %fusion.45 = (bf16[128,4,1,256]{3,2,1,0:T(2,128)(2,1)}, bf16[128,4,1,256]{3,2,1,0:T(2,128)(2,1)}) fusion(bf16[128,4,2,256]{3,2,1,0:T(2,128)(2,1)} %reshape_squeeze.3), kind=kLoop, calls=%fused_computation.103 | loop fusion | bytes 1048576 | tf_op jit(solution)/shard_map/slice | solution.py:247
  106.8 1.3 copy.65
  108.1 1.9 copy.66
  110.0 2.1 %broadcast_select_fusion.1 = (bf16[640,2048]{1,0:T(8,128)(2,1)S(1)}, bf16[640,2048]{1,0:T(8,128)(2,1)S(1)}) fusion(bf16[640,2048]{1,0:T(8,128)(2,1)S(1)} %copy-done.1, bf16[640,2048]{1,0:T(8,128)(2,1)} %collective-permute-done, pred[]{:T(512)S(6)} %eq.69), kind=kLoop, calls=%fused_computation.7 | loop fusion | flops 2621440 | bytes 10485761 | tf_op jit(solution)/shard_map/jit(_where)/select_n | solution.py:222
  112.1 1.3 fusion.43
  113.4 1.3 fusion.44
  114.7 0.9 convolution_bitcast_fusion.2
  115.8 1.6 multiply_convert_fusion.3
  117.4 1.6 fusion.4
  119.0 2.6 %collective-permute-start.1 = (bf16[4,640,256]{2,1,0:T(8,128)(2,1)}, bf16[4,640,256]{2,1,0:T(8,128)(2,1)}, u32[]{:S(2)}, u32[]{:S(2)}) collective-permute-start(bf16[4,640,256]{2,1,0:T(8,128)(2,1)} %fusion.4), channel_id=1, source_target_pairs={{0,1},{1,0},{2,3},{3,2},{4,5},{5,4},{6,7},{7,6},{8,9},{9,8},{10,11... | collective-permute-start | bytes 3932168 | tf_op jit(solution)/shard_map/ppermute | solution.py:143
  121.6 1.5 slice_reduce_fusion.2
  123.1 0.8 slice.79
  124.0 1.8 fusion.16
  125.9 3.4 %fusion.3 = bf16[1,128,2048]{2,1,0:T(8,128)(2,1)} fusion(bf16[128,640]{0,1:T(8,128)(2,1)S(1)} %get-tuple-element.23, bf16[640,1024]{1,0:T(8,128)(2,1)} %get-tuple-element.16, bf16[640,1024]{1,0:T(8,128)(2,1)} %get-tuple-element.14, f32[640]{0:T(1024)S(1)} %fusion.16), kind=kOutput, calls=%fused_computation.13 | convolution fusion | flops 343670784 | bytes 3312128 | tf_op jit(solution)/shard_map/dot_general | solution.py:262
  129.3 0.9 convolution_bitcast_fusion
  130.2 0.4 copy-done.4
  130.6 1.4 fusion.2
  132.1 1.5 fusion.1
  133.6 2.9 %fusion.x_ref = bf16[4,640,256]{2,1,0:T(8,128)(2,1)} fusion(bf16[4,640,256]{2,1,0:T(8,128)(2,1)} %collective-permute-done.1, bf16[128,4,1,256]{0,3,1,2:T(8,128)(2,1)S(1)} %copy.65, bf16[128,4,1,256]{0,3,1,2:T(8,128)(2,1)S(1)} %copy-done.2, pred[]{:T(512)S(6)} %eq.69, bf16[128,640]{0,1:T(8,128)(2,1)S(1)} %get-tuple-element.23), kind=kOutput, calls=%fused_computation.5 | convolution fusion | flops 171180032 | bytes 3309569 | tf_op jit(solution)/shard_map/hr,hzb->zrb/dot_general | solution.py:249
  136.5 36.9 %shard_map.121 = bf16[4,640,256]{2,1,0:T(8,128)(2,1)} custom-call(bf16[4,640,256]{2,1,0:T(8,128)(2,1)} %fusion.x_ref), custom_call_target="tpu_custom_call" | custom-call | tf_op jit(solution)/shard_map/pallas_call | solution.py:126
  173.4 1.6 reduce_sum.125
  175.1 0.9 reshape.167.x_ref
  175.9 24.0 %shard_map.122 = bf16[64,20,128]{2,1,0:T(8,128)(2,1)} custom-call(bf16[64,20,128]{2,1,0:T(8,128)(2,1)} %reshape.167.x_ref), custom_call_target="tpu_custom_call" | custom-call | tf_op jit(solution)/shard_map/pallas_call | solution.py:67
  199.9 1.2 reshape.168
  201.1 0.5 fusion.7
  201.8 0.9 reduce_sum.126
  (57 shorter events, 2.3 us)
Async XLA Ops:
  0.6 115.2 %copy-start = (bf16[1,128,2048]{2,1,0:T(8,128)(2,1)S(1)}, bf16[1,128,2048]{2,1,0:T(8,128)(2,1)}, u32[]{:S(2)}) copy-start(bf16[1,128,2048]{2,1,0:T(8,128)(2,1)} %param.16) | copy-start | bytes 1572868
  0.6 10.8 %copy-start.8 = (bf16[128,2048]{1,0:T(8,128)(2,1)S(1)}, bf16[128,2048]{1,0:T(8,128)(2,1)}, u32[]{:S(2)}) copy-start(bf16[128,2048]{1,0:T(8,128)(2,1)} %param.10) | copy-start | bytes 1572868
  0.7 10.8 %copy-start.9 = (bf16[128,2048]{1,0:T(8,128)(2,1)S(1)}, bf16[128,2048]{1,0:T(8,128)(2,1)}, u32[]{:S(2)}) copy-start(bf16[128,2048]{1,0:T(8,128)(2,1)} %param.9) | copy-start | bytes 1572868
  92.6 1.7 slice-start
  97.4 12.6 %collective-permute-start = (bf16[640,2048]{1,0:T(8,128)(2,1)}, bf16[640,2048]{1,0:T(8,128)(2,1)}, u32[]{:S(2)}, u32[]{:S(2)}) collective-permute-start(bf16[640,2048]{1,0:T(8,128)(2,1)} %reshape.166), channel_id=1, source_target_pairs={{0,1},{1,0},{2,3},{3,2},{4,5},{5,4},{6,7},{7,6},{8,9},{9,8},{10,11... | collective-permute-start | bytes 7864328 | tf_op jit(solution)/shard_map/ppermute | solution.py:143
  101.3 8.7 %copy-start.1 = (bf16[640,2048]{1,0:T(8,128)(2,1)S(1)}, bf16[640,2048]{1,0:T(8,128)(2,1)}, u32[]{:S(2)}) copy-start(bf16[640,2048]{1,0:T(8,128)(2,1)} %reshape.166) | copy-start | bytes 7864324
  113.4 1.3 copy-start.10
  114.7 1.1 copy-start.3
  115.8 1.6 copy-start.11
  115.8 1.6 copy-start.2
  119.0 14.6 %collective-permute-start.1 = (bf16[4,640,256]{2,1,0:T(8,128)(2,1)}, bf16[4,640,256]{2,1,0:T(8,128)(2,1)}, u32[]{:S(2)}, u32[]{:S(2)}) collective-permute-start(bf16[4,640,256]{2,1,0:T(8,128)(2,1)} %fusion.4), channel_id=1, source_target_pairs={{0,1},{1,0},{2,3},{3,2},{4,5},{5,4},{6,7},{7,6},{8,9},{9,8},{10,11... | collective-permute-start | bytes 3932168 | tf_op jit(solution)/shard_map/ppermute | solution.py:143
  125.8 3.4 %copy-start.5 = (bf16[640,1024]{1,0:T(8,128)(2,1)S(1)}, bf16[640,1024]{1,0:T(8,128)(2,1)}, u32[]{:S(2)}) copy-start(bf16[640,1024]{1,0:T(8,128)(2,1)} %get-tuple-element.14) | copy-start | bytes 3932164
  125.8 3.4 %copy-start.6 = (bf16[640,1024]{1,0:T(8,128)(2,1)S(1)}, bf16[640,1024]{1,0:T(8,128)(2,1)}, u32[]{:S(2)}) copy-start(bf16[640,1024]{1,0:T(8,128)(2,1)} %get-tuple-element.16) | copy-start | bytes 3932164
  125.9 3.4 %copy-start.7 = (bf16[1,128,2048]{2,1,0:T(8,128)(2,1)S(1)}, bf16[1,128,2048]{2,1,0:T(8,128)(2,1)}, u32[]{:S(2)}) copy-start(bf16[1,128,2048]{2,1,0:T(8,128)(2,1)} %param.17) | copy-start | bytes 1572868
  129.3 1.3 copy-start.4
  129.3 1.4 copy-start.12
  130.6 1.5 copy-start.13

commit v10 on v9

--- a/solution.py
+++ b/solution.py
@@ -139,6 +139,105 @@
     )(x)
 
 
+def _both_kernel(n, a_ref, b_ref, ya_ref, yb_ref, a_send, a_recv, a_own, relay_up, relay_down, b_send, b_recv, b_own):
+    me = lax.axis_index("dp")
+    at = lax.axis_index("zh")
+    up, down, across = lax.rem(at + 1, 4), lax.rem(at + 3, 4), lax.rem(at + 2, 4)
+    rows = b_ref.shape[1] // 2
+
+    def dp_copy(src, dst, slot_send, slot_recv, peer):
+        return pltpu.make_async_remote_copy(
+            src_ref=src,
+            dst_ref=dst,
+            send_sem=a_send.at[slot_send],
+            recv_sem=a_recv.at[slot_recv],
+            device_id={"dp": peer},
+            device_id_type=MESH,
+        )
+
+    def zh_copy(src, dst, slot, peer):
+        return pltpu.make_async_remote_copy(
+            src_ref=src,
+            dst_ref=dst,
+            send_sem=b_send.at[slot],
+            recv_sem=b_recv.at[slot],
+            device_id={"zh": peer},
+            device_id_type=MESH,
+        )
+
+    barrier = pltpu.get_barrier_semaphore()
+
+    def greet(i, carry):
+        pl.semaphore_signal(barrier, inc=1, device_id={"dp": lax.rem(me + i, n)}, device_id_type=MESH)
+        return carry
+
+    lax.fori_loop(1, n, greet, 0)
+    for peer in (up, down):
+        pl.semaphore_signal(barrier, inc=1, device_id={"zh": peer}, device_id_type=MESH)
+    pl.semaphore_wait(barrier, n + 1)
+
+    own_a = pltpu.make_async_copy(a_ref.at[me], ya_ref.at[me], a_own)
+    own_a.start()
+    own_b = pltpu.make_async_copy(b_ref.at[at], yb_ref.at[at], b_own)
+    own_b.start()
+    to_up = zh_copy(b_ref.at[up], yb_ref.at[at], 0, up)
+    to_down = zh_copy(b_ref.at[down], yb_ref.at[at], 1, down)
+    lift = zh_copy(b_ref.at[across, pl.ds(0, rows)], relay_up, 2, up)
+    drop = zh_copy(b_ref.at[across, pl.ds(rows, rows)], relay_down, 3, down)
+    for copy in (to_up, to_down, lift, drop):
+        copy.start()
+
+    def send(i, carry):
+        peer = lax.rem(me + i, n)
+        dp_copy(a_ref.at[peer], ya_ref.at[me], peer, me, peer).start()
+        return carry
+
+    lax.fori_loop(1, n, send, 0)
+    lift.wait_recv()
+    pass_up = zh_copy(relay_up, yb_ref.at[down, pl.ds(0, rows)], 4, up)
+    pass_up.start()
+    drop.wait_recv()
+    pass_down = zh_copy(relay_down, yb_ref.at[up, pl.ds(rows, rows)], 5, down)
+    pass_down.start()
+
+    def finish(i, carry):
+        peer = lax.rem(me + i, n)
+        source = lax.rem(me + n - i, n)
+        dp_copy(a_ref.at[peer], ya_ref.at[me], peer, me, peer).wait_send()
+        dp_copy(a_ref.at[source], ya_ref.at[source], source, source, source).wait_recv()
+        return carry
+
+    lax.fori_loop(1, n, finish, 0)
+    for copy in (to_up, to_down, lift, drop, pass_up, pass_down):
+        copy.wait_send()
+    for copy in (to_up, to_down, pass_up, pass_down):
+        copy.wait_recv()
+    own_a.wait()
+    own_b.wait()
+
+
+def _exchange_both(a, b, collective_id):
+    n = a.shape[0]
+    rows = b.shape[1] // 2
+    return pl.pallas_call(
+        functools.partial(_both_kernel, n),
+        out_shape=(jax.ShapeDtypeStruct(a.shape, a.dtype), jax.ShapeDtypeStruct(b.shape, b.dtype)),
+        in_specs=[pl.BlockSpec(memory_space=pl.ANY)] * 2,
+        out_specs=(pl.BlockSpec(memory_space=pl.ANY), pl.BlockSpec(memory_space=pl.ANY)),
+        scratch_shapes=[
+            pltpu.SemaphoreType.DMA((n,)),
+            pltpu.SemaphoreType.DMA((n,)),
+            pltpu.SemaphoreType.DMA(()),
+            pltpu.VMEM((rows,) + b.shape[2:], b.dtype),
+            pltpu.VMEM((rows,) + b.shape[2:], b.dtype),
+            pltpu.SemaphoreType.DMA((6,)),
+            pltpu.SemaphoreType.DMA((6,)),
+            pltpu.SemaphoreType.DMA(()),
+        ],
+        compiler_params=pltpu.CompilerParams(collective_id=collective_id, has_side_effects=True),
+    )(a, b)
+
+
 def _swap_pair(x):
     return lax.ppermute(x, "core", [(0, 1), (1, 0)])
 
@@ -208,30 +307,21 @@
     ).astype(jnp.bfloat16)
     my_tokens = lax.dynamic_slice_in_dim(tokens, core * half, half, axis=1)
     my_cotan = lax.dynamic_slice_in_dim(cotangent, core * half, half, axis=1)
-    both = jnp.concatenate([my_tokens, my_cotan], axis=1)
-    send = jnp.dot(hit_tok.astype(both.dtype), both, preferred_element_type=jnp.float32).astype(both.dtype)
     lanes = 128
+    pick = hit_tok.astype(tokens.dtype)
+    send_tok = jnp.dot(pick, my_tokens, preferred_element_type=jnp.float32).astype(tokens.dtype)
+    send_cot = jnp.dot(pick, my_cotan, preferred_element_type=jnp.float32).astype(tokens.dtype)
     send = jnp.concatenate(
-        [send.reshape(owners, capacity * features // lanes, lanes), meta.reshape(owners, features // lanes, lanes)],
+        [send_tok.reshape(owners, capacity * half // lanes, lanes), meta.reshape(owners, features // lanes, lanes)],
         axis=1,
     )
     recv = _exchange(send, 0)
-    got = recv[:, : capacity * features // lanes, :].reshape(slots_all, features)
-    got_meta = recv[:, capacity * features // lanes :, :].reshape(owners, features).astype(jnp.float32)
+    got = recv[:, : capacity * half // lanes, :].reshape(slots_all, half)
+    got_meta = recv[:, capacity * half // lanes :, :].reshape(owners, features).astype(jnp.float32)
     other = _swap_pair(got)
-    lower = jnp.where(is_first, got, other)
-    upper = jnp.where(is_first, other, got)
-    rows_in = jnp.concatenate([lower[:, :half], upper[:, :half]], axis=1)
-    cot_in = jnp.concatenate([lower[:, half:], upper[:, half:]], axis=1)
-
-    n_forget = jnp.sum(got_meta[:, capacity * 5])
-    n_retain = jnp.sum(got_meta[:, capacity * 5 + 1])
-    slot_meta = got_meta[:, : capacity * 5].reshape(slots_all, 5)
-    got_share = (slot_meta[:, 0] + slot_meta[:, 1]) + slot_meta[:, 2]
-    coefficient = float(top_count * tok_rows) * (
-        slot_meta[:, 4] / n_retain - slot_meta[:, 3] / n_forget
-    )
-    routed = ((coefficient * got_share)[:, None] * cot_in.astype(jnp.float32)).astype(jnp.bfloat16)
+    rows_in = jnp.concatenate(
+        [jnp.where(is_first, got, other), jnp.where(is_first, other, got)], axis=1
+    )
 
     contract_last = (((1,), (1,)), ((), ()))
     contract_first = (((0,), (0,)), ((), ()))
@@ -249,7 +339,20 @@
     keep = jnp.einsum("hr,hzb->zrb", hidden, keep_w, preferred_element_type=jnp.float32).astype(jnp.bfloat16)
     give = jnp.einsum("hr,hzb->zrb", hidden, give_w, preferred_element_type=jnp.float32).astype(jnp.bfloat16)
     pair_sum = (keep.astype(jnp.float32) + _swap_pair(give).astype(jnp.float32)).astype(jnp.bfloat16)
-    by_group = _ring4_exchange(pair_sum, 2, "zh")
+    got_cot, by_group = _exchange_both(send_cot.reshape(owners, capacity * half // lanes, lanes), pair_sum, 3)
+    got_cot = got_cot.reshape(slots_all, half)
+    other_cot = _swap_pair(got_cot)
+    cot_in = jnp.concatenate(
+        [jnp.where(is_first, got_cot, other_cot), jnp.where(is_first, other_cot, got_cot)], axis=1
+    )
+    n_forget = jnp.sum(got_meta[:, capacity * 5])
+    n_retain = jnp.sum(got_meta[:, capacity * 5 + 1])
+    slot_meta = got_meta[:, : capacity * 5].reshape(slots_all, 5)
+    got_share = (slot_meta[:, 0] + slot_meta[:, 1]) + slot_meta[:, 2]
+    coefficient = float(top_count * tok_rows) * (
+        slot_meta[:, 4] / n_retain - slot_meta[:, 3] / n_forget
+    )
+    routed = ((coefficient * got_share)[:, None] * cot_in.astype(jnp.float32)).astype(jnp.bfloat16)
     slice_sum = jnp.sum(by_group.astype(jnp.float32), axis=0).astype(jnp.bfloat16)
     returned = _exchange(slice_sum.reshape(owners, capacity * block // lanes, lanes), 1)
     picked = jnp.dot(

time: 205 us -> 186 us (0.907)
  local copies, waits for them, and re-layouts: 26.5 us -> 17.7 us
  Pallas kernels: 134 us -> 126 us
  other arithmetic: 20.7 us -> 17.7 us
    pallas_call x2, Pallas kernels: 97.5 us -> 66 us  [_exchange(): pl.pallas_call(functools.partial(_exchange_kernel, n, axis), out_shape=ja...]
    pallas_call x1, Pallas kernels: 36.9 us -> 60.1 us  [_exchange_both(): pl.pallas_call(functools.partial(_both_kernel, n), out_shape=(jax.ShapeDt...]
    slice x5 -> x3, local copies, waits for them, and re-layouts: 4.62 us -> 1.54 us  [the longest x2 1.31 us: body(): got = recv[:, :capacity * half // lanes, :].reshape(slots_all, half)]
    concatenate x1, other arithmetic: 3.54 us -> 1.26 us  [body(): jnp.concatenate([send_tok.reshape(owners, capacity * half // lanes, lanes...]
    ppermute x2 -> x3, starting transfers between devices: 4.48 us -> 6.42 us  [_swap_pair(): return lax.ppermute(x, 'core', [(0, 1), (1, 0)])]
    unnamed x33 -> x39, local copies, waits for them, and re-layouts: 5.78 us -> 4.47 us
    reshape x2 -> x4, local copies, waits for them, and re-layouts: 6.24 us -> 5.11 us  [the longest x1 2.48 us: body(): got_cot = got_cot.reshape(slots_all, half)]
  transfers between devices with their start and end apart: 2 -> 3, of which waited for: 0 -> 1; matrix products, arithmetic and copies ran while one was open for 11% -> 8% of each run, Pallas kernels for 0% -> 11%
where the time goes in v10:
time: 186 us; the launch traced here: 184 us
  Pallas kernels  126 us (68%)
  local copies, waits for them, and re-layouts  17.7 us (10%)
  other arithmetic  17.7 us (10%)
  matrix products  13.9 us (7%)
  starting transfers between devices  6.42 us (3%)
    pallas_call x2, Pallas kernels, _exchange(): pl.pallas_call(functools.partial(_exchange_kernel, n, axis), out_shape=ja...  66 us
    pallas_call x1, Pallas kernels, _exchange_both(): pl.pallas_call(functools.partial(_both_kernel, n), out_shape=(jax.ShapeDt...  60.1 us
    ppermute x3, starting transfers between devices, _swap_pair(): return lax.ppermute(x, 'core', [(0, 1), (1, 0)])  6.42 us
    unnamed x39, local copies, waits for them, and re-layouts  4.47 us
  transfers between devices with their start and end apart: 3, of which 1 were waited for; matrix products, arithmetic and copies ran while one was open for 8% of the time, Pallas kernels for 11%

profile of v10, /device:TPU:6, one launch (start us, length us, event | category | flops | bytes accessed | tf_op | source)
XLA Modules:
  0.0 183.9 jit_solution(8088373198399575345)
XLA Ops:
  0.6 0.8 copy.47
  1.7 1.2 reduce-window.6
  3.5 0.7 fusion.33
  4.2 1.3 fusion.41
  5.5 0.6 fusion.42
  6.2 0.7 reduce_sum.117
  6.9 0.7 broadcast_divide_fusion
  8.1 0.7 multiply_add_fusion
  8.9 0.2 select_reduce_fusion.1
  9.6 1.4 fusion.34
  11.3 0.5 convolution_convert_fusion.5
  11.8 0.6 reshape.171
  12.4 1.3 pad_maximum_fusion.1.x_ref
  13.7 45.7 %shard_map.120 = bf16[64,96,128]{2,1,0:T(8,128)(2,1)} custom-call(bf16[64,96,128]{2,1,0:T(8,128)(2,1)} %pad_maximum_fusion.1.x_ref), custom_call_target="tpu_custom_call" | custom-call | tf_op jit(solution)/shard_map/pallas_call | solution.py:67
  59.4 1.3 slice-done
  60.7 0.6 reshape.173
  61.3 1.9 %collective-permute-start = (bf16[640,1024]{1,0:T(8,128)(2,1)S(1)}, bf16[640,1024]{1,0:T(8,128)(2,1)}, u32[]{:S(2)}, u32[]{:S(2)}) collective-permute-start(bf16[640,1024]{1,0:T(8,128)(2,1)S(1)} %reshape.173), channel_id=1, source_target_pairs={{0,1},{1,0},{2,3},{3,2},{4,5},{5,4},{6,7},{7,6},{8,9},{9,8},{10,11... | collective-permute-start | bytes 3932168 | tf_op jit(solution)/shard_map/ppermute | solution.py:242
  63.2 1.4 reshape_squeeze.3
  64.7 1.5 fusion.43
  66.2 1.3 copy.65
  67.5 0.4 copy.66
  68.0 1.6 broadcast_select_fusion.3
  69.6 0.9 convolution_bitcast_fusion.2
  70.6 0.4 copy-done.6
  71.0 0.7 copy-done.14
  71.8 1.6 multiply_convert_fusion.3
  73.4 1.6 fusion.4
  74.9 2.4 %collective-permute-start.1 = (bf16[4,640,256]{2,1,0:T(8,128)(2,1)}, bf16[4,640,256]{2,1,0:T(8,128)(2,1)}, u32[]{:S(2)}, u32[]{:S(2)}) collective-permute-start(bf16[4,640,256]{2,1,0:T(8,128)(2,1)} %fusion.4), channel_id=1, source_target_pairs={{0,1},{1,0},{2,3},{3,2},{4,5},{5,4},{6,7},{7,6},{8,9},{9,8},{10,11... | collective-permute-start | bytes 3932168 | tf_op jit(solution)/shard_map/ppermute | solution.py:242
  77.4 0.5 convolution_convert_fusion.6
  77.9 1.4 reshape.170.a_ref
  79.3 1.0 collective-permute-done.1
  80.3 2.9 %fusion.b_ref = bf16[4,640,256]{2,1,0:T(8,128)(2,1)} fusion(bf16[4,640,256]{2,1,0:T(8,128)(2,1)} %collective-permute-done.1, bf16[128,4,1,256]{0,3,1,2:T(8,128)(2,1)S(1)} %copy.65, bf16[128,4,1,256]{0,3,1,2:T(8,128)(2,1)S(1)} %copy-done.3, pred[]{:T(512)S(6)} %eq.72, bf16[128,640]{0,1:T(8,128)(2,1)S(1)} %get-tuple-element.25), kind=kOutput, calls=%fused_computation.3 | convolution fusion | flops 171180032 | bytes 3309569 | tf_op jit(solution)/shard_map/hr,hzb->zrb/dot_general | solution.py:339
  83.2 60.1 %shard_map.121 = (bf16[64,80,128]{2,1,0:T(8,128)(2,1)}, bf16[4,640,256]{2,1,0:T(8,128)(2,1)}) custom-call(bf16[64,80,128]{2,1,0:T(8,128)(2,1)} %reshape.170.a_ref, bf16[4,640,256]{2,1,0:T(8,128)(2,1)} %fusion.b_ref), custom_call_target="tpu_custom_call" | custom-call | tf_op jit(solution)/shard_map/pallas_call | solution.py:222
  143.4 2.5 %reshape.178 = bf16[640,1024]{1,0:T(8,128)(2,1)S(1)} reshape(bf16[64,80,128]{2,1,0:T(8,128)(2,1)} %get-tuple-element.7) | data formatting | bytes 2621440 | tf_op jit(solution)/shard_map/reshape | solution.py:343
  145.8 2.1 %collective-permute-start.2 = (bf16[640,1024]{1,0:T(8,128)(2,1)S(1)}, bf16[640,1024]{1,0:T(8,128)(2,1)}, u32[]{:S(2)}, u32[]{:S(2)}) collective-permute-start(bf16[640,1024]{1,0:T(8,128)(2,1)S(1)} %reshape.178), channel_id=1, source_target_pairs={{0,1},{1,0},{2,3},{3,2},{4,5},{5,4},{6,7},{7,6},{8,9},{9,8},{10,11... | collective-permute-start | bytes 3932168 | tf_op jit(solution)/shard_map/ppermute | solution.py:242
  148.3 0.7 slice_reduce_fusion.2
  149.0 1.8 fusion.13
  150.8 1.6 reduce_sum.125
  152.5 0.9 reshape.174.x_ref
  153.4 20.3 %shard_map.122 = bf16[64,20,128]{2,1,0:T(8,128)(2,1)} custom-call(bf16[64,20,128]{2,1,0:T(8,128)(2,1)} %reshape.174.x_ref), custom_call_target="tpu_custom_call" | custom-call | tf_op jit(solution)/shard_map/pallas_call | solution.py:67
  173.7 1.2 reshape.175
  174.9 0.5 fusion.7
  175.6 0.9 reduce_sum.126
  176.5 1.5 broadcast_select_fusion.1
  178.1 0.9 convolution_bitcast_fusion
  179.0 1.6 fusion.3
  180.9 1.4 fusion.2
  182.4 1.5 fusion.1
  (66 shorter events, 3.2 us)
Async XLA Ops:
  0.6 10.7 %copy-start = (bf16[128,2048]{1,0:T(8,128)(2,1)S(1)}, bf16[128,2048]{1,0:T(8,128)(2,1)}, u32[]{:S(2)}) copy-start(bf16[128,2048]{1,0:T(8,128)(2,1)} %param.9) | copy-start | bytes 1572868
  59.4 1.3 slice-start
  61.3 6.7 %collective-permute-start = (bf16[640,1024]{1,0:T(8,128)(2,1)S(1)}, bf16[640,1024]{1,0:T(8,128)(2,1)}, u32[]{:S(2)}, u32[]{:S(2)}) collective-permute-start(bf16[640,1024]{1,0:T(8,128)(2,1)S(1)} %reshape.173), channel_id=1, source_target_pairs={{0,1},{1,0},{2,3},{3,2},{4,5},{5,4},{6,7},{7,6},{8,9},{9,8},{10,11... | collective-permute-start | bytes 3932168 | tf_op jit(solution)/shard_map/ppermute | solution.py:242
  67.9 5.4 %copy-start.2 = (bf16[128,4,1,256]{0,3,1,2:T(8,128)(2,1)}, bf16[128,4,1,256]{0,3,1,2:T(8,128)(2,1)S(1)}, u32[]{:S(2)}) copy-start(bf16[128,4,1,256]{0,3,1,2:T(8,128)(2,1)S(1)} %copy.66) | copy-start | bytes 786436
  67.9 1.6 copy-start.12
  69.6 1.1 copy-start.4
  69.6 1.5 copy-start.6
  69.6 2.2 %copy-start.13 = (bf16[1,128,2048]{2,1,0:T(8,128)(2,1)S(1)}, bf16[1,128,2048]{2,1,0:T(8,128)(2,1)}, u32[]{:S(2)}) copy-start(bf16[1,128,2048]{2,1,0:T(8,128)(2,1)} %param.16) | copy-start | bytes 1572868
  71.0 0.7 copy-start.14
  73.4 7.0 %copy-start.8 = (bf16[128,640]{0,1:T(8,128)(2,1)}, bf16[128,640]{0,1:T(8,128)(2,1)S(1)}, u32[]{:S(2)}) copy-start(bf16[128,640]{0,1:T(8,128)(2,1)S(1)} %get-tuple-element.25) | copy-start | bytes 491524
  73.4 4.0 %copy-start.11 = (bf16[128,2048]{1,0:T(8,128)(2,1)S(1)}, bf16[128,2048]{1,0:T(8,128)(2,1)}, u32[]{:S(2)}) copy-start(bf16[128,2048]{1,0:T(8,128)(2,1)} %param.10) | copy-start | bytes 1572868
  74.9 5.4 %collective-permute-start.1 = (bf16[4,640,256]{2,1,0:T(8,128)(2,1)}, bf16[4,640,256]{2,1,0:T(8,128)(2,1)}, u32[]{:S(2)}, u32[]{:S(2)}) collective-permute-start(bf16[4,640,256]{2,1,0:T(8,128)(2,1)} %fusion.4), channel_id=1, source_target_pairs={{0,1},{1,0},{2,3},{3,2},{4,5},{5,4},{6,7},{7,6},{8,9},{9,8},{10,11... | collective-permute-start | bytes 3932168 | tf_op jit(solution)/shard_map/ppermute | solution.py:242
  77.9 2.5 %copy-start.3 = (bf16[128,4,1,256]{0,3,1,2:T(8,128)(2,1)S(1)}, bf16[128,4,1,256]{0,3,1,2:T(8,128)(2,1)}, u32[]{:S(2)}) copy-start(bf16[128,4,1,256]{0,3,1,2:T(8,128)(2,1)} %copy-done.2) | copy-start | bytes 786436
  143.3 4.6 %copy-start.1 = (bf16[64,96,128]{2,1,0:T(8,128)(2,1)S(1)}, bf16[64,96,128]{2,1,0:T(8,128)(2,1)}, u32[]{:S(2)}) copy-start(bf16[64,96,128]{2,1,0:T(8,128)(2,1)} %shard_map.120) | copy-start | bytes 4718596
  145.8 30.7 %collective-permute-start.2 = (bf16[640,1024]{1,0:T(8,128)(2,1)S(1)}, bf16[640,1024]{1,0:T(8,128)(2,1)}, u32[]{:S(2)}, u32[]{:S(2)}) collective-permute-start(bf16[640,1024]{1,0:T(8,128)(2,1)S(1)} %reshape.178), channel_id=1, source_target_pairs={{0,1},{1,0},{2,3},{3,2},{4,5},{5,4},{6,7},{7,6},{8,9},{9,8},{10,11... | collective-permute-start | bytes 3932168 | tf_op jit(solution)/shard_map/ppermute | solution.py:242
  176.5 1.6 copy-start.10
  178.1 0.9 copy-start.9
  179.0 1.6 copy-start.5
  179.0 1.7 copy-start.7
  179.0 1.9 %copy-start.15 = (f32[128,640]{0,1:T(8,128)S(1)}, f32[128,640]{0,1:T(8,128)}, u32[]{:S(2)}) copy-start(f32[128,640]{0,1:T(8,128)} %copy-done.14) | copy-start | bytes 983044
  180.9 1.4 copy-start.16

commit v11 on v10

--- a/solution.py
+++ b/solution.py
@@ -311,13 +311,7 @@
     pick = hit_tok.astype(tokens.dtype)
     send_tok = jnp.dot(pick, my_tokens, preferred_element_type=jnp.float32).astype(tokens.dtype)
     send_cot = jnp.dot(pick, my_cotan, preferred_element_type=jnp.float32).astype(tokens.dtype)
-    send = jnp.concatenate(
-        [send_tok.reshape(owners, capacity * half // lanes, lanes), meta.reshape(owners, features // lanes, lanes)],
-        axis=1,
-    )
-    recv = _exchange(send, 0)
-    got = recv[:, : capacity * half // lanes, :].reshape(slots_all, half)
-    got_meta = recv[:, capacity * half // lanes :, :].reshape(owners, features).astype(jnp.float32)
+    got = _exchange(send_tok.reshape(owners, capacity * half // lanes, lanes), 0).reshape(slots_all, half)
     other = _swap_pair(got)
     rows_in = jnp.concatenate(
         [jnp.where(is_first, got, other), jnp.where(is_first, other, got)], axis=1
@@ -339,8 +333,13 @@
     keep = jnp.einsum("hr,hzb->zrb", hidden, keep_w, preferred_element_type=jnp.float32).astype(jnp.bfloat16)
     give = jnp.einsum("hr,hzb->zrb", hidden, give_w, preferred_element_type=jnp.float32).astype(jnp.bfloat16)
     pair_sum = (keep.astype(jnp.float32) + _swap_pair(give).astype(jnp.float32)).astype(jnp.bfloat16)
-    got_cot, by_group = _exchange_both(send_cot.reshape(owners, capacity * half // lanes, lanes), pair_sum, 3)
-    got_cot = got_cot.reshape(slots_all, half)
+    send = jnp.concatenate(
+        [send_cot.reshape(owners, capacity * half // lanes, lanes), meta.reshape(owners, features // lanes, lanes)],
+        axis=1,
+    )
+    recv, by_group = _exchange_both(send, pair_sum, 3)
+    got_cot = recv[:, : capacity * half // lanes, :].reshape(slots_all, half)
+    got_meta = recv[:, capacity * half // lanes :, :].reshape(owners, features).astype(jnp.float32)
     other_cot = _swap_pair(got_cot)
     cot_in = jnp.concatenate(
         [jnp.where(is_first, got_cot, other_cot), jnp.where(is_first, other_cot, got_cot)], axis=1

time: 186 us -> 181 us (0.973)
  Pallas kernels: 126 us -> 123 us
    pallas_call x2, Pallas kernels: 66 us -> 60.7 us  [_exchange(): pl.pallas_call(functools.partial(_exchange_kernel, n, axis), out_shape=ja...]
    pallas_call x1, Pallas kernels: 60.1 us -> 62.7 us  [_exchange_both(): pl.pallas_call(functools.partial(_both_kernel, n), out_shape=(jax.ShapeDt...]
    unnamed x39 -> x45, local copies, waits for them, and re-layouts: 4.47 us -> 4.6 us
  transfers between devices with their start and end apart: 3 -> 3, of which waited for: 1 -> 0; matrix products, arithmetic and copies ran while one was open for 8% -> 12% of each run, Pallas kernels for 11% -> 12%
where the time goes in v11:
time: 181 us; the launch traced here: 179 us
  Pallas kernels  123 us (68%)
  other arithmetic  17 us (9%)
  local copies, waits for them, and re-layouts  16.8 us (9%)
  matrix products  13.9 us (8%)
  starting transfers between devices  6.55 us (4%)
    pallas_call x1, Pallas kernels, _exchange_both(): pl.pallas_call(functools.partial(_both_kernel, n), out_shape=(jax.ShapeDt...  62.7 us
    pallas_call x2, Pallas kernels, _exchange(): pl.pallas_call(functools.partial(_exchange_kernel, n, axis), out_shape=ja...  60.7 us
    ppermute x3, starting transfers between devices, _swap_pair(): return lax.ppermute(x, 'core', [(0, 1), (1, 0)])  6.55 us
    unnamed x45, local copies, waits for them, and re-layouts  4.6 us
  transfers between devices with their start and end apart: 3, of which 0 were waited for; matrix products, arithmetic and copies ran while one was open for 12% of the time, Pallas kernels for 12%

profile of v11, /device:TPU:6, one launch (start us, length us, event | category | flops | bytes accessed | tf_op | source)
XLA Modules:
  0.0 178.8 jit_solution(15507023157226952749)
XLA Ops:
  0.6 0.8 copy.47
  1.7 1.2 reduce-window.6
  2.9 0.2 slice_reduce_fusion
  3.5 0.7 multiply_add_fusion
  4.4 0.5 convolution_convert_fusion.5
  4.9 1.4 reshape.172.x_ref
  6.4 40.1 %shard_map.120 = bf16[64,80,128]{2,1,0:T(8,128)(2,1)} custom-call(bf16[64,80,128]{2,1,0:T(8,128)(2,1)} %reshape.172.x_ref), custom_call_target="tpu_custom_call" | custom-call | tf_op jit(solution)/shard_map/pallas_call | solution.py:67
  46.5 2.4 %reshape.173 = bf16[640,1024]{1,0:T(8,128)(2,1)S(1)} reshape(bf16[64,80,128]{2,1,0:T(8,128)(2,1)} %shard_map.120) | data formatting | bytes 2621440 | tf_op jit(solution)/shard_map/reshape | solution.py:314
  48.9 1.9 %collective-permute-start = (bf16[640,1024]{1,0:T(8,128)(2,1)S(1)}, bf16[640,1024]{1,0:T(8,128)(2,1)}, u32[]{:S(2)}, u32[]{:S(2)}) collective-permute-start(bf16[640,1024]{1,0:T(8,128)(2,1)S(1)} %reshape.173), channel_id=1, source_target_pairs={{0,1},{1,0},{2,3},{3,2},{4,5},{5,4},{6,7},{7,6},{8,9},{9,8},{10,11... | collective-permute-start | bytes 3932168 | tf_op jit(solution)/shard_map/ppermute | solution.py:242
  51.1 0.4 reshape_squeeze.3
  51.5 1.5 fusion.43
  53.0 1.3 copy.65
  54.4 0.4 copy.66
  54.9 0.6 fusion.41
  55.6 0.6 fusion.42
  56.2 1.5 broadcast_select_fusion.3
  57.8 0.8 convolution_bitcast_fusion.2
  58.9 0.4 copy-done.5
  59.3 1.6 multiply_convert_fusion.3
  60.9 1.6 fusion.4
  62.5 2.5 %collective-permute-start.1 = (bf16[4,640,256]{2,1,0:T(8,128)(2,1)}, bf16[4,640,256]{2,1,0:T(8,128)(2,1)}, u32[]{:S(2)}, u32[]{:S(2)}) collective-permute-start(bf16[4,640,256]{2,1,0:T(8,128)(2,1)} %fusion.4), channel_id=1, source_target_pairs={{0,1},{1,0},{2,3},{3,2},{4,5},{5,4},{6,7},{7,6},{8,9},{9,8},{10,11... | collective-permute-start | bytes 3932168 | tf_op jit(solution)/shard_map/ppermute | solution.py:242
  65.0 0.2 select_reduce_fusion.1
  66.0 1.4 fusion.34
  67.4 0.2 concatenate.17
  67.6 0.8 copy.68
  68.4 0.5 convolution_convert_fusion.6
  68.9 0.6 reshape.170
  69.5 2.3 %pad_maximum_fusion.1.a_ref = bf16[64,96,128]{2,1,0:T(8,128)(2,1)} fusion(bf16[64,16,128]{2,1,0:T(8,128)(2,1)} %bitcast.73, bf16[64,80,128]{2,1,0:T(8,128)(2,1)S(1)} %reshape.170), kind=kLoop, calls=%fused_computation.14 | loop fusion | flops 3145728 | bytes 3145728 | tf_op jit(solution)/shard_map/concatenate | solution.py:336
  71.8 2.9 %fusion.b_ref = bf16[4,640,256]{2,1,0:T(8,128)(2,1)} fusion(bf16[4,640,256]{2,1,0:T(8,128)(2,1)} %collective-permute-done.1, bf16[128,4,1,256]{0,3,1,2:T(8,128)(2,1)S(1)} %copy.65, bf16[128,4,1,256]{0,3,1,2:T(8,128)(2,1)S(1)} %copy-done.2, pred[]{:T(512)S(6)} %eq.75, bf16[128,640]{0,1:T(8,128)(2,1)S(1)} %copy-done.8), kind=kOutput, calls=%fused_computation.3 | convolution fusion | flops 171180032 | bytes 3309569 | tf_op jit(solution)/shard_map/hr,hzb->zrb/dot_general | solution.py:333
  74.7 62.7 %shard_map.121 = (bf16[64,96,128]{2,1,0:T(8,128)(2,1)}, bf16[4,640,256]{2,1,0:T(8,128)(2,1)}) custom-call(bf16[64,96,128]{2,1,0:T(8,128)(2,1)} %pad_maximum_fusion.1.a_ref, bf16[4,640,256]{2,1,0:T(8,128)(2,1)} %fusion.b_ref), custom_call_target="tpu_custom_call" | custom-call | tf_op jit(solution)/shard_map/pallas_call | solution.py:222
  137.4 1.4 slice.57
  138.8 0.6 reshape.178
  139.4 2.1 %collective-permute-start.2 = (bf16[640,1024]{1,0:T(8,128)(2,1)S(1)}, bf16[640,1024]{1,0:T(8,128)(2,1)}, u32[]{:S(2)}, u32[]{:S(2)}) collective-permute-start(bf16[640,1024]{1,0:T(8,128)(2,1)S(1)} %reshape.178), channel_id=1, source_target_pairs={{0,1},{1,0},{2,3},{3,2},{4,5},{5,4},{6,7},{7,6},{8,9},{9,8},{10,11... | collective-permute-start | bytes 3932168 | tf_op jit(solution)/shard_map/ppermute | solution.py:242
  141.5 1.6 reduce_sum.125
  143.2 0.9 reshape.174.x_ref
  144.1 20.6 %shard_map.122 = bf16[64,20,128]{2,1,0:T(8,128)(2,1)} custom-call(bf16[64,20,128]{2,1,0:T(8,128)(2,1)} %reshape.174.x_ref), custom_call_target="tpu_custom_call" | custom-call | tf_op jit(solution)/shard_map/pallas_call | solution.py:67
  164.7 1.2 reshape.175
  165.9 0.5 fusion.7
  166.6 0.9 reduce_sum.126
  167.5 1.0 slice_convert_fusion
  168.8 0.7 slice_reduce_fusion.2
  169.6 1.8 %fusion.13 = f32[640]{0:T(1024)S(1)} fusion(f32[640,5]{1,0:T(8,128)S(1)} %reshape.177, f32[]{:T(128)} %get-tuple-element.9, f32[]{:T(128)} %get-tuple-element.8), kind=kLoop, calls=%fused_computation.36 | loop fusion | flops 4480 | bytes 15368 | tf_op jit(solution)/shard_map/mul | solution.py:354
  171.4 1.5 broadcast_select_fusion.1
  172.9 0.9 convolution_bitcast_fusion
  173.9 1.6 fusion.3
  175.6 0.2 copy-done.18
  175.8 1.4 fusion.2
  177.3 1.5 fusion.1
  (71 shorter events, 2.6 us)
Async XLA Ops:
  0.6 3.8 %copy-start = (bf16[128,2048]{1,0:T(8,128)(2,1)S(1)}, bf16[128,2048]{1,0:T(8,128)(2,1)}, u32[]{:S(2)}) copy-start(bf16[128,2048]{1,0:T(8,128)(2,1)} %param.9) | copy-start | bytes 1572868
  46.5 4.4 %copy-start.12 = (f32[128,4]{0,1:T(4,128)S(1)}, f32[128,4]{0,1:T(4,128)}, u32[]{:S(2)}) copy-start(f32[128,4]{0,1:T(4,128)} %param.12) | copy-start | bytes 6148
  46.5 4.6 %copy-start.9 = (bf16[1,128,2048]{2,1,0:T(8,128)(2,1)S(1)}, bf16[1,128,2048]{2,1,0:T(8,128)(2,1)}, u32[]{:S(2)}) copy-start(bf16[1,128,2048]{2,1,0:T(8,128)(2,1)} %param.17) | copy-start | bytes 1572868
  48.9 7.3 %collective-permute-start = (bf16[640,1024]{1,0:T(8,128)(2,1)S(1)}, bf16[640,1024]{1,0:T(8,128)(2,1)}, u32[]{:S(2)}, u32[]{:S(2)}) collective-permute-start(bf16[640,1024]{1,0:T(8,128)(2,1)S(1)} %reshape.173), channel_id=1, source_target_pairs={{0,1},{1,0},{2,3},{3,2},{4,5},{5,4},{6,7},{7,6},{8,9},{9,8},{10,11... | collective-permute-start | bytes 3932168 | tf_op jit(solution)/shard_map/ppermute | solution.py:242
  53.0 1.8 %copy-start.16 = (s32[2]{0:T(128)S(1)}, s32[2]{0:T(128)}, u32[]{:S(2)}) copy-start(s32[2]{0:T(128)} %param.14) | copy-start | bytes 28
  53.0 1.9 %copy-start.13 = (s32[128]{0:T(128)S(1)}, s32[128]{0:T(128)}, u32[]{:S(2)}) copy-start(s32[128]{0:T(128)} %param.13) | copy-start | bytes 1540
  54.8 6.1 %copy-start.1 = (bf16[128,4,1,256]{0,3,1,2:T(8,128)(2,1)}, bf16[128,4,1,256]{0,3,1,2:T(8,128)(2,1)S(1)}, u32[]{:S(2)}) copy-start(bf16[128,4,1,256]{0,3,1,2:T(8,128)(2,1)S(1)} %copy.66) | copy-start | bytes 786436
  56.2 1.6 copy-start.14
  57.8 1.1 copy-start.3
  57.8 1.5 copy-start.5
  57.8 1.5 copy-start.15
  59.3 1.6 copy-start.17
  60.9 6.4 %copy-start.7 = (bf16[128,640]{0,1:T(8,128)(2,1)}, bf16[128,640]{0,1:T(8,128)(2,1)S(1)}, u32[]{:S(2)}) copy-start(bf16[128,640]{0,1:T(8,128)(2,1)S(1)} %get-tuple-element.25) | copy-start | bytes 491524
  62.5 5.9 %copy-start.11 = (bf16[128,2048]{1,0:T(8,128)(2,1)S(1)}, bf16[128,2048]{1,0:T(8,128)(2,1)}, u32[]{:S(2)}) copy-start(bf16[128,2048]{1,0:T(8,128)(2,1)} %param.10) | copy-start | bytes 1572868
  62.5 9.3 %collective-permute-start.1 = (bf16[4,640,256]{2,1,0:T(8,128)(2,1)}, bf16[4,640,256]{2,1,0:T(8,128)(2,1)}, u32[]{:S(2)}, u32[]{:S(2)}) collective-permute-start(bf16[4,640,256]{2,1,0:T(8,128)(2,1)} %fusion.4), channel_id=1, source_target_pairs={{0,1},{1,0},{2,3},{3,2},{4,5},{5,4},{6,7},{7,6},{8,9},{9,8},{10,11... | collective-permute-start | bytes 3932168 | tf_op jit(solution)/shard_map/ppermute | solution.py:242
  69.5 2.3 %copy-start.2 = (bf16[128,4,1,256]{0,3,1,2:T(8,128)(2,1)S(1)}, bf16[128,4,1,256]{0,3,1,2:T(8,128)(2,1)}, u32[]{:S(2)}) copy-start(bf16[128,4,1,256]{0,3,1,2:T(8,128)(2,1)} %copy-done.1) | copy-start | bytes 786436
  69.5 2.3 %copy-start.8 = (bf16[128,640]{0,1:T(8,128)(2,1)S(1)}, bf16[128,640]{0,1:T(8,128)(2,1)}, u32[]{:S(2)}) copy-start(bf16[128,640]{0,1:T(8,128)(2,1)} %copy-done.7) | copy-start | bytes 491524
  139.4 31.9 %collective-permute-start.2 = (bf16[640,1024]{1,0:T(8,128)(2,1)S(1)}, bf16[640,1024]{1,0:T(8,128)(2,1)}, u32[]{:S(2)}, u32[]{:S(2)}) collective-permute-start(bf16[640,1024]{1,0:T(8,128)(2,1)S(1)} %reshape.178), channel_id=1, source_target_pairs={{0,1},{1,0},{2,3},{3,2},{4,5},{5,4},{6,7},{7,6},{8,9},{9,8},{10,11... | collective-permute-start | bytes 3932168 | tf_op jit(solution)/shard_map/ppermute | solution.py:242
  171.4 1.6 copy-start.10
  173.9 1.6 copy-start.4
  173.9 1.7 copy-start.6
  173.9 1.9 %copy-start.18 = (f32[128,640]{0,1:T(8,128)S(1)}, f32[128,640]{0,1:T(8,128)}, u32[]{:S(2)}) copy-start(f32[128,640]{0,1:T(8,128)} %copy-done.17) | copy-start | bytes 983044
  175.8 1.4 copy-start.19

commit v12 on v11

--- a/solution.py
+++ b/solution.py
@@ -353,7 +353,9 @@
     )
     routed = ((coefficient * got_share)[:, None] * cot_in.astype(jnp.float32)).astype(jnp.bfloat16)
     slice_sum = jnp.sum(by_group.astype(jnp.float32), axis=0).astype(jnp.bfloat16)
-    returned = _exchange(slice_sum.reshape(owners, capacity * block // lanes, lanes), 1)
+    returned = lax.all_to_all(
+        slice_sum.reshape(owners, capacity, block), "dp", split_axis=0, concat_axis=0, tiled=True
+    )
     picked = jnp.dot(
         hit.T.astype(returned.dtype),
         returned.reshape(slots_all, block),

time: 181 us -> 178 us (0.983)
  Pallas kernels: 123 us -> 103 us
  waiting for transfers between devices: 0.01 us -> 13 us
  starting transfers between devices: 6.55 us -> 13.7 us
    pallas_call x2 -> x1, Pallas kernels: 60.7 us -> 40.1 us  [_exchange(): pl.pallas_call(functools.partial(_exchange_kernel, n, axis), out_shape=ja...]
    all_to_all x0 -> x1, waiting for transfers between devices: none -> 13 us  [body(): lax.all_to_all(slice_sum.reshape(owners, capacity, block), 'dp', split_ax...]
    all_to_all x0 -> x1, starting transfers between devices: none -> 7.28 us  [body(): lax.all_to_all(slice_sum.reshape(owners, capacity, block), 'dp', split_ax...]
  transfers between devices with their start and end apart: 3 -> 4, of which waited for: 0 -> 1; matrix products, arithmetic and copies ran while one was open for 12% -> 11% of each run, Pallas kernels for 12% -> 0%
where the time goes in v12:
time: 178 us; the launch traced here: 177 us
  Pallas kernels  103 us (58%)
  other arithmetic  17.1 us (10%)
  local copies, waits for them, and re-layouts  15.8 us (9%)
  matrix products  13.9 us (8%)
  starting transfers between devices  13.7 us (8%)
  waiting for transfers between devices  13 us (7%)
    pallas_call x1, Pallas kernels, _exchange_both(): pl.pallas_call(functools.partial(_both_kernel, n), out_shape=(jax.ShapeDt...  62.7 us
    pallas_call x1, Pallas kernels, _exchange(): pl.pallas_call(functools.partial(_exchange_kernel, n, axis), out_shape=ja...  40.1 us
    all_to_all x1, waiting for transfers between devices, body(): lax.all_to_all(slice_sum.reshape(owners, capacity, block), 'dp', split_ax...  13 us
    all_to_all x1, starting transfers between devices, body(): lax.all_to_all(slice_sum.reshape(owners, capacity, block), 'dp', split_ax...  7.28 us
    ppermute x3, starting transfers between devices, _swap_pair(): return lax.ppermute(x, 'core', [(0, 1), (1, 0)])  6.37 us
    unnamed x45, local copies, waits for them, and re-layouts  4.6 us
  transfers between devices with their start and end apart: 4, of which 1 were waited for; matrix products, arithmetic and copies ran while one was open for 11% of the time, Pallas kernels for 0%

profile of v12, /device:TPU:6, one launch (start us, length us, event | category | flops | bytes accessed | tf_op | source)
XLA Modules:
  0.0 177.3 jit_solution(14003821329449451773)
XLA Ops:
  0.6 0.8 copy.47
  1.7 1.2 reduce-window.6
  2.9 0.2 slice_reduce_fusion
  3.5 0.7 multiply_add_fusion
  4.4 0.5 convolution_convert_fusion.5
  4.9 1.4 reshape.172.x_ref
  6.4 40.1 %shard_map.120 = bf16[64,80,128]{2,1,0:T(8,128)(2,1)} custom-call(bf16[64,80,128]{2,1,0:T(8,128)(2,1)} %reshape.172.x_ref), custom_call_target="tpu_custom_call" | custom-call | tf_op jit(solution)/shard_map/pallas_call | solution.py:67
  46.5 2.4 %reshape.173 = bf16[640,1024]{1,0:T(8,128)(2,1)S(1)} reshape(bf16[64,80,128]{2,1,0:T(8,128)(2,1)} %shard_map.120) | data formatting | bytes 2621440 | tf_op jit(solution)/shard_map/reshape | solution.py:314
  48.9 1.9 %collective-permute-start = (bf16[640,1024]{1,0:T(8,128)(2,1)S(1)}, bf16[640,1024]{1,0:T(8,128)(2,1)}, u32[]{:S(2)}, u32[]{:S(2)}) collective-permute-start(bf16[640,1024]{1,0:T(8,128)(2,1)S(1)} %reshape.173), channel_id=1, source_target_pairs={{0,1},{1,0},{2,3},{3,2},{4,5},{5,4},{6,7},{7,6},{8,9},{9,8},{10,11... | collective-permute-start | bytes 3932168 | tf_op jit(solution)/shard_map/ppermute | solution.py:242
  51.1 0.4 reshape_squeeze.3
  51.5 1.5 fusion.43
  53.0 1.3 copy.65
  54.4 0.4 copy.66
  54.9 0.6 fusion.41
  55.6 0.6 fusion.42
  56.2 1.5 broadcast_select_fusion.3
  57.8 0.8 convolution_bitcast_fusion.2
  58.9 0.4 copy-done.5
  59.3 1.6 multiply_convert_fusion.3
  60.9 1.6 fusion.4
  62.5 2.5 %collective-permute-start.1 = (bf16[4,640,256]{2,1,0:T(8,128)(2,1)}, bf16[4,640,256]{2,1,0:T(8,128)(2,1)}, u32[]{:S(2)}, u32[]{:S(2)}) collective-permute-start(bf16[4,640,256]{2,1,0:T(8,128)(2,1)} %fusion.4), channel_id=1, source_target_pairs={{0,1},{1,0},{2,3},{3,2},{4,5},{5,4},{6,7},{7,6},{8,9},{9,8},{10,11... | collective-permute-start | bytes 3932168 | tf_op jit(solution)/shard_map/ppermute | solution.py:242
  65.0 0.2 select_reduce_fusion.1
  66.0 1.4 fusion.34
  67.4 0.2 concatenate.17
  67.6 0.8 copy.68
  68.4 0.5 convolution_convert_fusion.6
  68.9 0.6 reshape.170
  69.5 2.3 %pad_maximum_fusion.1.a_ref = bf16[64,96,128]{2,1,0:T(8,128)(2,1)} fusion(bf16[64,16,128]{2,1,0:T(8,128)(2,1)} %bitcast.73, bf16[64,80,128]{2,1,0:T(8,128)(2,1)S(1)} %reshape.170), kind=kLoop, calls=%fused_computation.14 | loop fusion | flops 3145728 | bytes 3145728 | tf_op jit(solution)/shard_map/concatenate | solution.py:336
  71.8 2.9 %fusion.b_ref = bf16[4,640,256]{2,1,0:T(8,128)(2,1)} fusion(bf16[4,640,256]{2,1,0:T(8,128)(2,1)} %collective-permute-done.1, bf16[128,4,1,256]{0,3,1,2:T(8,128)(2,1)S(1)} %copy.65, bf16[128,4,1,256]{0,3,1,2:T(8,128)(2,1)S(1)} %copy-done.2, pred[]{:T(512)S(6)} %eq.75, bf16[128,640]{0,1:T(8,128)(2,1)S(1)} %copy-done.8), kind=kOutput, calls=%fused_computation.3 | convolution fusion | flops 171180032 | bytes 3309569 | tf_op jit(solution)/shard_map/hr,hzb->zrb/dot_general | solution.py:333
  74.7 62.7 %shard_map.121 = (bf16[64,96,128]{2,1,0:T(8,128)(2,1)}, bf16[4,640,256]{2,1,0:T(8,128)(2,1)}) custom-call(bf16[64,96,128]{2,1,0:T(8,128)(2,1)} %pad_maximum_fusion.1.a_ref, bf16[4,640,256]{2,1,0:T(8,128)(2,1)} %fusion.b_ref), custom_call_target="tpu_custom_call" | custom-call | tf_op jit(solution)/shard_map/pallas_call | solution.py:222
  137.4 1.4 slice.57
  138.8 0.6 reshape.178
  139.4 1.9 %collective-permute-start.2 = (bf16[640,1024]{1,0:T(8,128)(2,1)S(1)}, bf16[640,1024]{1,0:T(8,128)(2,1)}, u32[]{:S(2)}, u32[]{:S(2)}) collective-permute-start(bf16[640,1024]{1,0:T(8,128)(2,1)S(1)} %reshape.178), channel_id=1, source_target_pairs={{0,1},{1,0},{2,3},{3,2},{4,5},{5,4},{6,7},{7,6},{8,9},{9,8},{10,11... | collective-permute-start | bytes 3932168 | tf_op jit(solution)/shard_map/ppermute | solution.py:242
  141.4 1.6 reduce_sum.125
  143.0 0.9 reshape.174
  143.9 7.3 %all-to-all-start = ((bf16[64,10,256]{2,1,0:T(8,128)(2,1)}), bf16[64,10,256]{2,1,0:T(8,128)(2,1)S(1)}, u32[]{:S(2)}, u32[]{:S(2)}) async-start(bf16[64,10,256]{2,1,0:T(8,128)(2,1)} %reshape.174), calls=%async_computation | async-start | bytes 1048576 | tf_op jit(solution)/shard_map/all_to_all | solution.py:356
  151.2 1.0 slice_convert_fusion
  152.5 0.8 slice_reduce_fusion.2
  153.3 1.9 %fusion.13 = f32[640]{0:T(1024)S(1)} fusion(f32[640,5]{1,0:T(8,128)S(1)} %reshape.177, f32[]{:T(128)} %get-tuple-element.9, f32[]{:T(128)} %get-tuple-element.8), kind=kLoop, calls=%fused_computation.36 | loop fusion | flops 4480 | bytes 15368 | tf_op jit(solution)/shard_map/mul | solution.py:354
  155.2 13.0 %all-to-all-done = bf16[64,10,256]{2,1,0:T(8,128)(2,1)S(1)} async-done(((bf16[64,10,256]{2,1,0:T(8,128)(2,1)}), bf16[64,10,256]{2,1,0:T(8,128)(2,1)S(1)}, u32[]{:S(2)}, u32[]{:S(2)}) %all-to-all-start) | async-done | bytes 327712 | tf_op jit(solution)/shard_map/all_to_all | solution.py:356
  168.3 0.5 fusion.7
  169.0 0.9 reduce_sum.126
  169.9 1.5 broadcast_select_fusion.1
  171.5 0.9 convolution_bitcast_fusion
  172.5 1.6 fusion.3
  174.1 0.2 copy-done.18
  174.4 1.4 fusion.2
  175.8 1.5 fusion.1
  (72 shorter events, 2.7 us)
Async XLA Ops:
  0.6 3.8 %copy-start = (bf16[128,2048]{1,0:T(8,128)(2,1)S(1)}, bf16[128,2048]{1,0:T(8,128)(2,1)}, u32[]{:S(2)}) copy-start(bf16[128,2048]{1,0:T(8,128)(2,1)} %param.9) | copy-start | bytes 1572868
  46.5 4.4 %copy-start.12 = (f32[128,4]{0,1:T(4,128)S(1)}, f32[128,4]{0,1:T(4,128)}, u32[]{:S(2)}) copy-start(f32[128,4]{0,1:T(4,128)} %param.12) | copy-start | bytes 6148
  46.5 4.6 %copy-start.9 = (bf16[1,128,2048]{2,1,0:T(8,128)(2,1)S(1)}, bf16[1,128,2048]{2,1,0:T(8,128)(2,1)}, u32[]{:S(2)}) copy-start(bf16[1,128,2048]{2,1,0:T(8,128)(2,1)} %param.17) | copy-start | bytes 1572868
  48.9 7.3 %collective-permute-start = (bf16[640,1024]{1,0:T(8,128)(2,1)S(1)}, bf16[640,1024]{1,0:T(8,128)(2,1)}, u32[]{:S(2)}, u32[]{:S(2)}) collective-permute-start(bf16[640,1024]{1,0:T(8,128)(2,1)S(1)} %reshape.173), channel_id=1, source_target_pairs={{0,1},{1,0},{2,3},{3,2},{4,5},{5,4},{6,7},{7,6},{8,9},{9,8},{10,11... | collective-permute-start | bytes 3932168 | tf_op jit(solution)/shard_map/ppermute | solution.py:242
  53.0 1.8 %copy-start.16 = (s32[2]{0:T(128)S(1)}, s32[2]{0:T(128)}, u32[]{:S(2)}) copy-start(s32[2]{0:T(128)} %param.14) | copy-start | bytes 28
  53.0 1.9 %copy-start.13 = (s32[128]{0:T(128)S(1)}, s32[128]{0:T(128)}, u32[]{:S(2)}) copy-start(s32[128]{0:T(128)} %param.13) | copy-start | bytes 1540
  54.8 6.1 %copy-start.1 = (bf16[128,4,1,256]{0,3,1,2:T(8,128)(2,1)}, bf16[128,4,1,256]{0,3,1,2:T(8,128)(2,1)S(1)}, u32[]{:S(2)}) copy-start(bf16[128,4,1,256]{0,3,1,2:T(8,128)(2,1)S(1)} %copy.66) | copy-start | bytes 786436
  56.2 1.6 copy-start.14
  57.8 1.1 copy-start.3
  57.8 1.5 copy-start.5
  57.8 1.5 copy-start.15
  59.3 1.6 copy-start.17
  60.9 6.4 %copy-start.7 = (bf16[128,640]{0,1:T(8,128)(2,1)}, bf16[128,640]{0,1:T(8,128)(2,1)S(1)}, u32[]{:S(2)}) copy-start(bf16[128,640]{0,1:T(8,128)(2,1)S(1)} %get-tuple-element.25) | copy-start | bytes 491524
  62.5 5.9 %copy-start.11 = (bf16[128,2048]{1,0:T(8,128)(2,1)S(1)}, bf16[128,2048]{1,0:T(8,128)(2,1)}, u32[]{:S(2)}) copy-start(bf16[128,2048]{1,0:T(8,128)(2,1)} %param.10) | copy-start | bytes 1572868
  62.5 9.3 %collective-permute-start.1 = (bf16[4,640,256]{2,1,0:T(8,128)(2,1)}, bf16[4,640,256]{2,1,0:T(8,128)(2,1)}, u32[]{:S(2)}, u32[]{:S(2)}) collective-permute-start(bf16[4,640,256]{2,1,0:T(8,128)(2,1)} %fusion.4), channel_id=1, source_target_pairs={{0,1},{1,0},{2,3},{3,2},{4,5},{5,4},{6,7},{7,6},{8,9},{9,8},{10,11... | collective-permute-start | bytes 3932168 | tf_op jit(solution)/shard_map/ppermute | solution.py:242
  69.5 2.3 %copy-start.2 = (bf16[128,4,1,256]{0,3,1,2:T(8,128)(2,1)S(1)}, bf16[128,4,1,256]{0,3,1,2:T(8,128)(2,1)}, u32[]{:S(2)}) copy-start(bf16[128,4,1,256]{0,3,1,2:T(8,128)(2,1)} %copy-done.1) | copy-start | bytes 786436
  69.5 2.3 %copy-start.8 = (bf16[128,640]{0,1:T(8,128)(2,1)S(1)}, bf16[128,640]{0,1:T(8,128)(2,1)}, u32[]{:S(2)}) copy-start(bf16[128,640]{0,1:T(8,128)(2,1)} %copy-done.7) | copy-start | bytes 491524
  139.4 30.5 %collective-permute-start.2 = (bf16[640,1024]{1,0:T(8,128)(2,1)S(1)}, bf16[640,1024]{1,0:T(8,128)(2,1)}, u32[]{:S(2)}, u32[]{:S(2)}) collective-permute-start(bf16[640,1024]{1,0:T(8,128)(2,1)S(1)} %reshape.178), channel_id=1, source_target_pairs={{0,1},{1,0},{2,3},{3,2},{4,5},{5,4},{6,7},{7,6},{8,9},{9,8},{10,11... | collective-permute-start | bytes 3932168 | tf_op jit(solution)/shard_map/ppermute | solution.py:242
  143.9 24.2 %all-to-all-start = ((bf16[64,10,256]{2,1,0:T(8,128)(2,1)}), bf16[64,10,256]{2,1,0:T(8,128)(2,1)S(1)}, u32[]{:S(2)}, u32[]{:S(2)}) async-start(bf16[64,10,256]{2,1,0:T(8,128)(2,1)} %reshape.174), calls=%async_computation | async-start | bytes 1048576 | tf_op jit(solution)/shard_map/all_to_all | solution.py:356
  169.9 1.6 copy-start.10
  172.4 1.6 copy-start.4
  172.4 1.7 copy-start.6
  172.4 1.9 %copy-start.18 = (f32[128,640]{0,1:T(8,128)S(1)}, f32[128,640]{0,1:T(8,128)}, u32[]{:S(2)}) copy-start(f32[128,640]{0,1:T(8,128)} %copy-done.17) | copy-start | bytes 983044
  174.4 1.4 copy-start.19

commit v13 on v12

--- a/solution.py
+++ b/solution.py
@@ -139,7 +139,7 @@
     )(x)
 
 
-def _both_kernel(n, a_ref, b_ref, ya_ref, yb_ref, a_send, a_recv, a_own, relay_up, relay_down, b_send, b_recv, b_own):
+def _both_kernel(n, a_ref, b_ref, ya_ref, yb_ref, yp_ref, a_send, a_recv, a_own, relay_up, relay_down, b_send, b_recv, b_own, p_sem):
     me = lax.axis_index("dp")
     at = lax.axis_index("zh")
     up, down, across = lax.rem(at + 1, 4), lax.rem(at + 3, 4), lax.rem(at + 2, 4)
@@ -174,7 +174,9 @@
     lax.fori_loop(1, n, greet, 0)
     for peer in (up, down):
         pl.semaphore_signal(barrier, inc=1, device_id={"zh": peer}, device_id_type=MESH)
-    pl.semaphore_wait(barrier, n + 1)
+    partner = 1 - lax.axis_index("core")
+    pl.semaphore_signal(barrier, inc=1, device_id={"core": partner}, device_id_type=MESH)
+    pl.semaphore_wait(barrier, n + 2)
 
     own_a = pltpu.make_async_copy(a_ref.at[me], ya_ref.at[me], a_own)
     own_a.start()
@@ -208,12 +210,22 @@
         return carry
 
     lax.fori_loop(1, n, finish, 0)
+    own_a.wait()
+    to_partner = pltpu.make_async_remote_copy(
+        src_ref=ya_ref,
+        dst_ref=yp_ref,
+        send_sem=p_sem.at[0],
+        recv_sem=p_sem.at[1],
+        device_id={"core": partner},
+        device_id_type=MESH,
+    )
+    to_partner.start()
     for copy in (to_up, to_down, lift, drop, pass_up, pass_down):
         copy.wait_send()
     for copy in (to_up, to_down, pass_up, pass_down):
         copy.wait_recv()
-    own_a.wait()
     own_b.wait()
+    to_partner.wait()
 
 
 def _exchange_both(a, b, collective_id):
@@ -221,9 +233,13 @@
     rows = b.shape[1] // 2
     return pl.pallas_call(
         functools.partial(_both_kernel, n),
-        out_shape=(jax.ShapeDtypeStruct(a.shape, a.dtype), jax.ShapeDtypeStruct(b.shape, b.dtype)),
+        out_shape=(
+            jax.ShapeDtypeStruct(a.shape, a.dtype),
+            jax.ShapeDtypeStruct(b.shape, b.dtype),
+            jax.ShapeDtypeStruct(a.shape, a.dtype),
+        ),
         in_specs=[pl.BlockSpec(memory_space=pl.ANY)] * 2,
-        out_specs=(pl.BlockSpec(memory_space=pl.ANY), pl.BlockSpec(memory_space=pl.ANY)),
+        out_specs=(pl.BlockSpec(memory_space=pl.ANY),) * 3,
         scratch_shapes=[
             pltpu.SemaphoreType.DMA((n,)),
             pltpu.SemaphoreType.DMA((n,)),
@@ -233,6 +249,7 @@
             pltpu.SemaphoreType.DMA((6,)),
             pltpu.SemaphoreType.DMA((6,)),
             pltpu.SemaphoreType.DMA(()),
+            pltpu.SemaphoreType.DMA((2,)),
         ],
         compiler_params=pltpu.CompilerParams(collective_id=collective_id, has_side_effects=True),
     )(a, b)
@@ -337,10 +354,10 @@
         [send_cot.reshape(owners, capacity * half // lanes, lanes), meta.reshape(owners, features // lanes, lanes)],
         axis=1,
     )
-    recv, by_group = _exchange_both(send, pair_sum, 3)
+    recv, by_group, recv_other = _exchange_both(send, pair_sum, 3)
     got_cot = recv[:, : capacity * half // lanes, :].reshape(slots_all, half)
     got_meta = recv[:, capacity * half // lanes :, :].reshape(owners, features).astype(jnp.float32)
-    other_cot = _swap_pair(got_cot)
+    other_cot = recv_other[:, : capacity * half // lanes, :].reshape(slots_all, half)
     cot_in = jnp.concatenate(
         [jnp.where(is_first, got_cot, other_cot), jnp.where(is_first, other_cot, got_cot)], axis=1
     )

time: 178 us -> 168 us (0.944)
  waiting for transfers between devices: 13 us -> 2.75 us
  starting transfers between devices: 13.7 us -> 11.8 us
  local copies, waits for them, and re-layouts: 15.8 us -> 17.6 us
    all_to_all x1, waiting for transfers between devices: 13 us -> 2.75 us  [body(): lax.all_to_all(slice_sum.reshape(owners, capacity, block), 'dp', split_ax...]
    select_n x0 -> x2, local copies, waits for them, and re-layouts: none -> 2.88 us  [the longest x1 1.45 us: body(): jnp.where(is_first, other_cot, got_cot)]
    ppermute x3 -> x2, starting transfers between devices: 6.37 us -> 4.32 us  [_swap_pair(): return lax.ppermute(x, 'core', [(0, 1), (1, 0)])]
    unnamed x45 -> x51, local copies, waits for them, and re-layouts: 4.6 us -> 4.55 us
  transfers between devices with their start and end apart: 4 -> 3, of which waited for: 1 -> 1; matrix products, arithmetic and copies ran while one was open for 11% -> 15% of each run, Pallas kernels for 0% -> 0%
where the time goes in v13:
time: 168 us; the launch traced here: 167 us
  Pallas kernels  103 us (61%)
  local copies, waits for them, and re-layouts  17.6 us (10%)
  other arithmetic  16.2 us (10%)
  matrix products  15 us (9%)
  starting transfers between devices  11.8 us (7%)
  waiting for transfers between devices  2.75 us (2%)
    pallas_call x1, Pallas kernels, _exchange_both(): pl.pallas_call(functools.partial(_both_kernel, n), out_shape=(jax.ShapeDt...  62.7 us
    pallas_call x1, Pallas kernels, _exchange(): pl.pallas_call(functools.partial(_exchange_kernel, n, axis), out_shape=ja...  40.1 us
    all_to_all x1, starting transfers between devices, body(): lax.all_to_all(slice_sum.reshape(owners, capacity, block), 'dp', split_ax...  7.48 us
    unnamed x51, local copies, waits for them, and re-layouts  4.55 us
    ppermute x2, starting transfers between devices, _swap_pair(): return lax.ppermute(x, 'core', [(0, 1), (1, 0)])  4.32 us
  transfers between devices with their start and end apart: 3, of which 1 were waited for; matrix products, arithmetic and copies ran while one was open for 15% of the time, Pallas kernels for 0%

profile of v13, /device:TPU:6, one launch (start us, length us, event | category | flops | bytes accessed | tf_op | source)
XLA Modules:
  0.0 167.4 jit_solution(17137702194271016701)
XLA Ops:
  0.6 0.8 copy.47
  1.7 1.2 reduce-window.6
  2.9 0.2 slice_reduce_fusion
  3.5 0.7 multiply_add_fusion
  4.4 0.5 convolution_convert_fusion.5
  4.9 1.4 reshape.175.x_ref
  6.4 40.1 %shard_map.120 = bf16[64,80,128]{2,1,0:T(8,128)(2,1)} custom-call(bf16[64,80,128]{2,1,0:T(8,128)(2,1)} %reshape.175.x_ref), custom_call_target="tpu_custom_call" | custom-call | tf_op jit(solution)/shard_map/pallas_call | solution.py:67
  46.5 2.4 %reshape.176 = bf16[640,1024]{1,0:T(8,128)(2,1)S(1)} reshape(bf16[64,80,128]{2,1,0:T(8,128)(2,1)} %shard_map.120) | data formatting | bytes 2621440 | tf_op jit(solution)/shard_map/reshape | solution.py:331
  48.9 1.9 %collective-permute-start = (bf16[640,1024]{1,0:T(8,128)(2,1)S(1)}, bf16[640,1024]{1,0:T(8,128)(2,1)}, u32[]{:S(2)}, u32[]{:S(2)}) collective-permute-start(bf16[640,1024]{1,0:T(8,128)(2,1)S(1)} %reshape.176), channel_id=1, source_target_pairs={{0,1},{1,0},{2,3},{3,2},{4,5},{5,4},{6,7},{7,6},{8,9},{9,8},{10,11... | collective-permute-start | bytes 3932168 | tf_op jit(solution)/shard_map/ppermute | solution.py:259
  51.1 0.4 reshape_squeeze.3
  51.5 1.5 fusion.43
  53.1 1.3 copy.65
  54.4 0.4 copy.66
  54.9 0.6 fusion.41
  55.6 0.6 fusion.42
  56.2 1.5 broadcast_select_fusion.3
  57.8 0.9 convolution_bitcast_fusion.2
  58.9 0.4 copy-done.8
  59.3 1.6 multiply_convert_fusion.3
  60.9 1.6 fusion.4
  62.5 2.4 %collective-permute-start.1 = (bf16[4,640,256]{2,1,0:T(8,128)(2,1)}, bf16[4,640,256]{2,1,0:T(8,128)(2,1)}, u32[]{:S(2)}, u32[]{:S(2)}) collective-permute-start(bf16[4,640,256]{2,1,0:T(8,128)(2,1)} %fusion.4), channel_id=1, source_target_pairs={{0,1},{1,0},{2,3},{3,2},{4,5},{5,4},{6,7},{7,6},{8,9},{9,8},{10,11... | collective-permute-start | bytes 3932168 | tf_op jit(solution)/shard_map/ppermute | solution.py:259
  64.9 0.2 select_reduce_fusion.1
  65.8 1.4 fusion.34
  67.2 0.2 concatenate.17
  67.4 0.8 copy.68
  68.2 0.5 convolution_convert_fusion.6
  68.7 0.6 reshape.173
  69.3 2.3 %pad_maximum_fusion.1.a_ref = bf16[64,96,128]{2,1,0:T(8,128)(2,1)} fusion(bf16[64,16,128]{2,1,0:T(8,128)(2,1)} %bitcast.73, bf16[64,80,128]{2,1,0:T(8,128)(2,1)S(1)} %reshape.173), kind=kLoop, calls=%fused_computation.14 | loop fusion | flops 3145728 | bytes 3145728 | tf_op jit(solution)/shard_map/concatenate | solution.py:353
  71.6 2.9 %fusion.b_ref = bf16[4,640,256]{2,1,0:T(8,128)(2,1)} fusion(bf16[4,640,256]{2,1,0:T(8,128)(2,1)} %collective-permute-done.1, bf16[128,4,1,256]{0,3,1,2:T(8,128)(2,1)S(1)} %copy.65, bf16[128,4,1,256]{0,3,1,2:T(8,128)(2,1)S(1)} %copy-done.2, pred[]{:T(512)S(6)} %eq.75, bf16[128,640]{0,1:T(8,128)(2,1)S(1)} %copy-done.11), kind=kOutput, calls=%fused_computation.3 | convolution fusion | flops 171180032 | bytes 3309569 | tf_op jit(solution)/shard_map/hr,hzb->zrb/dot_general | solution.py:350
  74.6 62.7 %shard_map.121 = (bf16[64,96,128]{2,1,0:T(8,128)(2,1)}, bf16[4,640,256]{2,1,0:T(8,128)(2,1)}, bf16[64,96,128]{2,1,0:T(8,128)(2,1)}) custom-call(bf16[64,96,128]{2,1,0:T(8,128)(2,1)} %pad_maximum_fusion.1.a_ref, bf16[4,640,256]{2,1,0:T(8,128)(2,1)} %fusion.b_ref), custom_call_target="tpu_custom_call" | custom-call | tf_op jit(solution)/shard_map/pallas_call | solution.py:234
  137.3 1.1 slice_convert_fusion
  138.6 0.7 slice_reduce_fusion.2
  139.3 0.4 reduce_sum.125
  139.6 0.9 reshape.177
  140.6 7.5 %all-to-all-start = ((bf16[64,10,256]{2,1,0:T(8,128)(2,1)}), bf16[64,10,256]{2,1,0:T(8,128)(2,1)}, u32[]{:S(2)}, u32[]{:S(2)}) async-start(bf16[64,10,256]{2,1,0:T(8,128)(2,1)} %reshape.177), calls=%async_computation | async-start | bytes 1048576 | tf_op jit(solution)/shard_map/all_to_all | solution.py:373
  148.1 1.9 %broadcast_select_fusion.1 = (bf16[64,80,128]{2,1,0:T(8,128)(2,1)S(1)}, bf16[64,80,128]{2,1,0:T(8,128)(2,1)S(1)}) fusion(pred[]{:T(512)S(6)} %eq.75, bf16[64,96,128]{2,1,0:T(8,128)(2,1)} %get-tuple-element.9, bf16[64,96,128]{2,1,0:T(8,128)(2,1)} %get-tuple-element.8), kind=kLoop, calls=%fused_computation.22 | loop fusion | flops 1310720 | bytes 5242881 | tf_op jit(solution)/shard_map/jit(_where)/select_n | solution.py:362
  149.9 1.4 select_n.90
  151.5 1.4 select_n.92
  153.0 1.9 %fusion.13 = f32[640]{0:T(1024)S(1)} fusion(f32[640,5]{1,0:T(8,128)S(1)} %reshape.180, f32[]{:T(128)} %get-tuple-element.11, f32[]{:T(128)} %get-tuple-element.10), kind=kLoop, calls=%fused_computation.36 | loop fusion | flops 4480 | bytes 15368 | tf_op jit(solution)/shard_map/mul | solution.py:371
  154.9 2.0 %convolution_bitcast_fusion = f32[128,640]{0,1:T(8,128)S(1)} fusion(bf16[1,128,2048]{2,1,0:T(8,128)(2,1)} %param.17, bf16[640,1024]{1,0:T(8,128)(2,1)S(1)} %copy-done.5, bf16[640,1024]{1,0:T(8,128)(2,1)S(1)} %copy-done.4, f32[640]{0:T(1024)S(1)} %fusion.13), kind=kOutput, calls=%fused_computation.26 | convolution fusion | flops 343408640 | bytes 3475968 | tf_op jit(solution)/shard_map/dot_general | solution.py:384
  156.9 1.6 fusion.3
  158.6 0.2 copy-done.21
  158.9 1.4 fusion.2
  160.3 1.5 fusion.1
  161.8 2.7 %all-to-all-done = bf16[64,10,256]{2,1,0:T(8,128)(2,1)} async-done(((bf16[64,10,256]{2,1,0:T(8,128)(2,1)}), bf16[64,10,256]{2,1,0:T(8,128)(2,1)}, u32[]{:S(2)}, u32[]{:S(2)}) %all-to-all-start) | async-done | bytes 327712 | tf_op jit(solution)/shard_map/all_to_all | solution.py:373
  164.6 1.2 reshape.178
  165.7 0.5 fusion.7
  166.4 0.9 reduce_sum.126
  (76 shorter events, 2.6 us)
Async XLA Ops:
  0.6 3.8 %copy-start = (bf16[128,2048]{1,0:T(8,128)(2,1)S(1)}, bf16[128,2048]{1,0:T(8,128)(2,1)}, u32[]{:S(2)}) copy-start(bf16[128,2048]{1,0:T(8,128)(2,1)} %param.9) | copy-start | bytes 1572868
  46.5 4.4 %copy-start.15 = (f32[128,4]{0,1:T(4,128)S(1)}, f32[128,4]{0,1:T(4,128)}, u32[]{:S(2)}) copy-start(f32[128,4]{0,1:T(4,128)} %param.12) | copy-start | bytes 6148
  46.5 4.6 %copy-start.13 = (bf16[1,128,2048]{2,1,0:T(8,128)(2,1)S(1)}, bf16[1,128,2048]{2,1,0:T(8,128)(2,1)}, u32[]{:S(2)}) copy-start(bf16[1,128,2048]{2,1,0:T(8,128)(2,1)} %param.17) | copy-start | bytes 1572868
  48.9 7.3 %collective-permute-start = (bf16[640,1024]{1,0:T(8,128)(2,1)S(1)}, bf16[640,1024]{1,0:T(8,128)(2,1)}, u32[]{:S(2)}, u32[]{:S(2)}) collective-permute-start(bf16[640,1024]{1,0:T(8,128)(2,1)S(1)} %reshape.176), channel_id=1, source_target_pairs={{0,1},{1,0},{2,3},{3,2},{4,5},{5,4},{6,7},{7,6},{8,9},{9,8},{10,11... | collective-permute-start | bytes 3932168 | tf_op jit(solution)/shard_map/ppermute | solution.py:259
  51.5 3.3 %copy-start.19 = (s32[2]{0:T(128)S(1)}, s32[2]{0:T(128)}, u32[]{:S(2)}) copy-start(s32[2]{0:T(128)} %param.14) | copy-start | bytes 28
  51.5 3.4 %copy-start.16 = (s32[128]{0:T(128)S(1)}, s32[128]{0:T(128)}, u32[]{:S(2)}) copy-start(s32[128]{0:T(128)} %param.13) | copy-start | bytes 1540
  54.8 6.1 %copy-start.1 = (bf16[128,4,1,256]{0,3,1,2:T(8,128)(2,1)}, bf16[128,4,1,256]{0,3,1,2:T(8,128)(2,1)S(1)}, u32[]{:S(2)}) copy-start(bf16[128,4,1,256]{0,3,1,2:T(8,128)(2,1)S(1)} %copy.66) | copy-start | bytes 786436
  56.2 1.6 copy-start.17
  57.8 1.1 copy-start.6
  57.8 1.5 copy-start.8
  57.8 1.5 copy-start.18
  59.3 1.6 copy-start.20
  60.9 6.3 %copy-start.10 = (bf16[128,640]{0,1:T(8,128)(2,1)}, bf16[128,640]{0,1:T(8,128)(2,1)S(1)}, u32[]{:S(2)}) copy-start(bf16[128,640]{0,1:T(8,128)(2,1)S(1)} %get-tuple-element.27) | copy-start | bytes 491524
  60.9 7.3 %copy-start.14 = (bf16[128,2048]{1,0:T(8,128)(2,1)S(1)}, bf16[128,2048]{1,0:T(8,128)(2,1)}, u32[]{:S(2)}) copy-start(bf16[128,2048]{1,0:T(8,128)(2,1)} %param.10) | copy-start | bytes 1572868
  62.5 9.1 %collective-permute-start.1 = (bf16[4,640,256]{2,1,0:T(8,128)(2,1)}, bf16[4,640,256]{2,1,0:T(8,128)(2,1)}, u32[]{:S(2)}, u32[]{:S(2)}) collective-permute-start(bf16[4,640,256]{2,1,0:T(8,128)(2,1)} %fusion.4), channel_id=1, source_target_pairs={{0,1},{1,0},{2,3},{3,2},{4,5},{5,4},{6,7},{7,6},{8,9},{9,8},{10,11... | collective-permute-start | bytes 3932168 | tf_op jit(solution)/shard_map/ppermute | solution.py:259
  69.3 2.3 %copy-start.2 = (bf16[128,4,1,256]{0,3,1,2:T(8,128)(2,1)S(1)}, bf16[128,4,1,256]{0,3,1,2:T(8,128)(2,1)}, u32[]{:S(2)}) copy-start(bf16[128,4,1,256]{0,3,1,2:T(8,128)(2,1)} %copy-done.1) | copy-start | bytes 786436
  69.3 2.3 %copy-start.11 = (bf16[128,640]{0,1:T(8,128)(2,1)S(1)}, bf16[128,640]{0,1:T(8,128)(2,1)}, u32[]{:S(2)}) copy-start(bf16[128,640]{0,1:T(8,128)(2,1)} %copy-done.10) | copy-start | bytes 491524
  137.3 2.0 %copy-start.3 = (bf16[4,640,256]{2,1,0:T(8,128)(2,1)S(1)}, bf16[4,640,256]{2,1,0:T(8,128)(2,1)}, u32[]{:S(2)}) copy-start(bf16[4,640,256]{2,1,0:T(8,128)(2,1)} %get-tuple-element.7) | copy-start | bytes 3932164
  140.6 24.0 %all-to-all-start = ((bf16[64,10,256]{2,1,0:T(8,128)(2,1)}), bf16[64,10,256]{2,1,0:T(8,128)(2,1)}, u32[]{:S(2)}, u32[]{:S(2)}) async-start(bf16[64,10,256]{2,1,0:T(8,128)(2,1)} %reshape.177), calls=%async_computation | async-start | bytes 1048576 | tf_op jit(solution)/shard_map/all_to_all | solution.py:373
  151.5 3.4 %copy-start.4 = (bf16[640,1024]{1,0:T(8,128)(2,1)S(1)}, bf16[640,1024]{1,0:T(8,128)(2,1)}, u32[]{:S(2)}) copy-start(bf16[640,1024]{1,0:T(8,128)(2,1)} %select_n.90) | copy-start | bytes 3932164
  153.0 1.9 %copy-start.5 = (bf16[640,1024]{1,0:T(8,128)(2,1)S(1)}, bf16[640,1024]{1,0:T(8,128)(2,1)}, u32[]{:S(2)}) copy-start(bf16[640,1024]{1,0:T(8,128)(2,1)} %select_n.92) | copy-start | bytes 3932164
  154.9 2.0 %copy-start.12 = (bf16[128,640]{0,1:T(8,128)(2,1)S(1)}, bf16[128,640]{0,1:T(8,128)(2,1)}, u32[]{:S(2)}) copy-start(bf16[128,640]{0,1:T(8,128)(2,1)} %copy-done.10) | copy-start | bytes 491524
  156.9 1.6 copy-start.7
  156.9 1.7 %copy-start.9 = (bf16[640,1024]{1,0:T(8,128)(2,1)S(1)}, bf16[640,1024]{1,0:T(8,128)(2,1)}, u32[]{:S(2)}) copy-start(bf16[640,1024]{1,0:T(8,128)(2,1)} %copy-done.8) | copy-start | bytes 3932164
  156.9 1.9 %copy-start.21 = (f32[128,640]{0,1:T(8,128)S(1)}, f32[128,640]{0,1:T(8,128)}, u32[]{:S(2)}) copy-start(f32[128,640]{0,1:T(8,128)} %copy-done.20) | copy-start | bytes 983044
  158.9 1.4 copy-start.22

commit v14 on v13

--- a/solution.py
+++ b/solution.py
@@ -13,7 +13,7 @@
 MESH = pl.DeviceIdType.MESH
 
 
-def _exchange_kernel(n, axis, x_ref, y_ref, send_sem, recv_sem, own_sem):
+def _exchange_kernel(n, axis, x_ref, y_ref, yp_ref, send_sem, recv_sem, own_sem, p_sem):
     me = lax.axis_index(axis)
 
     def copy_to(peer):
@@ -43,7 +43,9 @@
         return carry
 
     lax.fori_loop(1, n, greet, 0)
-    pl.semaphore_wait(barrier, n - 1)
+    partner = 1 - lax.axis_index("core")
+    pl.semaphore_signal(barrier, inc=1, device_id={"core": partner}, device_id_type=MESH)
+    pl.semaphore_wait(barrier, n)
     own = pltpu.make_async_copy(x_ref.at[me], y_ref.at[me], own_sem)
     own.start()
 
@@ -60,19 +62,30 @@
 
     lax.fori_loop(1, n, finish, 0)
     own.wait()
+    to_partner = pltpu.make_async_remote_copy(
+        src_ref=y_ref,
+        dst_ref=yp_ref,
+        send_sem=p_sem.at[0],
+        recv_sem=p_sem.at[1],
+        device_id={"core": partner},
+        device_id_type=MESH,
+    )
+    to_partner.start()
+    to_partner.wait()
 
 
 def _exchange(x, collective_id, axis="dp"):
     n = x.shape[0]
     return pl.pallas_call(
         functools.partial(_exchange_kernel, n, axis),
-        out_shape=jax.ShapeDtypeStruct(x.shape, x.dtype),
+        out_shape=(jax.ShapeDtypeStruct(x.shape, x.dtype), jax.ShapeDtypeStruct(x.shape, x.dtype)),
         in_specs=[pl.BlockSpec(memory_space=pl.ANY)],
-        out_specs=pl.BlockSpec(memory_space=pl.ANY),
+        out_specs=(pl.BlockSpec(memory_space=pl.ANY), pl.BlockSpec(memory_space=pl.ANY)),
         scratch_shapes=[
             pltpu.SemaphoreType.DMA((n,)),
             pltpu.SemaphoreType.DMA((n,)),
             pltpu.SemaphoreType.DMA(()),
+            pltpu.SemaphoreType.DMA((2,)),
         ],
         compiler_params=pltpu.CompilerParams(collective_id=collective_id, has_side_effects=True),
     )(x)
@@ -328,8 +341,9 @@
     pick = hit_tok.astype(tokens.dtype)
     send_tok = jnp.dot(pick, my_tokens, preferred_element_type=jnp.float32).astype(tokens.dtype)
     send_cot = jnp.dot(pick, my_cotan, preferred_element_type=jnp.float32).astype(tokens.dtype)
-    got = _exchange(send_tok.reshape(owners, capacity * half // lanes, lanes), 0).reshape(slots_all, half)
-    other = _swap_pair(got)
+    got, other = _exchange(send_tok.reshape(owners, capacity * half // lanes, lanes), 0)
+    got = got.reshape(slots_all, half)
+    other = other.reshape(slots_all, half)
     rows_in = jnp.concatenate(
         [jnp.where(is_first, got, other), jnp.where(is_first, other, got)], axis=1
     )

time: 168 us -> 192 us (1.14)
  local copies, waits for them, and re-layouts: 17.6 us -> 32.9 us
  other arithmetic: 16.2 us -> 23 us
  Pallas kernels: 103 us -> 106 us
  waiting for transfers between devices: 2.75 us -> 0.01 us
  matrix products: 15 us -> 17.5 us
  starting transfers between devices: 11.8 us -> 9.73 us
    pallas_call x1, Pallas kernels: 40.1 us -> 43.1 us  [_exchange(): pl.pallas_call(functools.partial(_exchange_kernel, n, axis), out_shape=(j...]
    unnamed x51 -> x48, local copies, waits for them, and re-layouts: 4.55 us -> 7.57 us
    select_n x0 -> x2, local copies, waits for them, and re-layouts: none -> 2.86 us  [the longest x1 1.45 us: body(): jnp.where(is_first, other, got)]
    all_to_all x1, waiting for transfers between devices: 2.75 us -> 0.01 us  [body(): lax.all_to_all(slice_sum.reshape(owners, capacity, block), 'dp', split_ax...]
    reshape x1, local copies, waits for them, and re-layouts: 0.6 us -> 3.25 us  [body(): send_cot.reshape(owners, capacity * half // lanes, lanes)]
    reshape x1 -> x0, local copies, waits for them, and re-layouts: 2.42 us -> none  [body(): _exchange(send_tok.reshape(owners, capacity * half // lanes, lanes), 0)]
    ppermute x2 -> x1, starting transfers between devices: 4.32 us -> 2.26 us  [_swap_pair(): return lax.ppermute(x, 'core', [(0, 1), (1, 0)])]
    dot_general x1, matrix products: 0.49 us -> 2.53 us  [body(): jnp.dot(pick, my_cotan, preferred_element_type=jnp.float32)]
  transfers between devices with their start and end apart: 3 -> 2, of which waited for: 1 -> 0; matrix products, arithmetic and copies ran while one was open for 15% -> 22% of each run, Pallas kernels for 0% -> 0%
where the time goes in v14:
time: 192 us; the launch traced here: 190 us
  Pallas kernels  106 us (55%)
  local copies, waits for them, and re-layouts  32.9 us (17%)
  other arithmetic  23 us (12%)
  matrix products  17.5 us (9%)
  starting transfers between devices  9.73 us (5%)
    pallas_call x1, Pallas kernels, _exchange_both(): pl.pallas_call(functools.partial(_both_kernel, n), out_shape=(jax.ShapeDt...  62.9 us
    pallas_call x1, Pallas kernels, _exchange(): pl.pallas_call(functools.partial(_exchange_kernel, n, axis), out_shape=(j...  43.1 us
    unnamed x48, local copies, waits for them, and re-layouts  7.57 us
    all_to_all x1, starting transfers between devices, body(): lax.all_to_all(slice_sum.reshape(owners, capacity, block), 'dp', split_ax...  7.47 us
  transfers between devices with their start and end apart: 2, of which 0 were waited for; matrix products, arithmetic and copies ran while one was open for 22% of the time, Pallas kernels for 0%

profile of v14, /device:TPU:6, one launch (start us, length us, event | category | flops | bytes accessed | tf_op | source)
XLA Modules:
  0.0 190.1 jit_solution(338448145085982208)
XLA Ops:
  0.6 0.8 copy.47
  1.7 1.2 reduce-window.6
  3.5 0.7 multiply_add_fusion
  4.4 1.4 reshape_squeeze.3
  5.8 0.7 fusion.43
  7.0 1.1 copy.66
  8.6 1.4 reshape.178.x_ref
  10.0 43.1 %shard_map.120 = (bf16[64,80,128]{2,1,0:T(8,128)(2,1)}, bf16[64,80,128]{2,1,0:T(8,128)(2,1)}) custom-call(bf16[64,80,128]{2,1,0:T(8,128)(2,1)} %reshape.178.x_ref), custom_call_target="tpu_custom_call" | custom-call | tf_op jit(solution)/shard_map/pallas_call | solution.py:79
  53.2 1.9 broadcast_select_fusion.2
  55.1 1.4 select_n.91
  56.5 1.4 select_n.89
  57.9 1.5 constant_dynamic-update-slice_fusion.1
  59.8 0.9 copy-done.11
  60.7 0.9 convolution_bitcast_fusion.2
  61.7 1.6 multiply_convert_fusion.3
  63.3 1.6 fusion.4
  64.9 2.3 %collective-permute-start = (bf16[4,640,256]{2,1,0:T(8,128)(2,1)}, bf16[4,640,256]{2,1,0:T(8,128)(2,1)}, u32[]{:S(2)}, u32[]{:S(2)}) collective-permute-start(bf16[4,640,256]{2,1,0:T(8,128)(2,1)} %fusion.4), channel_id=1, source_target_pairs={{0,1},{1,0},{2,3},{3,2},{4,5},{5,4},{6,7},{7,6},{8,9},{9,8},{10,11... | collective-permute-start | bytes 3932168 | tf_op jit(solution)/shard_map/ppermute | solution.py:272
  68.5 1.2 fusion.42
  70.3 0.8 copy.51
  71.8 0.9 select_reduce_fusion.1
  72.7 0.7 multiply_add_fusion.1
  73.4 0.9 select_reduce_fusion
  74.4 0.8 copy.52
  75.2 1.1 reshape.177
  76.3 1.3 fusion.34
  77.7 0.7 broadcast_in_dim.81
  78.4 1.9 concatenate.17
  80.3 1.7 copy.68
  82.0 2.5 %convolution_convert_fusion.6 = bf16[640,1024]{1,0:T(8,128)(2,1)} fusion(pred[640,128]{1,0:T(8,128)(4,1)S(1)} %fusion.6, bf16[128,2048]{1,0:T(8,128)(2,1)} %param.10, s32[]{:T(128)S(6)} %select_n.78), kind=kOutput, calls=%fused_computation.12 | convolution fusion | flops 168427520 | bytes 1654788 | tf_op jit(solution)/shard_map/dot_general | solution.py:343
  84.5 3.2 %reshape.176 = bf16[64,80,128]{2,1,0:T(8,128)(2,1)} reshape(bf16[640,1024]{1,0:T(8,128)(2,1)} %convolution_convert_fusion.6) | data formatting | bytes 2621440 | tf_op jit(solution)/shard_map/reshape | solution.py:368
  87.7 2.7 %pad_maximum_fusion.a_ref = bf16[64,96,128]{2,1,0:T(8,128)(2,1)} fusion(bf16[64,16,128]{2,1,0:T(8,128)(2,1)} %bitcast.77, bf16[64,80,128]{2,1,0:T(8,128)(2,1)} %reshape.176), kind=kLoop, calls=%fused_computation.13 | loop fusion | flops 3145728 | bytes 3145728 | tf_op jit(solution)/shard_map/concatenate | solution.py:367
  90.4 2.9 %fusion.b_ref = bf16[4,640,256]{2,1,0:T(8,128)(2,1)} fusion(bf16[4,640,256]{2,1,0:T(8,128)(2,1)} %collective-permute-done, bf16[128,4,1,256]{0,3,1,2:T(8,128)(2,1)S(1)} %copy.65, bf16[128,4,1,256]{0,3,1,2:T(8,128)(2,1)S(1)} %copy-done.5, pred[]{:T(512)S(6)} %eq.75, bf16[128,640]{0,1:T(8,128)(2,1)S(1)} %copy-done.9), kind=kOutput, calls=%fused_computation.2 | convolution fusion | flops 171180032 | bytes 3309569 | tf_op jit(solution)/shard_map/hr,hzb->zrb/dot_general | solution.py:364
  93.4 62.9 %shard_map.121 = (bf16[64,96,128]{2,1,0:T(8,128)(2,1)}, bf16[4,640,256]{2,1,0:T(8,128)(2,1)}, bf16[64,96,128]{2,1,0:T(8,128)(2,1)}) custom-call(bf16[64,96,128]{2,1,0:T(8,128)(2,1)} %pad_maximum_fusion.a_ref, bf16[4,640,256]{2,1,0:T(8,128)(2,1)} %fusion.b_ref), custom_call_target="tpu_custom_call" | custom-call | tf_op jit(solution)/shard_map/pallas_call | solution.py:247
  156.3 1.0 slice_convert_fusion
  157.5 0.8 slice_reduce_fusion.2
  158.2 1.6 reduce_sum.125
  159.9 0.9 reshape.179
  160.8 7.5 %all-to-all-start = ((bf16[64,10,256]{2,1,0:T(8,128)(2,1)}), bf16[64,10,256]{2,1,0:T(8,128)(2,1)}, u32[]{:S(2)}, u32[]{:S(2)}) async-start(bf16[64,10,256]{2,1,0:T(8,128)(2,1)} %reshape.179), calls=%async_computation | async-start | bytes 1048576 | tf_op jit(solution)/shard_map/all_to_all | solution.py:387
  168.3 3.4 %broadcast_select_fusion.1 = (bf16[64,80,128]{2,1,0:T(8,128)(2,1)}, bf16[64,80,128]{2,1,0:T(8,128)(2,1)}) fusion(pred[]{:T(512)S(6)} %eq.75, bf16[64,96,128]{2,1,0:T(8,128)(2,1)} %get-tuple-element.13, bf16[64,96,128]{2,1,0:T(8,128)(2,1)} %get-tuple-element.12), kind=kLoop, calls=%fused_computation.21 | loop fusion | flops 1310720 | bytes 5242881 | tf_op jit(solution)/shard_map/jit(_where)/select_n | solution.py:376
  171.7 3.3 %select_n.95 = bf16[640,1024]{1,0:T(8,128)(2,1)} reshape(bf16[64,80,128]{2,1,0:T(8,128)(2,1)} %get-tuple-element.22) | data formatting | bytes 2621440 | tf_op jit(solution)/shard_map/jit(_where)/select_n | solution.py:376
  175.1 3.2 %select_n.97 = bf16[640,1024]{1,0:T(8,128)(2,1)} reshape(bf16[64,80,128]{2,1,0:T(8,128)(2,1)} %get-tuple-element.23) | data formatting | bytes 2621440 | tf_op jit(solution)/shard_map/jit(_where)/select_n | solution.py:376
  178.3 2.0 %fusion.13 = f32[640]{0:T(1024)S(1)} fusion(f32[640,5]{1,0:T(8,128)S(1)} %reshape.182, f32[]{:T(128)} %get-tuple-element.15, f32[]{:T(128)} %get-tuple-element.14), kind=kLoop, calls=%fused_computation.35 | loop fusion | flops 4480 | bytes 15368 | tf_op jit(solution)/shard_map/mul | solution.py:385
  180.3 2.4 %convolution_bitcast_fusion = f32[128,640]{0,1:T(8,128)S(1)} fusion(bf16[1,128,2048]{2,1,0:T(8,128)(2,1)} %param.17, bf16[640,1024]{1,0:T(8,128)(2,1)} %select_n.97, bf16[640,1024]{1,0:T(8,128)(2,1)S(1)} %copy-done.6, f32[640]{0:T(1024)S(1)} %fusion.13), kind=kOutput, calls=%fused_computation.25 | convolution fusion | flops 343408640 | bytes 3475968 | tf_op jit(solution)/shard_map/dot_general | solution.py:398
  182.8 1.6 fusion.3
  184.3 1.4 fusion.2
  185.8 1.5 fusion.1
  187.3 1.2 reshape.180
  189.2 0.9 reduce_sum.126
  (73 shorter events, 6.0 us)
Async XLA Ops:
  0.6 7.5 %copy-start = (bf16[128,2048]{1,0:T(8,128)(2,1)S(1)}, bf16[128,2048]{1,0:T(8,128)(2,1)}, u32[]{:S(2)}) copy-start(bf16[128,2048]{1,0:T(8,128)(2,1)} %param.9) | copy-start | bytes 1572868
  1.6 2.6 %copy-start.13 = (s32[512]{0:T(512)}, s32[512]{0:T(512)S(1)}, u32[]{:S(2)}) copy-start(s32[512]{0:T(512)S(1)} %reshape.174) | copy-start | bytes 6148
  3.4 0.9 copy-start.14
  57.9 1.7 copy-start.1
  59.6 1.0 copy-start.11
  60.7 1.0 copy-start.19
  61.7 1.6 copy-start.2
  61.7 1.6 copy-start.4
  63.3 1.6 copy-start.8
  63.3 3.9 %copy-start.20 = (s32[2]{0:T(128)S(1)}, s32[2]{0:T(128)}, u32[]{:S(2)}) copy-start(s32[2]{0:T(128)} %param.14) | copy-start | bytes 28
  63.3 4.0 %copy-start.18 = (s32[128]{0:T(128)S(1)}, s32[128]{0:T(128)}, u32[]{:S(2)}) copy-start(s32[128]{0:T(128)} %param.13) | copy-start | bytes 1540
  63.3 6.4 %copy-start.15 = (f32[128,4]{0,1:T(4,128)S(1)}, f32[128,4]{0,1:T(4,128)}, u32[]{:S(2)}) copy-start(f32[128,4]{0,1:T(4,128)} %param.12) | copy-start | bytes 6148
  64.9 25.5 %collective-permute-start = (bf16[4,640,256]{2,1,0:T(8,128)(2,1)}, bf16[4,640,256]{2,1,0:T(8,128)(2,1)}, u32[]{:S(2)}, u32[]{:S(2)}) collective-permute-start(bf16[4,640,256]{2,1,0:T(8,128)(2,1)} %fusion.4), channel_id=1, source_target_pairs={{0,1},{1,0},{2,3},{3,2},{4,5},{5,4},{6,7},{7,6},{8,9},{9,8},{10,11... | collective-permute-start | bytes 3932168 | tf_op jit(solution)/shard_map/ppermute | solution.py:272
  68.0 0.5 copy-start.17
  87.7 2.7 %copy-start.5 = (bf16[128,4,1,256]{0,3,1,2:T(8,128)(2,1)S(1)}, bf16[128,4,1,256]{0,3,1,2:T(8,128)(2,1)}, u32[]{:S(2)}) copy-start(bf16[128,4,1,256]{0,3,1,2:T(8,128)(2,1)} %copy.66) | copy-start | bytes 786436
  87.7 2.7 %copy-start.9 = (bf16[128,640]{0,1:T(8,128)(2,1)S(1)}, bf16[128,640]{0,1:T(8,128)(2,1)}, u32[]{:S(2)}) copy-start(bf16[128,640]{0,1:T(8,128)(2,1)} %copy-done.8) | copy-start | bytes 491524
  160.8 26.5 %all-to-all-start = ((bf16[64,10,256]{2,1,0:T(8,128)(2,1)}), bf16[64,10,256]{2,1,0:T(8,128)(2,1)}, u32[]{:S(2)}, u32[]{:S(2)}) async-start(bf16[64,10,256]{2,1,0:T(8,128)(2,1)} %reshape.179), calls=%async_computation | async-start | bytes 1048576 | tf_op jit(solution)/shard_map/all_to_all | solution.py:387
  178.3 2.0 %copy-start.6 = (bf16[640,1024]{1,0:T(8,128)(2,1)S(1)}, bf16[640,1024]{1,0:T(8,128)(2,1)}, u32[]{:S(2)}) copy-start(bf16[640,1024]{1,0:T(8,128)(2,1)} %select_n.95) | copy-start | bytes 3932164
  180.3 2.5 %copy-start.7 = (bf16[640,1024]{1,0:T(8,128)(2,1)S(1)}, bf16[640,1024]{1,0:T(8,128)(2,1)}, u32[]{:S(2)}) copy-start(bf16[640,1024]{1,0:T(8,128)(2,1)} %select_n.97) | copy-start | bytes 3932164
  180.3 2.5 %copy-start.10 = (bf16[128,640]{0,1:T(8,128)(2,1)S(1)}, bf16[128,640]{0,1:T(8,128)(2,1)}, u32[]{:S(2)}) copy-start(bf16[128,640]{0,1:T(8,128)(2,1)} %copy-done.8) | copy-start | bytes 491524
  182.8 1.6 copy-start.3
  184.3 1.4 copy-start.12
  185.8 2.7 %copy-start.16 = (f32[512]{0:T(512)S(1)}, f32[512]{0:T(512)}, u32[]{:S(2)}) copy-start(f32[512]{0:T(512)} %broadcast_in_dim.72) | copy-start | bytes 6148

commit v15 on v13

--- a/solution.py
+++ b/solution.py
@@ -139,7 +139,7 @@
     )(x)
 
 
-def _both_kernel(n, a_ref, b_ref, ya_ref, yb_ref, yp_ref, a_send, a_recv, a_own, relay_up, relay_down, b_send, b_recv, b_own, p_sem):
+def _both_kernel(n, a_ref, b_ref, ya_ref, yb_ref, yp_ref, a_send, a_recv, a_own, relay_up, relay_down, b_send, b_recv, b_own, p_send, p_recv):
     me = lax.axis_index("dp")
     at = lax.axis_index("zh")
     up, down, across = lax.rem(at + 1, 4), lax.rem(at + 3, 4), lax.rem(at + 2, 4)
@@ -202,30 +202,39 @@
     pass_down = zh_copy(relay_down, yb_ref.at[up, pl.ds(rows, rows)], 5, down)
     pass_down.start()
 
+    def hand(source):
+        return pltpu.make_async_remote_copy(
+            src_ref=ya_ref.at[source],
+            dst_ref=yp_ref.at[source],
+            send_sem=p_send.at[source],
+            recv_sem=p_recv.at[source],
+            device_id={"core": partner},
+            device_id_type=MESH,
+        )
+
     def finish(i, carry):
         peer = lax.rem(me + i, n)
         source = lax.rem(me + n - i, n)
         dp_copy(a_ref.at[peer], ya_ref.at[me], peer, me, peer).wait_send()
         dp_copy(a_ref.at[source], ya_ref.at[source], source, source, source).wait_recv()
+        hand(source).start()
         return carry
 
     lax.fori_loop(1, n, finish, 0)
     own_a.wait()
-    to_partner = pltpu.make_async_remote_copy(
-        src_ref=ya_ref,
-        dst_ref=yp_ref,
-        send_sem=p_sem.at[0],
-        recv_sem=p_sem.at[1],
-        device_id={"core": partner},
-        device_id_type=MESH,
-    )
-    to_partner.start()
+    hand(me).start()
     for copy in (to_up, to_down, lift, drop, pass_up, pass_down):
         copy.wait_send()
     for copy in (to_up, to_down, pass_up, pass_down):
         copy.wait_recv()
     own_b.wait()
-    to_partner.wait()
+
+    def handed(i, carry):
+        hand(i).wait_send()
+        hand(i).wait_recv()
+        return carry
+
+    lax.fori_loop(0, n, handed, 0)
 
 
 def _exchange_both(a, b, collective_id):
@@ -249,7 +258,8 @@
             pltpu.SemaphoreType.DMA((6,)),
             pltpu.SemaphoreType.DMA((6,)),
             pltpu.SemaphoreType.DMA(()),
-            pltpu.SemaphoreType.DMA((2,)),
+            pltpu.SemaphoreType.DMA((n,)),
+            pltpu.SemaphoreType.DMA((n,)),
         ],
         compiler_params=pltpu.CompilerParams(collective_id=collective_id, has_side_effects=True),
     )(a, b)

time: 168 us -> 169 us (level)
  no operation moved by 1% of the time
where the time goes in v15:
time: 169 us
  Pallas kernels  104 us (62%)
  local copies, waits for them, and re-layouts  17.6 us (10%)
  other arithmetic  16.2 us (10%)
  matrix products  15 us (9%)
  starting transfers between devices  11.8 us (7%)
  waiting for transfers between devices  2.44 us (1%)
    pallas_call x1, Pallas kernels, _exchange_both(): pl.pallas_call(functools.partial(_both_kernel, n), out_shape=(jax.ShapeDt...  64.3 us
    pallas_call x1, Pallas kernels, _exchange(): pl.pallas_call(functools.partial(_exchange_kernel, n, axis), out_shape=ja...  40.1 us
    all_to_all x1, starting transfers between devices, body(): lax.all_to_all(slice_sum.reshape(owners, capacity, block), 'dp', split_ax...  7.48 us
    unnamed x51, local copies, waits for them, and re-layouts  4.55 us
    ppermute x2, starting transfers between devices, _swap_pair(): return lax.ppermute(x, 'core', [(0, 1), (1, 0)])  4.32 us
  transfers between devices with their start and end apart: 3, of which 1 were waited for; matrix products, arithmetic and copies ran while one was open for 15% of the time, Pallas kernels for 0%

profile of v15, /device:TPU:6, one launch (start us, length us, event | category | flops | bytes accessed | tf_op | source)
XLA Modules:
  0.0 168.6 jit_solution(7372086845481433587)
XLA Ops:
  0.6 0.8 copy.47
  1.7 1.2 reduce-window.6
  2.9 0.2 slice_reduce_fusion
  3.5 0.7 multiply_add_fusion
  4.4 0.5 convolution_convert_fusion.5
  4.9 1.4 reshape.175.x_ref
  6.4 40.1 %shard_map.120 = bf16[64,80,128]{2,1,0:T(8,128)(2,1)} custom-call(bf16[64,80,128]{2,1,0:T(8,128)(2,1)} %reshape.175.x_ref), custom_call_target="tpu_custom_call" | custom-call | tf_op jit(solution)/shard_map/pallas_call | solution.py:67
  46.5 2.4 %reshape.176 = bf16[640,1024]{1,0:T(8,128)(2,1)S(1)} reshape(bf16[64,80,128]{2,1,0:T(8,128)(2,1)} %shard_map.120) | data formatting | bytes 2621440 | tf_op jit(solution)/shard_map/reshape | solution.py:341
  48.9 1.9 %collective-permute-start = (bf16[640,1024]{1,0:T(8,128)(2,1)S(1)}, bf16[640,1024]{1,0:T(8,128)(2,1)}, u32[]{:S(2)}, u32[]{:S(2)}) collective-permute-start(bf16[640,1024]{1,0:T(8,128)(2,1)S(1)} %reshape.176), channel_id=1, source_target_pairs={{0,1},{1,0},{2,3},{3,2},{4,5},{5,4},{6,7},{7,6},{8,9},{9,8},{10,11... | collective-permute-start | bytes 3932168 | tf_op jit(solution)/shard_map/ppermute | solution.py:269
  51.1 0.4 reshape_squeeze.3
  51.5 1.5 fusion.43
  53.1 1.3 copy.65
  54.4 0.4 copy.66
  54.9 0.6 fusion.41
  55.6 0.6 fusion.42
  56.2 1.5 broadcast_select_fusion.3
  57.8 0.9 convolution_bitcast_fusion.2
  58.9 0.4 copy-done.8
  59.3 1.6 multiply_convert_fusion.3
  60.9 1.6 fusion.4
  62.5 2.4 %collective-permute-start.1 = (bf16[4,640,256]{2,1,0:T(8,128)(2,1)}, bf16[4,640,256]{2,1,0:T(8,128)(2,1)}, u32[]{:S(2)}, u32[]{:S(2)}) collective-permute-start(bf16[4,640,256]{2,1,0:T(8,128)(2,1)} %fusion.4), channel_id=1, source_target_pairs={{0,1},{1,0},{2,3},{3,2},{4,5},{5,4},{6,7},{7,6},{8,9},{9,8},{10,11... | collective-permute-start | bytes 3932168 | tf_op jit(solution)/shard_map/ppermute | solution.py:269
  64.9 0.2 select_reduce_fusion.1
  65.8 1.4 fusion.34
  67.2 0.2 concatenate.17
  67.4 0.8 copy.68
  68.2 0.5 convolution_convert_fusion.6
  68.7 0.6 reshape.173
  69.3 2.3 %pad_maximum_fusion.1.a_ref = bf16[64,96,128]{2,1,0:T(8,128)(2,1)} fusion(bf16[64,16,128]{2,1,0:T(8,128)(2,1)} %bitcast.73, bf16[64,80,128]{2,1,0:T(8,128)(2,1)S(1)} %reshape.173), kind=kLoop, calls=%fused_computation.14 | loop fusion | flops 3145728 | bytes 3145728 | tf_op jit(solution)/shard_map/concatenate | solution.py:363
  71.6 2.9 %fusion.b_ref = bf16[4,640,256]{2,1,0:T(8,128)(2,1)} fusion(bf16[4,640,256]{2,1,0:T(8,128)(2,1)} %collective-permute-done.1, bf16[128,4,1,256]{0,3,1,2:T(8,128)(2,1)S(1)} %copy.65, bf16[128,4,1,256]{0,3,1,2:T(8,128)(2,1)S(1)} %copy-done.2, pred[]{:T(512)S(6)} %eq.75, bf16[128,640]{0,1:T(8,128)(2,1)S(1)} %copy-done.11), kind=kOutput, calls=%fused_computation.3 | convolution fusion | flops 171180032 | bytes 3309569 | tf_op jit(solution)/shard_map/hr,hzb->zrb/dot_general | solution.py:360
  74.6 64.3 %shard_map.121 = (bf16[64,96,128]{2,1,0:T(8,128)(2,1)}, bf16[4,640,256]{2,1,0:T(8,128)(2,1)}, bf16[64,96,128]{2,1,0:T(8,128)(2,1)}) custom-call(bf16[64,96,128]{2,1,0:T(8,128)(2,1)} %pad_maximum_fusion.1.a_ref, bf16[4,640,256]{2,1,0:T(8,128)(2,1)} %fusion.b_ref), custom_call_target="tpu_custom_call" | custom-call | tf_op jit(solution)/shard_map/pallas_call | solution.py:243
  138.9 1.1 slice_convert_fusion
  140.2 0.7 slice_reduce_fusion.2
  140.9 0.4 reduce_sum.125
  141.2 0.9 reshape.177
  142.1 7.5 %all-to-all-start = ((bf16[64,10,256]{2,1,0:T(8,128)(2,1)}), bf16[64,10,256]{2,1,0:T(8,128)(2,1)}, u32[]{:S(2)}, u32[]{:S(2)}) async-start(bf16[64,10,256]{2,1,0:T(8,128)(2,1)} %reshape.177), calls=%async_computation | async-start | bytes 1048576 | tf_op jit(solution)/shard_map/all_to_all | solution.py:383
  149.6 1.9 %broadcast_select_fusion.1 = (bf16[64,80,128]{2,1,0:T(8,128)(2,1)S(1)}, bf16[64,80,128]{2,1,0:T(8,128)(2,1)S(1)}) fusion(pred[]{:T(512)S(6)} %eq.75, bf16[64,96,128]{2,1,0:T(8,128)(2,1)} %get-tuple-element.9, bf16[64,96,128]{2,1,0:T(8,128)(2,1)} %get-tuple-element.8), kind=kLoop, calls=%fused_computation.22 | loop fusion | flops 1310720 | bytes 5242881 | tf_op jit(solution)/shard_map/jit(_where)/select_n | solution.py:372
  151.5 1.4 select_n.90
  153.1 1.4 select_n.92
  154.6 1.9 %fusion.13 = f32[640]{0:T(1024)S(1)} fusion(f32[640,5]{1,0:T(8,128)S(1)} %reshape.180, f32[]{:T(128)} %get-tuple-element.11, f32[]{:T(128)} %get-tuple-element.10), kind=kLoop, calls=%fused_computation.36 | loop fusion | flops 4480 | bytes 15368 | tf_op jit(solution)/shard_map/mul | solution.py:381
  156.5 2.0 %convolution_bitcast_fusion = f32[128,640]{0,1:T(8,128)S(1)} fusion(bf16[1,128,2048]{2,1,0:T(8,128)(2,1)} %param.17, bf16[640,1024]{1,0:T(8,128)(2,1)S(1)} %copy-done.5, bf16[640,1024]{1,0:T(8,128)(2,1)S(1)} %copy-done.4, f32[640]{0:T(1024)S(1)} %fusion.13), kind=kOutput, calls=%fused_computation.26 | convolution fusion | flops 343408640 | bytes 3475968 | tf_op jit(solution)/shard_map/dot_general | solution.py:394
  158.5 1.6 fusion.3
  160.2 0.2 copy-done.21
  160.4 1.4 fusion.2
  161.9 1.5 fusion.1
  163.4 2.4 %all-to-all-done = bf16[64,10,256]{2,1,0:T(8,128)(2,1)} async-done(((bf16[64,10,256]{2,1,0:T(8,128)(2,1)}), bf16[64,10,256]{2,1,0:T(8,128)(2,1)}, u32[]{:S(2)}, u32[]{:S(2)}) %all-to-all-start) | async-done | bytes 327712 | tf_op jit(solution)/shard_map/all_to_all | solution.py:383
  165.8 1.2 reshape.178
  167.0 0.5 fusion.7
  167.7 0.9 reduce_sum.126
  (76 shorter events, 2.6 us)
Async XLA Ops:
  0.6 3.8 %copy-start = (bf16[128,2048]{1,0:T(8,128)(2,1)S(1)}, bf16[128,2048]{1,0:T(8,128)(2,1)}, u32[]{:S(2)}) copy-start(bf16[128,2048]{1,0:T(8,128)(2,1)} %param.9) | copy-start | bytes 1572868
  46.5 4.4 %copy-start.15 = (f32[128,4]{0,1:T(4,128)S(1)}, f32[128,4]{0,1:T(4,128)}, u32[]{:S(2)}) copy-start(f32[128,4]{0,1:T(4,128)} %param.12) | copy-start | bytes 6148
  46.5 4.6 %copy-start.13 = (bf16[1,128,2048]{2,1,0:T(8,128)(2,1)S(1)}, bf16[1,128,2048]{2,1,0:T(8,128)(2,1)}, u32[]{:S(2)}) copy-start(bf16[1,128,2048]{2,1,0:T(8,128)(2,1)} %param.17) | copy-start | bytes 1572868
  48.9 7.3 %collective-permute-start = (bf16[640,1024]{1,0:T(8,128)(2,1)S(1)}, bf16[640,1024]{1,0:T(8,128)(2,1)}, u32[]{:S(2)}, u32[]{:S(2)}) collective-permute-start(bf16[640,1024]{1,0:T(8,128)(2,1)S(1)} %reshape.176), channel_id=1, source_target_pairs={{0,1},{1,0},{2,3},{3,2},{4,5},{5,4},{6,7},{7,6},{8,9},{9,8},{10,11... | collective-permute-start | bytes 3932168 | tf_op jit(solution)/shard_map/ppermute | solution.py:269
  51.5 3.3 %copy-start.19 = (s32[2]{0:T(128)S(1)}, s32[2]{0:T(128)}, u32[]{:S(2)}) copy-start(s32[2]{0:T(128)} %param.14) | copy-start | bytes 28
  51.5 3.4 %copy-start.16 = (s32[128]{0:T(128)S(1)}, s32[128]{0:T(128)}, u32[]{:S(2)}) copy-start(s32[128]{0:T(128)} %param.13) | copy-start | bytes 1540
  54.8 6.1 %copy-start.1 = (bf16[128,4,1,256]{0,3,1,2:T(8,128)(2,1)}, bf16[128,4,1,256]{0,3,1,2:T(8,128)(2,1)S(1)}, u32[]{:S(2)}) copy-start(bf16[128,4,1,256]{0,3,1,2:T(8,128)(2,1)S(1)} %copy.66) | copy-start | bytes 786436
  56.2 1.6 copy-start.17
  57.8 1.1 copy-start.6
  57.8 1.5 copy-start.8
  57.8 1.5 copy-start.18
  59.3 1.6 copy-start.20
  60.9 6.3 %copy-start.10 = (bf16[128,640]{0,1:T(8,128)(2,1)}, bf16[128,640]{0,1:T(8,128)(2,1)S(1)}, u32[]{:S(2)}) copy-start(bf16[128,640]{0,1:T(8,128)(2,1)S(1)} %get-tuple-element.27) | copy-start | bytes 491524
  60.9 7.3 %copy-start.14 = (bf16[128,2048]{1,0:T(8,128)(2,1)S(1)}, bf16[128,2048]{1,0:T(8,128)(2,1)}, u32[]{:S(2)}) copy-start(bf16[128,2048]{1,0:T(8,128)(2,1)} %param.10) | copy-start | bytes 1572868
  62.5 9.1 %collective-permute-start.1 = (bf16[4,640,256]{2,1,0:T(8,128)(2,1)}, bf16[4,640,256]{2,1,0:T(8,128)(2,1)}, u32[]{:S(2)}, u32[]{:S(2)}) collective-permute-start(bf16[4,640,256]{2,1,0:T(8,128)(2,1)} %fusion.4), channel_id=1, source_target_pairs={{0,1},{1,0},{2,3},{3,2},{4,5},{5,4},{6,7},{7,6},{8,9},{9,8},{10,11... | collective-permute-start | bytes 3932168 | tf_op jit(solution)/shard_map/ppermute | solution.py:269
  69.3 2.3 %copy-start.2 = (bf16[128,4,1,256]{0,3,1,2:T(8,128)(2,1)S(1)}, bf16[128,4,1,256]{0,3,1,2:T(8,128)(2,1)}, u32[]{:S(2)}) copy-start(bf16[128,4,1,256]{0,3,1,2:T(8,128)(2,1)} %copy-done.1) | copy-start | bytes 786436
  69.3 2.3 %copy-start.11 = (bf16[128,640]{0,1:T(8,128)(2,1)S(1)}, bf16[128,640]{0,1:T(8,128)(2,1)}, u32[]{:S(2)}) copy-start(bf16[128,640]{0,1:T(8,128)(2,1)} %copy-done.10) | copy-start | bytes 491524
  138.9 2.0 %copy-start.3 = (bf16[4,640,256]{2,1,0:T(8,128)(2,1)S(1)}, bf16[4,640,256]{2,1,0:T(8,128)(2,1)}, u32[]{:S(2)}) copy-start(bf16[4,640,256]{2,1,0:T(8,128)(2,1)} %get-tuple-element.7) | copy-start | bytes 3932164
  142.1 23.7 %all-to-all-start = ((bf16[64,10,256]{2,1,0:T(8,128)(2,1)}), bf16[64,10,256]{2,1,0:T(8,128)(2,1)}, u32[]{:S(2)}, u32[]{:S(2)}) async-start(bf16[64,10,256]{2,1,0:T(8,128)(2,1)} %reshape.177), calls=%async_computation | async-start | bytes 1048576 | tf_op jit(solution)/shard_map/all_to_all | solution.py:383
  153.1 3.4 %copy-start.4 = (bf16[640,1024]{1,0:T(8,128)(2,1)S(1)}, bf16[640,1024]{1,0:T(8,128)(2,1)}, u32[]{:S(2)}) copy-start(bf16[640,1024]{1,0:T(8,128)(2,1)} %select_n.90) | copy-start | bytes 3932164
  154.6 1.9 %copy-start.5 = (bf16[640,1024]{1,0:T(8,128)(2,1)S(1)}, bf16[640,1024]{1,0:T(8,128)(2,1)}, u32[]{:S(2)}) copy-start(bf16[640,1024]{1,0:T(8,128)(2,1)} %select_n.92) | copy-start | bytes 3932164
  156.5 2.0 %copy-start.12 = (bf16[128,640]{0,1:T(8,128)(2,1)S(1)}, bf16[128,640]{0,1:T(8,128)(2,1)}, u32[]{:S(2)}) copy-start(bf16[128,640]{0,1:T(8,128)(2,1)} %copy-done.10) | copy-start | bytes 491524
  158.5 1.6 copy-start.7
  158.5 1.7 %copy-start.9 = (bf16[640,1024]{1,0:T(8,128)(2,1)S(1)}, bf16[640,1024]{1,0:T(8,128)(2,1)}, u32[]{:S(2)}) copy-start(bf16[640,1024]{1,0:T(8,128)(2,1)} %copy-done.8) | copy-start | bytes 3932164
  158.5 1.9 %copy-start.21 = (f32[128,640]{0,1:T(8,128)S(1)}, f32[128,640]{0,1:T(8,128)}, u32[]{:S(2)}) copy-start(f32[128,640]{0,1:T(8,128)} %copy-done.20) | copy-start | bytes 983044
  160.4 1.4 copy-start.22

commit v16 on v13

--- a/solution.py
+++ b/solution.py
@@ -182,19 +182,19 @@
     own_a.start()
     own_b = pltpu.make_async_copy(b_ref.at[at], yb_ref.at[at], b_own)
     own_b.start()
+    def send(i, carry):
+        peer = lax.rem(me + i, n)
+        dp_copy(a_ref.at[peer], ya_ref.at[me], peer, me, peer).start()
+        return carry
+
+    lax.fori_loop(1, n, send, 0)
+
     to_up = zh_copy(b_ref.at[up], yb_ref.at[at], 0, up)
     to_down = zh_copy(b_ref.at[down], yb_ref.at[at], 1, down)
     lift = zh_copy(b_ref.at[across, pl.ds(0, rows)], relay_up, 2, up)
     drop = zh_copy(b_ref.at[across, pl.ds(rows, rows)], relay_down, 3, down)
     for copy in (to_up, to_down, lift, drop):
         copy.start()
-
-    def send(i, carry):
-        peer = lax.rem(me + i, n)
-        dp_copy(a_ref.at[peer], ya_ref.at[me], peer, me, peer).start()
-        return carry
-
-    lax.fori_loop(1, n, send, 0)
     lift.wait_recv()
     pass_up = zh_copy(relay_up, yb_ref.at[down, pl.ds(0, rows)], 4, up)
     pass_up.start()

time: 168 us -> 171 us (1.018)
  Pallas kernels: 103 us -> 105 us
    pallas_call x1, Pallas kernels: 62.7 us -> 64.7 us  [_exchange_both(): pl.pallas_call(functools.partial(_both_kernel, n), out_shape=(jax.ShapeDt...]
where the time goes in v16:
time: 171 us; the launch traced here: 170 us
  Pallas kernels  105 us (61%)
  local copies, waits for them, and re-layouts  17.6 us (10%)
  other arithmetic  16.2 us (9%)
  matrix products  15 us (9%)
  starting transfers between devices  12.6 us (7%)
  waiting for transfers between devices  2.95 us (2%)
    pallas_call x1, Pallas kernels, _exchange_both(): pl.pallas_call(functools.partial(_both_kernel, n), out_shape=(jax.ShapeDt...  64.7 us
    pallas_call x1, Pallas kernels, _exchange(): pl.pallas_call(functools.partial(_exchange_kernel, n, axis), out_shape=ja...  40.1 us
    all_to_all x1, starting transfers between devices, body(): lax.all_to_all(slice_sum.reshape(owners, capacity, block), 'dp', split_ax...  8.28 us
    unnamed x51, local copies, waits for them, and re-layouts  4.55 us
    ppermute x2, starting transfers between devices, _swap_pair(): return lax.ppermute(x, 'core', [(0, 1), (1, 0)])  4.32 us
  transfers between devices with their start and end apart: 3, of which 1 were waited for; matrix products, arithmetic and copies ran while one was open for 15% of the time, Pallas kernels for 0%

profile of v16, /device:TPU:6, one launch (start us, length us, event | category | flops | bytes accessed | tf_op | source)
XLA Modules:
  0.0 170.4 jit_solution(1605074885504255280)
XLA Ops:
  0.6 0.8 copy.47
  1.7 1.2 reduce-window.6
  2.9 0.2 slice_reduce_fusion
  3.5 0.7 multiply_add_fusion
  4.4 0.5 convolution_convert_fusion.5
  4.9 1.4 reshape.175.x_ref
  6.4 40.1 %shard_map.120 = bf16[64,80,128]{2,1,0:T(8,128)(2,1)} custom-call(bf16[64,80,128]{2,1,0:T(8,128)(2,1)} %reshape.175.x_ref), custom_call_target="tpu_custom_call" | custom-call | tf_op jit(solution)/shard_map/pallas_call | solution.py:67
  46.5 2.4 %reshape.176 = bf16[640,1024]{1,0:T(8,128)(2,1)S(1)} reshape(bf16[64,80,128]{2,1,0:T(8,128)(2,1)} %shard_map.120) | data formatting | bytes 2621440 | tf_op jit(solution)/shard_map/reshape | solution.py:331
  48.9 1.9 %collective-permute-start = (bf16[640,1024]{1,0:T(8,128)(2,1)S(1)}, bf16[640,1024]{1,0:T(8,128)(2,1)}, u32[]{:S(2)}, u32[]{:S(2)}) collective-permute-start(bf16[640,1024]{1,0:T(8,128)(2,1)S(1)} %reshape.176), channel_id=1, source_target_pairs={{0,1},{1,0},{2,3},{3,2},{4,5},{5,4},{6,7},{7,6},{8,9},{9,8},{10,11... | collective-permute-start | bytes 3932168 | tf_op jit(solution)/shard_map/ppermute | solution.py:259
  51.1 0.4 reshape_squeeze.3
  51.5 1.5 fusion.43
  53.1 1.3 copy.65
  54.4 0.4 copy.66
  54.9 0.6 fusion.41
  55.6 0.6 fusion.42
  56.2 1.5 broadcast_select_fusion.3
  57.8 0.9 convolution_bitcast_fusion.2
  58.9 0.4 copy-done.8
  59.3 1.6 multiply_convert_fusion.3
  60.9 1.6 fusion.4
  62.5 2.4 %collective-permute-start.1 = (bf16[4,640,256]{2,1,0:T(8,128)(2,1)}, bf16[4,640,256]{2,1,0:T(8,128)(2,1)}, u32[]{:S(2)}, u32[]{:S(2)}) collective-permute-start(bf16[4,640,256]{2,1,0:T(8,128)(2,1)} %fusion.4), channel_id=1, source_target_pairs={{0,1},{1,0},{2,3},{3,2},{4,5},{5,4},{6,7},{7,6},{8,9},{9,8},{10,11... | collective-permute-start | bytes 3932168 | tf_op jit(solution)/shard_map/ppermute | solution.py:259
  64.9 0.2 select_reduce_fusion.1
  65.8 1.4 fusion.34
  67.2 0.2 concatenate.17
  67.4 0.8 copy.68
  68.2 0.5 convolution_convert_fusion.6
  68.7 0.6 reshape.173
  69.3 2.3 %pad_maximum_fusion.1.a_ref = bf16[64,96,128]{2,1,0:T(8,128)(2,1)} fusion(bf16[64,16,128]{2,1,0:T(8,128)(2,1)} %bitcast.73, bf16[64,80,128]{2,1,0:T(8,128)(2,1)S(1)} %reshape.173), kind=kLoop, calls=%fused_computation.14 | loop fusion | flops 3145728 | bytes 3145728 | tf_op jit(solution)/shard_map/concatenate | solution.py:353
  71.6 2.9 %fusion.b_ref = bf16[4,640,256]{2,1,0:T(8,128)(2,1)} fusion(bf16[4,640,256]{2,1,0:T(8,128)(2,1)} %collective-permute-done.1, bf16[128,4,1,256]{0,3,1,2:T(8,128)(2,1)S(1)} %copy.65, bf16[128,4,1,256]{0,3,1,2:T(8,128)(2,1)S(1)} %copy-done.2, pred[]{:T(512)S(6)} %eq.75, bf16[128,640]{0,1:T(8,128)(2,1)S(1)} %copy-done.11), kind=kOutput, calls=%fused_computation.3 | convolution fusion | flops 171180032 | bytes 3309569 | tf_op jit(solution)/shard_map/hr,hzb->zrb/dot_general | solution.py:350
  74.6 64.7 %shard_map.121 = (bf16[64,96,128]{2,1,0:T(8,128)(2,1)}, bf16[4,640,256]{2,1,0:T(8,128)(2,1)}, bf16[64,96,128]{2,1,0:T(8,128)(2,1)}) custom-call(bf16[64,96,128]{2,1,0:T(8,128)(2,1)} %pad_maximum_fusion.1.a_ref, bf16[4,640,256]{2,1,0:T(8,128)(2,1)} %fusion.b_ref), custom_call_target="tpu_custom_call" | custom-call | tf_op jit(solution)/shard_map/pallas_call | solution.py:234
  139.3 1.1 slice_convert_fusion
  140.6 0.7 slice_reduce_fusion.2
  141.3 0.4 reduce_sum.125
  141.6 0.9 reshape.177
  142.6 8.3 %all-to-all-start = ((bf16[64,10,256]{2,1,0:T(8,128)(2,1)}), bf16[64,10,256]{2,1,0:T(8,128)(2,1)}, u32[]{:S(2)}, u32[]{:S(2)}) async-start(bf16[64,10,256]{2,1,0:T(8,128)(2,1)} %reshape.177), calls=%async_computation | async-start | bytes 1048576 | tf_op jit(solution)/shard_map/all_to_all | solution.py:373
  150.9 1.9 %broadcast_select_fusion.1 = (bf16[64,80,128]{2,1,0:T(8,128)(2,1)S(1)}, bf16[64,80,128]{2,1,0:T(8,128)(2,1)S(1)}) fusion(pred[]{:T(512)S(6)} %eq.75, bf16[64,96,128]{2,1,0:T(8,128)(2,1)} %get-tuple-element.9, bf16[64,96,128]{2,1,0:T(8,128)(2,1)} %get-tuple-element.8), kind=kLoop, calls=%fused_computation.22 | loop fusion | flops 1310720 | bytes 5242881 | tf_op jit(solution)/shard_map/jit(_where)/select_n | solution.py:362
  152.7 1.4 select_n.90
  154.3 1.4 select_n.92
  155.8 1.9 %fusion.13 = f32[640]{0:T(1024)S(1)} fusion(f32[640,5]{1,0:T(8,128)S(1)} %reshape.180, f32[]{:T(128)} %get-tuple-element.11, f32[]{:T(128)} %get-tuple-element.10), kind=kLoop, calls=%fused_computation.36 | loop fusion | flops 4480 | bytes 15368 | tf_op jit(solution)/shard_map/mul | solution.py:371
  157.7 2.0 %convolution_bitcast_fusion = f32[128,640]{0,1:T(8,128)S(1)} fusion(bf16[1,128,2048]{2,1,0:T(8,128)(2,1)} %param.17, bf16[640,1024]{1,0:T(8,128)(2,1)S(1)} %copy-done.5, bf16[640,1024]{1,0:T(8,128)(2,1)S(1)} %copy-done.4, f32[640]{0:T(1024)S(1)} %fusion.13), kind=kOutput, calls=%fused_computation.26 | convolution fusion | flops 343408640 | bytes 3475968 | tf_op jit(solution)/shard_map/dot_general | solution.py:384
  159.7 1.6 fusion.3
  161.4 0.2 copy-done.21
  161.7 1.4 fusion.2
  163.1 1.5 fusion.1
  164.6 2.9 %all-to-all-done = bf16[64,10,256]{2,1,0:T(8,128)(2,1)} async-done(((bf16[64,10,256]{2,1,0:T(8,128)(2,1)}), bf16[64,10,256]{2,1,0:T(8,128)(2,1)}, u32[]{:S(2)}, u32[]{:S(2)}) %all-to-all-start) | async-done | bytes 327712 | tf_op jit(solution)/shard_map/all_to_all | solution.py:373
  167.6 1.2 reshape.178
  168.7 0.5 fusion.7
  169.4 0.9 reduce_sum.126
  (76 shorter events, 2.6 us)
Async XLA Ops:
  0.6 3.8 %copy-start = (bf16[128,2048]{1,0:T(8,128)(2,1)S(1)}, bf16[128,2048]{1,0:T(8,128)(2,1)}, u32[]{:S(2)}) copy-start(bf16[128,2048]{1,0:T(8,128)(2,1)} %param.9) | copy-start | bytes 1572868
  46.5 4.4 %copy-start.15 = (f32[128,4]{0,1:T(4,128)S(1)}, f32[128,4]{0,1:T(4,128)}, u32[]{:S(2)}) copy-start(f32[128,4]{0,1:T(4,128)} %param.12) | copy-start | bytes 6148
  46.5 4.6 %copy-start.13 = (bf16[1,128,2048]{2,1,0:T(8,128)(2,1)S(1)}, bf16[1,128,2048]{2,1,0:T(8,128)(2,1)}, u32[]{:S(2)}) copy-start(bf16[1,128,2048]{2,1,0:T(8,128)(2,1)} %param.17) | copy-start | bytes 1572868
  48.9 7.3 %collective-permute-start = (bf16[640,1024]{1,0:T(8,128)(2,1)S(1)}, bf16[640,1024]{1,0:T(8,128)(2,1)}, u32[]{:S(2)}, u32[]{:S(2)}) collective-permute-start(bf16[640,1024]{1,0:T(8,128)(2,1)S(1)} %reshape.176), channel_id=1, source_target_pairs={{0,1},{1,0},{2,3},{3,2},{4,5},{5,4},{6,7},{7,6},{8,9},{9,8},{10,11... | collective-permute-start | bytes 3932168 | tf_op jit(solution)/shard_map/ppermute | solution.py:259
  51.5 3.3 %copy-start.19 = (s32[2]{0:T(128)S(1)}, s32[2]{0:T(128)}, u32[]{:S(2)}) copy-start(s32[2]{0:T(128)} %param.14) | copy-start | bytes 28
  51.5 3.4 %copy-start.16 = (s32[128]{0:T(128)S(1)}, s32[128]{0:T(128)}, u32[]{:S(2)}) copy-start(s32[128]{0:T(128)} %param.13) | copy-start | bytes 1540
  54.8 6.1 %copy-start.1 = (bf16[128,4,1,256]{0,3,1,2:T(8,128)(2,1)}, bf16[128,4,1,256]{0,3,1,2:T(8,128)(2,1)S(1)}, u32[]{:S(2)}) copy-start(bf16[128,4,1,256]{0,3,1,2:T(8,128)(2,1)S(1)} %copy.66) | copy-start | bytes 786436
  56.2 1.6 copy-start.17
  57.8 1.1 copy-start.6
  57.8 1.5 copy-start.8
  57.8 1.5 copy-start.18
  59.3 1.6 copy-start.20
  60.9 6.3 %copy-start.10 = (bf16[128,640]{0,1:T(8,128)(2,1)}, bf16[128,640]{0,1:T(8,128)(2,1)S(1)}, u32[]{:S(2)}) copy-start(bf16[128,640]{0,1:T(8,128)(2,1)S(1)} %get-tuple-element.27) | copy-start | bytes 491524
  60.9 7.3 %copy-start.14 = (bf16[128,2048]{1,0:T(8,128)(2,1)S(1)}, bf16[128,2048]{1,0:T(8,128)(2,1)}, u32[]{:S(2)}) copy-start(bf16[128,2048]{1,0:T(8,128)(2,1)} %param.10) | copy-start | bytes 1572868
  62.5 9.1 %collective-permute-start.1 = (bf16[4,640,256]{2,1,0:T(8,128)(2,1)}, bf16[4,640,256]{2,1,0:T(8,128)(2,1)}, u32[]{:S(2)}, u32[]{:S(2)}) collective-permute-start(bf16[4,640,256]{2,1,0:T(8,128)(2,1)} %fusion.4), channel_id=1, source_target_pairs={{0,1},{1,0},{2,3},{3,2},{4,5},{5,4},{6,7},{7,6},{8,9},{9,8},{10,11... | collective-permute-start | bytes 3932168 | tf_op jit(solution)/shard_map/ppermute | solution.py:259
  69.3 2.3 %copy-start.2 = (bf16[128,4,1,256]{0,3,1,2:T(8,128)(2,1)S(1)}, bf16[128,4,1,256]{0,3,1,2:T(8,128)(2,1)}, u32[]{:S(2)}) copy-start(bf16[128,4,1,256]{0,3,1,2:T(8,128)(2,1)} %copy-done.1) | copy-start | bytes 786436
  69.3 2.3 %copy-start.11 = (bf16[128,640]{0,1:T(8,128)(2,1)S(1)}, bf16[128,640]{0,1:T(8,128)(2,1)}, u32[]{:S(2)}) copy-start(bf16[128,640]{0,1:T(8,128)(2,1)} %copy-done.10) | copy-start | bytes 491524
  139.3 2.0 %copy-start.3 = (bf16[4,640,256]{2,1,0:T(8,128)(2,1)S(1)}, bf16[4,640,256]{2,1,0:T(8,128)(2,1)}, u32[]{:S(2)}) copy-start(bf16[4,640,256]{2,1,0:T(8,128)(2,1)} %get-tuple-element.7) | copy-start | bytes 3932164
  142.6 25.0 %all-to-all-start = ((bf16[64,10,256]{2,1,0:T(8,128)(2,1)}), bf16[64,10,256]{2,1,0:T(8,128)(2,1)}, u32[]{:S(2)}, u32[]{:S(2)}) async-start(bf16[64,10,256]{2,1,0:T(8,128)(2,1)} %reshape.177), calls=%async_computation | async-start | bytes 1048576 | tf_op jit(solution)/shard_map/all_to_all | solution.py:373
  154.3 3.4 %copy-start.4 = (bf16[640,1024]{1,0:T(8,128)(2,1)S(1)}, bf16[640,1024]{1,0:T(8,128)(2,1)}, u32[]{:S(2)}) copy-start(bf16[640,1024]{1,0:T(8,128)(2,1)} %select_n.90) | copy-start | bytes 3932164
  155.8 1.9 %copy-start.5 = (bf16[640,1024]{1,0:T(8,128)(2,1)S(1)}, bf16[640,1024]{1,0:T(8,128)(2,1)}, u32[]{:S(2)}) copy-start(bf16[640,1024]{1,0:T(8,128)(2,1)} %select_n.92) | copy-start | bytes 3932164
  157.7 2.0 %copy-start.12 = (bf16[128,640]{0,1:T(8,128)(2,1)S(1)}, bf16[128,640]{0,1:T(8,128)(2,1)}, u32[]{:S(2)}) copy-start(bf16[128,640]{0,1:T(8,128)(2,1)} %copy-done.10) | copy-start | bytes 491524
  159.7 1.6 copy-start.7
  159.7 1.7 copy-start.9
  159.7 1.9 %copy-start.21 = (f32[128,640]{0,1:T(8,128)S(1)}, f32[128,640]{0,1:T(8,128)}, u32[]{:S(2)}) copy-start(f32[128,640]{0,1:T(8,128)} %copy-done.20) | copy-start | bytes 983044
  161.7 1.4 copy-start.22

commit v17 on v13

--- a/solution.py
+++ b/solution.py
@@ -211,9 +211,10 @@
 
     lax.fori_loop(1, n, finish, 0)
     own_a.wait()
+    body_rows = a_ref.shape[1] - 16
     to_partner = pltpu.make_async_remote_copy(
-        src_ref=ya_ref,
-        dst_ref=yp_ref,
+        src_ref=ya_ref.at[:, pl.ds(0, body_rows)],
+        dst_ref=yp_ref.at[:, pl.ds(0, body_rows)],
         send_sem=p_sem.at[0],
         recv_sem=p_sem.at[1],
         device_id={"core": partner},

time: 168 us -> 168 us (level)
  no operation moved by 1% of the time
where the time goes in v17:
time: 168 us; the launch traced here: 167 us
  Pallas kernels  103 us (61%)
  local copies, waits for them, and re-layouts  17.6 us (10%)
  other arithmetic  16.2 us (10%)
  matrix products  15 us (9%)
  starting transfers between devices  11.8 us (7%)
  waiting for transfers between devices  2.44 us (1%)
    pallas_call x1, Pallas kernels, _exchange_both(): pl.pallas_call(functools.partial(_both_kernel, n), out_shape=(jax.ShapeDt...  62.7 us
    pallas_call x1, Pallas kernels, _exchange(): pl.pallas_call(functools.partial(_exchange_kernel, n, axis), out_shape=ja...  40.1 us
    all_to_all x1, starting transfers between devices, body(): lax.all_to_all(slice_sum.reshape(owners, capacity, block), 'dp', split_ax...  7.48 us
    unnamed x51, local copies, waits for them, and re-layouts  4.55 us
    ppermute x2, starting transfers between devices, _swap_pair(): return lax.ppermute(x, 'core', [(0, 1), (1, 0)])  4.32 us
  transfers between devices with their start and end apart: 3, of which 1 were waited for; matrix products, arithmetic and copies ran while one was open for 15% of the time, Pallas kernels for 0%

profile of v17, /device:TPU:6, one launch (start us, length us, event | category | flops | bytes accessed | tf_op | source)
XLA Modules:
  0.0 167.1 jit_solution(15191107613737872241)
XLA Ops:
  0.6 0.8 copy.47
  1.7 1.2 reduce-window.6
  2.9 0.2 slice_reduce_fusion
  3.5 0.7 multiply_add_fusion
  4.4 0.5 convolution_convert_fusion.5
  4.9 1.4 reshape.175.x_ref
  6.4 40.1 %shard_map.120 = bf16[64,80,128]{2,1,0:T(8,128)(2,1)} custom-call(bf16[64,80,128]{2,1,0:T(8,128)(2,1)} %reshape.175.x_ref), custom_call_target="tpu_custom_call" | custom-call | tf_op jit(solution)/shard_map/pallas_call | solution.py:67
  46.5 2.4 %reshape.176 = bf16[640,1024]{1,0:T(8,128)(2,1)S(1)} reshape(bf16[64,80,128]{2,1,0:T(8,128)(2,1)} %shard_map.120) | data formatting | bytes 2621440 | tf_op jit(solution)/shard_map/reshape | solution.py:332
  48.9 1.9 %collective-permute-start = (bf16[640,1024]{1,0:T(8,128)(2,1)S(1)}, bf16[640,1024]{1,0:T(8,128)(2,1)}, u32[]{:S(2)}, u32[]{:S(2)}) collective-permute-start(bf16[640,1024]{1,0:T(8,128)(2,1)S(1)} %reshape.176), channel_id=1, source_target_pairs={{0,1},{1,0},{2,3},{3,2},{4,5},{5,4},{6,7},{7,6},{8,9},{9,8},{10,11... | collective-permute-start | bytes 3932168 | tf_op jit(solution)/shard_map/ppermute | solution.py:260
  51.1 0.4 reshape_squeeze.3
  51.5 1.5 fusion.43
  53.1 1.3 copy.65
  54.4 0.4 copy.66
  54.9 0.6 fusion.41
  55.6 0.6 fusion.42
  56.2 1.5 broadcast_select_fusion.3
  57.8 0.9 convolution_bitcast_fusion.2
  58.9 0.4 copy-done.8
  59.3 1.6 multiply_convert_fusion.3
  60.9 1.6 fusion.4
  62.5 2.4 %collective-permute-start.1 = (bf16[4,640,256]{2,1,0:T(8,128)(2,1)}, bf16[4,640,256]{2,1,0:T(8,128)(2,1)}, u32[]{:S(2)}, u32[]{:S(2)}) collective-permute-start(bf16[4,640,256]{2,1,0:T(8,128)(2,1)} %fusion.4), channel_id=1, source_target_pairs={{0,1},{1,0},{2,3},{3,2},{4,5},{5,4},{6,7},{7,6},{8,9},{9,8},{10,11... | collective-permute-start | bytes 3932168 | tf_op jit(solution)/shard_map/ppermute | solution.py:260
  64.9 0.2 select_reduce_fusion.1
  65.8 1.4 fusion.34
  67.2 0.2 concatenate.17
  67.4 0.8 copy.68
  68.2 0.5 convolution_convert_fusion.6
  68.7 0.6 reshape.173
  69.3 2.3 %pad_maximum_fusion.1.a_ref = bf16[64,96,128]{2,1,0:T(8,128)(2,1)} fusion(bf16[64,16,128]{2,1,0:T(8,128)(2,1)} %bitcast.73, bf16[64,80,128]{2,1,0:T(8,128)(2,1)S(1)} %reshape.173), kind=kLoop, calls=%fused_computation.14 | loop fusion | flops 3145728 | bytes 3145728 | tf_op jit(solution)/shard_map/concatenate | solution.py:354
  71.6 2.9 %fusion.b_ref = bf16[4,640,256]{2,1,0:T(8,128)(2,1)} fusion(bf16[4,640,256]{2,1,0:T(8,128)(2,1)} %collective-permute-done.1, bf16[128,4,1,256]{0,3,1,2:T(8,128)(2,1)S(1)} %copy.65, bf16[128,4,1,256]{0,3,1,2:T(8,128)(2,1)S(1)} %copy-done.2, pred[]{:T(512)S(6)} %eq.75, bf16[128,640]{0,1:T(8,128)(2,1)S(1)} %copy-done.11), kind=kOutput, calls=%fused_computation.3 | convolution fusion | flops 171180032 | bytes 3309569 | tf_op jit(solution)/shard_map/hr,hzb->zrb/dot_general | solution.py:351
  74.6 62.7 %shard_map.121 = (bf16[64,96,128]{2,1,0:T(8,128)(2,1)}, bf16[4,640,256]{2,1,0:T(8,128)(2,1)}, bf16[64,96,128]{2,1,0:T(8,128)(2,1)}) custom-call(bf16[64,96,128]{2,1,0:T(8,128)(2,1)} %pad_maximum_fusion.1.a_ref, bf16[4,640,256]{2,1,0:T(8,128)(2,1)} %fusion.b_ref), custom_call_target="tpu_custom_call" | custom-call | tf_op jit(solution)/shard_map/pallas_call | solution.py:235
  137.3 1.1 slice_convert_fusion
  138.6 0.7 slice_reduce_fusion.2
  139.3 0.4 reduce_sum.125
  139.6 0.9 reshape.177
  140.6 7.5 %all-to-all-start = ((bf16[64,10,256]{2,1,0:T(8,128)(2,1)}), bf16[64,10,256]{2,1,0:T(8,128)(2,1)}, u32[]{:S(2)}, u32[]{:S(2)}) async-start(bf16[64,10,256]{2,1,0:T(8,128)(2,1)} %reshape.177), calls=%async_computation | async-start | bytes 1048576 | tf_op jit(solution)/shard_map/all_to_all | solution.py:374
  148.1 1.9 %broadcast_select_fusion.1 = (bf16[64,80,128]{2,1,0:T(8,128)(2,1)S(1)}, bf16[64,80,128]{2,1,0:T(8,128)(2,1)S(1)}) fusion(pred[]{:T(512)S(6)} %eq.75, bf16[64,96,128]{2,1,0:T(8,128)(2,1)} %get-tuple-element.9, bf16[64,96,128]{2,1,0:T(8,128)(2,1)} %get-tuple-element.8), kind=kLoop, calls=%fused_computation.22 | loop fusion | flops 1310720 | bytes 5242881 | tf_op jit(solution)/shard_map/jit(_where)/select_n | solution.py:363
  149.9 1.4 select_n.90
  151.5 1.4 select_n.92
  153.0 1.9 %fusion.13 = f32[640]{0:T(1024)S(1)} fusion(f32[640,5]{1,0:T(8,128)S(1)} %reshape.180, f32[]{:T(128)} %get-tuple-element.11, f32[]{:T(128)} %get-tuple-element.10), kind=kLoop, calls=%fused_computation.36 | loop fusion | flops 4480 | bytes 15368 | tf_op jit(solution)/shard_map/mul | solution.py:372
  154.9 2.0 %convolution_bitcast_fusion = f32[128,640]{0,1:T(8,128)S(1)} fusion(bf16[1,128,2048]{2,1,0:T(8,128)(2,1)} %param.17, bf16[640,1024]{1,0:T(8,128)(2,1)S(1)} %copy-done.5, bf16[640,1024]{1,0:T(8,128)(2,1)S(1)} %copy-done.4, f32[640]{0:T(1024)S(1)} %fusion.13), kind=kOutput, calls=%fused_computation.26 | convolution fusion | flops 343408640 | bytes 3475968 | tf_op jit(solution)/shard_map/dot_general | solution.py:385
  156.9 1.6 fusion.3
  158.6 0.2 copy-done.21
  158.9 1.4 fusion.2
  160.3 1.5 fusion.1
  161.8 2.4 %all-to-all-done = bf16[64,10,256]{2,1,0:T(8,128)(2,1)} async-done(((bf16[64,10,256]{2,1,0:T(8,128)(2,1)}), bf16[64,10,256]{2,1,0:T(8,128)(2,1)}, u32[]{:S(2)}, u32[]{:S(2)}) %all-to-all-start) | async-done | bytes 327712 | tf_op jit(solution)/shard_map/all_to_all | solution.py:374
  164.2 1.2 reshape.178
  165.4 0.5 fusion.7
  166.1 0.9 reduce_sum.126
  (76 shorter events, 2.6 us)
Async XLA Ops:
  0.6 3.8 %copy-start = (bf16[128,2048]{1,0:T(8,128)(2,1)S(1)}, bf16[128,2048]{1,0:T(8,128)(2,1)}, u32[]{:S(2)}) copy-start(bf16[128,2048]{1,0:T(8,128)(2,1)} %param.9) | copy-start | bytes 1572868
  46.5 4.4 %copy-start.15 = (f32[128,4]{0,1:T(4,128)S(1)}, f32[128,4]{0,1:T(4,128)}, u32[]{:S(2)}) copy-start(f32[128,4]{0,1:T(4,128)} %param.12) | copy-start | bytes 6148
  46.5 4.6 %copy-start.13 = (bf16[1,128,2048]{2,1,0:T(8,128)(2,1)S(1)}, bf16[1,128,2048]{2,1,0:T(8,128)(2,1)}, u32[]{:S(2)}) copy-start(bf16[1,128,2048]{2,1,0:T(8,128)(2,1)} %param.17) | copy-start | bytes 1572868
  48.9 7.3 %collective-permute-start = (bf16[640,1024]{1,0:T(8,128)(2,1)S(1)}, bf16[640,1024]{1,0:T(8,128)(2,1)}, u32[]{:S(2)}, u32[]{:S(2)}) collective-permute-start(bf16[640,1024]{1,0:T(8,128)(2,1)S(1)} %reshape.176), channel_id=1, source_target_pairs={{0,1},{1,0},{2,3},{3,2},{4,5},{5,4},{6,7},{7,6},{8,9},{9,8},{10,11... | collective-permute-start | bytes 3932168 | tf_op jit(solution)/shard_map/ppermute | solution.py:260
  51.5 3.3 %copy-start.19 = (s32[2]{0:T(128)S(1)}, s32[2]{0:T(128)}, u32[]{:S(2)}) copy-start(s32[2]{0:T(128)} %param.14) | copy-start | bytes 28
  51.5 3.4 %copy-start.16 = (s32[128]{0:T(128)S(1)}, s32[128]{0:T(128)}, u32[]{:S(2)}) copy-start(s32[128]{0:T(128)} %param.13) | copy-start | bytes 1540
  54.8 6.1 %copy-start.1 = (bf16[128,4,1,256]{0,3,1,2:T(8,128)(2,1)}, bf16[128,4,1,256]{0,3,1,2:T(8,128)(2,1)S(1)}, u32[]{:S(2)}) copy-start(bf16[128,4,1,256]{0,3,1,2:T(8,128)(2,1)S(1)} %copy.66) | copy-start | bytes 786436
  56.2 1.6 copy-start.17
  57.8 1.1 copy-start.6
  57.8 1.5 copy-start.8
  57.8 1.5 copy-start.18
  59.3 1.6 copy-start.20
  60.9 6.3 %copy-start.10 = (bf16[128,640]{0,1:T(8,128)(2,1)}, bf16[128,640]{0,1:T(8,128)(2,1)S(1)}, u32[]{:S(2)}) copy-start(bf16[128,640]{0,1:T(8,128)(2,1)S(1)} %get-tuple-element.27) | copy-start | bytes 491524
  60.9 7.3 %copy-start.14 = (bf16[128,2048]{1,0:T(8,128)(2,1)S(1)}, bf16[128,2048]{1,0:T(8,128)(2,1)}, u32[]{:S(2)}) copy-start(bf16[128,2048]{1,0:T(8,128)(2,1)} %param.10) | copy-start | bytes 1572868
  62.5 9.1 %collective-permute-start.1 = (bf16[4,640,256]{2,1,0:T(8,128)(2,1)}, bf16[4,640,256]{2,1,0:T(8,128)(2,1)}, u32[]{:S(2)}, u32[]{:S(2)}) collective-permute-start(bf16[4,640,256]{2,1,0:T(8,128)(2,1)} %fusion.4), channel_id=1, source_target_pairs={{0,1},{1,0},{2,3},{3,2},{4,5},{5,4},{6,7},{7,6},{8,9},{9,8},{10,11... | collective-permute-start | bytes 3932168 | tf_op jit(solution)/shard_map/ppermute | solution.py:260
  69.3 2.3 %copy-start.2 = (bf16[128,4,1,256]{0,3,1,2:T(8,128)(2,1)S(1)}, bf16[128,4,1,256]{0,3,1,2:T(8,128)(2,1)}, u32[]{:S(2)}) copy-start(bf16[128,4,1,256]{0,3,1,2:T(8,128)(2,1)} %copy-done.1) | copy-start | bytes 786436
  69.3 2.3 %copy-start.11 = (bf16[128,640]{0,1:T(8,128)(2,1)S(1)}, bf16[128,640]{0,1:T(8,128)(2,1)}, u32[]{:S(2)}) copy-start(bf16[128,640]{0,1:T(8,128)(2,1)} %copy-done.10) | copy-start | bytes 491524
  137.3 2.0 %copy-start.3 = (bf16[4,640,256]{2,1,0:T(8,128)(2,1)S(1)}, bf16[4,640,256]{2,1,0:T(8,128)(2,1)}, u32[]{:S(2)}) copy-start(bf16[4,640,256]{2,1,0:T(8,128)(2,1)} %get-tuple-element.7) | copy-start | bytes 3932164
  140.6 23.7 %all-to-all-start = ((bf16[64,10,256]{2,1,0:T(8,128)(2,1)}), bf16[64,10,256]{2,1,0:T(8,128)(2,1)}, u32[]{:S(2)}, u32[]{:S(2)}) async-start(bf16[64,10,256]{2,1,0:T(8,128)(2,1)} %reshape.177), calls=%async_computation | async-start | bytes 1048576 | tf_op jit(solution)/shard_map/all_to_all | solution.py:374
  151.5 3.4 %copy-start.4 = (bf16[640,1024]{1,0:T(8,128)(2,1)S(1)}, bf16[640,1024]{1,0:T(8,128)(2,1)}, u32[]{:S(2)}) copy-start(bf16[640,1024]{1,0:T(8,128)(2,1)} %select_n.90) | copy-start | bytes 3932164
  153.0 1.9 %copy-start.5 = (bf16[640,1024]{1,0:T(8,128)(2,1)S(1)}, bf16[640,1024]{1,0:T(8,128)(2,1)}, u32[]{:S(2)}) copy-start(bf16[640,1024]{1,0:T(8,128)(2,1)} %select_n.92) | copy-start | bytes 3932164
  154.9 2.0 %copy-start.12 = (bf16[128,640]{0,1:T(8,128)(2,1)S(1)}, bf16[128,640]{0,1:T(8,128)(2,1)}, u32[]{:S(2)}) copy-start(bf16[128,640]{0,1:T(8,128)(2,1)} %copy-done.10) | copy-start | bytes 491524
  156.9 1.6 copy-start.7
  156.9 1.7 %copy-start.9 = (bf16[640,1024]{1,0:T(8,128)(2,1)S(1)}, bf16[640,1024]{1,0:T(8,128)(2,1)}, u32[]{:S(2)}) copy-start(bf16[640,1024]{1,0:T(8,128)(2,1)} %copy-done.8) | copy-start | bytes 3932164
  156.9 1.9 %copy-start.21 = (f32[128,640]{0,1:T(8,128)S(1)}, f32[128,640]{0,1:T(8,128)}, u32[]{:S(2)}) copy-start(f32[128,640]{0,1:T(8,128)} %copy-done.20) | copy-start | bytes 983044
  158.9 1.4 copy-start.22
